TPU v7x, 256 devices: a whole 4x4x8 slice. The times are simulated.
256 devices in a mesh: section: 16 (over y_hi, z), fsdp: 16 (over x, y_lo, core).
Axes of the slice: x: 4, y: 4 (y_hi: 2, y_lo: 2; y = y_hi * 2 + y_lo), z: 8, core: 2. Of those that a mesh axis runs over, the one named last changes fastest.
Arguments:
- branch_in: bfloat16 [16, 8192, 128], P('section', 'fsdp'), may hold values from -0.0625 to 0.0625
- branch_out: bfloat16 [16, 128, 8192], P('section', None, 'fsdp'), may hold values from -0.5 to 0.5
- down_inputs: bfloat16 [16, 12, 128, 8192], P('section', None, 'fsdp'), may hold values from -6 to 6
- up_inputs: bfloat16 [16, 12, 128, 8192], P('section', None, 'fsdp'), may hold values from -6 to 6
- top_grads: bfloat16 [2, 12, 128, 8192], P(None, None, 'fsdp'), may hold values from -6 to 6
- plan: int32 [2, 12], replicated, may hold values from 0 to 11, each once within a row
- reward_pos: int32 [2, 12, 16], replicated, may hold values from 0 to 7
- reward_cot: float32 [2, 12, 16], replicated, may hold values from -4 to 4
- reward_head: float32 [8192], replicated, may hold values from -5 to 5
Outputs:
- grad_in: float32 [16, 8192, 128], P('section', 'fsdp')
- grad_out: float32 [16, 128, 8192], P('section', None, 'fsdp')
Inputs may be any that keep to these rules, and one draw needn't show every extreme that they name: Each row of plan names every microbatch once.
All inputs are finite; a program needn't handle non-finite values.
Results may differ from a plain program's by a relative error of at most 0.03.
Values may be sent and summed in bfloat16 or wider, within the bound.
No kernel may reach another device: no remote copies, remote signals or barrier semaphores. Data moves between devices by JAX's collectives and lax.ppermute only.
A program may use at most 128 MiB of HBM per device.

v0:
```python
import jax
import jax.numpy as jnp
from jax import lax
from jax.sharding import PartitionSpec as P


def from_partner(value, axis, apart):
    mask = 2**apart
    pairs = [(source, source ^ mask) for source in range(lax.axis_size(axis))]
    return lax.ppermute(value, axis, pairs)


def passed_along(value, axis, steps):
    count = lax.axis_size(axis)
    initial, last = (max(0, -steps), min(count, count - steps))
    return lax.ppermute(value, axis, [(source, source + steps) for source in range(initial, last)])


def branch_grads(inputs, grad, w_in, w_out):
    pre_act = jnp.dot(inputs, w_in, preferred_element_type=jnp.float32)
    sig_val = jax.nn.sigmoid(pre_act)
    hidden = (pre_act * sig_val).astype(jnp.bfloat16)
    grad_hidden = lax.dot_general(
        grad, w_out, (((1,), (1,)), ((), ())), preferred_element_type=jnp.float32
    )
    grad_pre = (grad_hidden * sig_val * (1.0 + pre_act * (1.0 - sig_val))).astype(jnp.bfloat16)
    back_term = lax.dot_general(
        grad_pre, w_in, (((1,), (1,)), ((), ())), preferred_element_type=jnp.float32
    )
    back = (grad.astype(jnp.float32) + back_term).astype(jnp.bfloat16)
    return (hidden, grad_pre, back)


def bit_order(count):
    return list(range(count))


def fetch_mirror(packed):
    hops = lax.axis_size("section").bit_length() - 1
    for bit_index in bit_order(hops):
        packed = from_partner(packed, "section", bit_index)
    return packed


def send_mirror(packed):
    hops = lax.axis_size("section").bit_length() - 1
    for bit_index in bit_order(hops):
        packed = from_partner(packed.astype(jnp.bfloat16), "section", bit_index).astype(
            packed.dtype
        )
    return packed


def slot_pass(
    slot,
    starting,
    received,
    inputs,
    top,
    order,
    positions,
    rewards,
    head,
    row_global,
    seq_len,
    w_in,
    w_out,
    state,
):
    micro_count = inputs.shape[0]
    valid = jnp.logical_and(slot >= 0, slot < micro_count)
    clipped = jnp.clip(slot, 0, micro_count - 1)

    def active(operands):
        acc_in, acc_out = operands
        ident = lax.dynamic_index_in_dim(order, clipped, 0, keepdims=False)
        picked = jnp.arange(micro_count, dtype=jnp.int32) == ident
        pos_now = jnp.sum(jnp.where(picked[:, None], positions, 0), axis=0)
        cot_now = jnp.sum(jnp.where(picked[:, None], rewards, 0.0), axis=0)
        target = jnp.arange(positions.shape[1], dtype=jnp.int32) * seq_len + pos_now
        row_weight = jnp.sum(
            jnp.where(target[:, None] == row_global[None, :], cot_now[:, None], 0.0), axis=0
        )
        top_now = lax.dynamic_index_in_dim(top, clipped, 0, keepdims=False)
        first_grad = (top_now.astype(jnp.float32) + row_weight[:, None] * head[None, :]).astype(
            jnp.bfloat16
        )
        grad = jnp.where(starting, first_grad, received)
        rows_in = lax.dynamic_index_in_dim(inputs, ident, 0, keepdims=False)
        hidden, grad_pre, back = branch_grads(rows_in, grad, w_in, w_out)
        acc_in = acc_in + lax.dot_general(
            rows_in, grad_pre, (((0,), (0,)), ((), ())), preferred_element_type=jnp.float32
        )
        acc_out = acc_out + lax.dot_general(
            hidden, grad, (((0,), (0,)), ((), ())), preferred_element_type=jnp.float32
        )
        return ((acc_in, acc_out), back)

    def resting(operands):
        return (operands, jnp.zeros_like(received))

    return lax.cond(valid, active, resting, state)


def on_device(
    branch_in,
    branch_out,
    down_inputs,
    up_inputs,
    top_grads,
    plan,
    reward_pos,
    reward_cot,
    reward_head,
):
    section_count = lax.axis_size("section")
    section_idx = lax.axis_index("section")
    fsdp_count = lax.axis_size("fsdp")
    micro_count = down_inputs.shape[1]
    local_rows = down_inputs.shape[2]
    width = down_inputs.shape[3]
    seq_count = reward_pos.shape[2]
    seq_len = local_rows * fsdp_count // seq_count
    row_global = lax.axis_index("fsdp") * local_rows + jnp.arange(local_rows, dtype=jnp.int32)
    own_in_shard = branch_in[0]
    own_out_shard = branch_out[0]
    packed_own = jnp.stack([own_in_shard.reshape(own_out_shard.shape), own_out_shard])
    packed_far = fetch_mirror(packed_own)
    far_in_shard = packed_far[0].reshape(own_in_shard.shape)
    far_out_shard = packed_far[1]
    own_in, own_out = (
        lax.all_gather(own_in_shard, "fsdp", axis=0, tiled=True),
        lax.all_gather(own_out_shard, "fsdp", axis=1, tiled=True),
    )
    far_in, far_out = (
        lax.all_gather(far_in_shard, "fsdp", axis=0, tiled=True),
        lax.all_gather(far_out_shard, "fsdp", axis=1, tiled=True),
    )
    zero_in = jnp.zeros(own_in.shape, jnp.float32)
    zero_out = jnp.zeros(own_out.shape, jnp.float32)
    zero_rows = jnp.zeros((local_rows, width), jnp.bfloat16)
    down_state = (zero_in, zero_out)
    up_state = (zero_in, zero_out)

    def advance(step_idx, carry):
        recv_down, recv_up, state_down, state_up = carry
        slot_down = step_idx - (section_count - 1 - section_idx)
        slot_up = step_idx - section_idx
        state_down, back_down = slot_pass(
            slot_down,
            section_idx == section_count - 1,
            recv_down,
            down_inputs[0],
            top_grads[0],
            plan[0],
            reward_pos[0],
            reward_cot[0],
            reward_head,
            row_global,
            seq_len,
            own_in,
            own_out,
            state_down,
        )
        state_up, back_up = slot_pass(
            slot_up,
            section_idx == 0,
            recv_up,
            up_inputs[0],
            top_grads[1],
            plan[1],
            reward_pos[1],
            reward_cot[1],
            reward_head,
            row_global,
            seq_len,
            far_in,
            far_out,
            state_up,
        )
        recv_down = passed_along(back_down, "section", -1)
        recv_up = passed_along(back_up, "section", 1)
        return (recv_down, recv_up, state_down, state_up)

    carry = lax.fori_loop(
        0, section_count + micro_count - 1, advance, (zero_rows, zero_rows, down_state, up_state)
    )
    state_down = carry[2]
    state_up = carry[3]
    shares = (
        lax.psum_scatter(
            state_down[0].astype(jnp.bfloat16), "fsdp", scatter_dimension=0, tiled=True
        ).astype(jnp.float32),
        lax.psum_scatter(
            state_down[1].astype(jnp.bfloat16), "fsdp", scatter_dimension=1, tiled=True
        ).astype(jnp.float32),
        lax.psum_scatter(
            state_up[0].astype(jnp.bfloat16), "fsdp", scatter_dimension=0, tiled=True
        ).astype(jnp.float32),
        lax.psum_scatter(
            state_up[1].astype(jnp.bfloat16), "fsdp", scatter_dimension=1, tiled=True
        ).astype(jnp.float32),
    )
    packed_up = jnp.stack([shares[2].reshape(shares[3].shape), shares[3]])
    packed_back = send_mirror(packed_up)
    grad_in = shares[0] + packed_back[0].reshape(shares[0].shape)
    grad_out = shares[1] + packed_back[1]
    return (grad_in[None], grad_out[None])


def solution(mesh):
    in_specs = (
        P("section", "fsdp", None),
        P("section", None, "fsdp"),
        P("section", None, "fsdp", None),
        P("section", None, "fsdp", None),
        P(None, None, "fsdp", None),
        P(),
        P(),
        P(),
        P(),
    )
    out_specs = (P("section", "fsdp", None), P("section", None, "fsdp"))
    return jax.shard_map(
        on_device, mesh=mesh, in_specs=in_specs, out_specs=out_specs, check_vma=False
    )
```

profile of v0, /device:TPU:16, one launch (start us, length us, event | category | flops | bytes accessed | tf_op | source)
XLA Modules:
  0.0 1438.2 jit_solution(11273259088735241867)
XLA Ops:
  61.6 25.2 %all-gather.10.cloned.1.call-done = bf16[1,128,8192]{2,1,0:T(8,128)(2,1)} async-done(((bf16[1,128,512]{2,1,0:T(8,128)(2,1)}), bf16[1,128,8192]{2,1,0:T(8,128)(2,1)}) %all-gather.10.cloned.1.call-update) | async-done | bytes 2097168 | tf_op jit(solution)/shard_map/all_gather | solution.py:133
  86.9 38.9 %all-gather.8.cloned.1.call-done = bf16[8192,128]{1,0:T(8,128)(2,1)} async-done(((bf16[512,128]{1,0:T(8,128)(2,1)}), bf16[8192,128]{1,0:T(8,128)(2,1)}) %all-gather.8.cloned.1.call-update) | async-done | bytes 2097168 | tf_op jit(solution)/shard_map/all_gather | solution.py:136
  125.7 38.6 %all-gather.14.cloned.1.call-done = bf16[1,128,8192]{2,1,0:T(8,128)(2,1)} async-done(((bf16[1,128,512]{2,1,0:T(8,128)(2,1)}), bf16[1,128,8192]{2,1,0:T(8,128)(2,1)}) %all-gather.14.cloned.1.call-update) | async-done | bytes 2097168 | tf_op jit(solution)/shard_map/all_gather | solution.py:137
  173.9 920.0 %while.25 = (s32[]{:T(128)}, bf16[8,8192]{1,0:T(8,128)(2,1)S(1)}, bf16[8,8192]{1,0:T(8,128)(2,1)S(1)}, f32[8192,128]{1,0:T(8,128)}, f32[128,8192]{1,0:T(8,128)},...) while((s32[]{:T(128)}, bf16[8,8192]{1,0:T(8,128)(2,1)S(1)}, ...), condition=%wide.region_11.12_spmd.clone, body=%wide.region_0.11_spmd.clone.sunk | while | flops 173046048 | bytes 206939488 | solution.py:185
  234.7 19.0 %collective-permute-done.1 = bf16[8,8192]{1,0:T(8,128)(2,1)S(1)} collective-permute-done((bf16[8,8192]{1,0:T(8,128)(2,1)S(1)}, bf16[8,8192]{1,0:T(8,128)(2,1)S(1)}, u32[]{:S(2)}, u32[]{:S(2)}) %collective-permute-start.1) | collective-permute-done | bytes 131104 | tf_op jit(solution)/shard_map/while/body/eval_jaxpr/ppermute | solution.py:16
  253.7 21.6 %collective-permute-start = (bf16[8,8192]{1,0:T(8,128)(2,1)S(1)}, bf16[8,8192]{1,0:T(8,128)(2,1)S(1)}, u32[]{:S(2)}, u32[]{:S(2)}) collective-permute-start(bf16[8,8192]{1,0:T(8,128)(2,1)S(1)} %get-tuple-element.853), channel_id=1, source_target_pairs={{16,0},{32,16},{48,32},{64,48},{80,64},{96,80},{112,96},{128,112},... | collective-permute-start | bytes 393224 | tf_op jit(solution)/shard_map/while/body/eval_jaxpr/ppermute | solution.py:16
  277.7 22.3 %collective-permute-done.1 = bf16[8,8192]{1,0:T(8,128)(2,1)S(1)} collective-permute-done((bf16[8,8192]{1,0:T(8,128)(2,1)S(1)}, bf16[8,8192]{1,0:T(8,128)(2,1)S(1)}, u32[]{:S(2)}, u32[]{:S(2)}) %collective-permute-start.1) | collective-permute-done | bytes 131104 | tf_op jit(solution)/shard_map/while/body/eval_jaxpr/ppermute | solution.py:16
  300.1 21.9 %collective-permute-start = (bf16[8,8192]{1,0:T(8,128)(2,1)S(1)}, bf16[8,8192]{1,0:T(8,128)(2,1)S(1)}, u32[]{:S(2)}, u32[]{:S(2)}) collective-permute-start(bf16[8,8192]{1,0:T(8,128)(2,1)S(1)} %get-tuple-element.853), channel_id=1, source_target_pairs={{16,0},{32,16},{48,32},{64,48},{80,64},{96,80},{112,96},{128,112},... | collective-permute-start | bytes 393224 | tf_op jit(solution)/shard_map/while/body/eval_jaxpr/ppermute | solution.py:16
  322.0 19.6 %collective-permute-start.1 = (bf16[8,8192]{1,0:T(8,128)(2,1)S(1)}, bf16[8,8192]{1,0:T(8,128)(2,1)S(1)}, u32[]{:S(2)}, u32[]{:S(2)}) collective-permute-start(bf16[8,8192]{1,0:T(8,128)(2,1)S(1)} %get-tuple-element.854), channel_id=1, source_target_pairs={{0,16},{16,32},{32,48},{48,64},{64,80},{80,96},{96,112},{112,128},... | collective-permute-start | bytes 393224 | tf_op jit(solution)/shard_map/while/body/eval_jaxpr/ppermute | solution.py:16
  372.4 22.3 %collective-permute-done.1 = bf16[8,8192]{1,0:T(8,128)(2,1)S(1)} collective-permute-done((bf16[8,8192]{1,0:T(8,128)(2,1)S(1)}, bf16[8,8192]{1,0:T(8,128)(2,1)S(1)}, u32[]{:S(2)}, u32[]{:S(2)}) %collective-permute-start.1) | collective-permute-done | bytes 131104 | tf_op jit(solution)/shard_map/while/body/eval_jaxpr/ppermute | solution.py:16
  415.3 18.0 %conditional.7 = (f32[8192,128]{1,0:T(8,128)}, f32[128,8192]{1,0:T(8,128)}, bf16[8,8192]{1,0:T(8,128)(2,1)S(1)}) conditional(s32[]{:T(128)} %convert_element_type.120, (f32[8192,128]{1,0:T(8,128)}, f32[128,8192]{1,0:T(8,128)}) %tuple.68, (s32[2,12]{1,0:T(2,128)S(1)}, s32[]{:T(128)}, bf16[1,12,8,8192]{3,2,1,0:T(8,128)(2,1)}, pred[]{:T(512)}, ...), branch_computations={%region_6.6_spmd, %region_7.10_spmd} | conditional | flops 86523016 | bytes 102945120 | solution.py:102
  509.2 18.0 %conditional.7 = (f32[8192,128]{1,0:T(8,128)}, f32[128,8192]{1,0:T(8,128)}, bf16[8,8192]{1,0:T(8,128)(2,1)S(1)}) conditional(s32[]{:T(128)} %convert_element_type.120, (f32[8192,128]{1,0:T(8,128)}, f32[128,8192]{1,0:T(8,128)}) %tuple.68, (s32[2,12]{1,0:T(2,128)S(1)}, s32[]{:T(128)}, bf16[1,12,8,8192]{3,2,1,0:T(8,128)(2,1)}, pred[]{:T(512)}, ...), branch_computations={%region_6.6_spmd, %region_7.10_spmd} | conditional | flops 86523016 | bytes 102945120 | solution.py:102
  603.1 18.0 %conditional.7 = (f32[8192,128]{1,0:T(8,128)}, f32[128,8192]{1,0:T(8,128)}, bf16[8,8192]{1,0:T(8,128)(2,1)S(1)}) conditional(s32[]{:T(128)} %convert_element_type.120, (f32[8192,128]{1,0:T(8,128)}, f32[128,8192]{1,0:T(8,128)}) %tuple.68, (s32[2,12]{1,0:T(2,128)S(1)}, s32[]{:T(128)}, bf16[1,12,8,8192]{3,2,1,0:T(8,128)(2,1)}, pred[]{:T(512)}, ...), branch_computations={%region_6.6_spmd, %region_7.10_spmd} | conditional | flops 86523016 | bytes 102945120 | solution.py:102
  697.1 18.0 %conditional.7 = (f32[8192,128]{1,0:T(8,128)}, f32[128,8192]{1,0:T(8,128)}, bf16[8,8192]{1,0:T(8,128)(2,1)S(1)}) conditional(s32[]{:T(128)} %convert_element_type.120, (f32[8192,128]{1,0:T(8,128)}, f32[128,8192]{1,0:T(8,128)}) %tuple.68, (s32[2,12]{1,0:T(2,128)S(1)}, s32[]{:T(128)}, bf16[1,12,8,8192]{3,2,1,0:T(8,128)(2,1)}, pred[]{:T(512)}, ...), branch_computations={%region_6.6_spmd, %region_7.10_spmd} | conditional | flops 86523016 | bytes 102945120 | solution.py:102
  791.0 18.0 %conditional.7 = (f32[8192,128]{1,0:T(8,128)}, f32[128,8192]{1,0:T(8,128)}, bf16[8,8192]{1,0:T(8,128)(2,1)S(1)}) conditional(s32[]{:T(128)} %convert_element_type.120, (f32[8192,128]{1,0:T(8,128)}, f32[128,8192]{1,0:T(8,128)}) %tuple.68, (s32[2,12]{1,0:T(2,128)S(1)}, s32[]{:T(128)}, bf16[1,12,8,8192]{3,2,1,0:T(8,128)(2,1)}, pred[]{:T(512)}, ...), branch_computations={%region_6.6_spmd, %region_7.10_spmd} | conditional | flops 86523016 | bytes 102945120 | solution.py:102
  913.4 18.0 %collective-permute-start = (bf16[8,8192]{1,0:T(8,128)(2,1)S(1)}, bf16[8,8192]{1,0:T(8,128)(2,1)S(1)}, u32[]{:S(2)}, u32[]{:S(2)}) collective-permute-start(bf16[8,8192]{1,0:T(8,128)(2,1)S(1)} %get-tuple-element.853), channel_id=1, source_target_pairs={{16,0},{32,16},{48,32},{64,48},{80,64},{96,80},{112,96},{128,112},... | collective-permute-start | bytes 393224 | tf_op jit(solution)/shard_map/while/body/eval_jaxpr/ppermute | solution.py:16
  961.9 21.9 %collective-permute-start.1 = (bf16[8,8192]{1,0:T(8,128)(2,1)S(1)}, bf16[8,8192]{1,0:T(8,128)(2,1)S(1)}, u32[]{:S(2)}, u32[]{:S(2)}) collective-permute-start(bf16[8,8192]{1,0:T(8,128)(2,1)S(1)} %get-tuple-element.854), channel_id=1, source_target_pairs={{0,16},{16,32},{32,48},{48,64},{64,80},{80,96},{96,112},{112,128},... | collective-permute-start | bytes 393224 | tf_op jit(solution)/shard_map/while/body/eval_jaxpr/ppermute | solution.py:16
  1000.8 18.2 %collective-permute-start.1 = (bf16[8,8192]{1,0:T(8,128)(2,1)S(1)}, bf16[8,8192]{1,0:T(8,128)(2,1)S(1)}, u32[]{:S(2)}, u32[]{:S(2)}) collective-permute-start(bf16[8,8192]{1,0:T(8,128)(2,1)S(1)} %get-tuple-element.854), channel_id=1, source_target_pairs={{0,16},{16,32},{32,48},{48,64},{64,80},{80,96},{96,112},{112,128},... | collective-permute-start | bytes 393224 | tf_op jit(solution)/shard_map/while/body/eval_jaxpr/ppermute | solution.py:16
  1036.1 18.2 %collective-permute-start.1 = (bf16[8,8192]{1,0:T(8,128)(2,1)S(1)}, bf16[8,8192]{1,0:T(8,128)(2,1)S(1)}, u32[]{:S(2)}, u32[]{:S(2)}) collective-permute-start(bf16[8,8192]{1,0:T(8,128)(2,1)S(1)} %get-tuple-element.854), channel_id=1, source_target_pairs={{0,16},{16,32},{32,48},{48,64},{64,80},{80,96},{96,112},{112,128},... | collective-permute-start | bytes 393224 | tf_op jit(solution)/shard_map/while/body/eval_jaxpr/ppermute | solution.py:16
  1071.4 20.0 %collective-permute-start.1 = (bf16[8,8192]{1,0:T(8,128)(2,1)S(1)}, bf16[8,8192]{1,0:T(8,128)(2,1)S(1)}, u32[]{:S(2)}, u32[]{:S(2)}) collective-permute-start(bf16[8,8192]{1,0:T(8,128)(2,1)S(1)} %get-tuple-element.854), channel_id=1, source_target_pairs={{0,16},{16,32},{32,48},{48,64},{64,80},{80,96},{96,112},{112,128},... | collective-permute-start | bytes 393224 | tf_op jit(solution)/shard_map/while/body/eval_jaxpr/ppermute | solution.py:16
  1109.2 115.3 %reduce-scatter.7.cloned.1.call-done = bf16[512,128]{1,0:T(8,128)(2,1)} async-done(((bf16[8192,128]{1,0:T(8,128)(2,1)}), bf16[512,128]{1,0:T(8,128)(2,1)}) %reduce-scatter.7.cloned.1.call-update) | async-done | bytes 131088 | tf_op jit(solution)/shard_map/reduce_scatter | solution.py:197
  1225.5 67.2 %reduce-scatter.9.cloned.1.call-done = bf16[128,512]{1,0:T(8,128)(2,1)} async-done(((bf16[128,8192]{1,0:T(8,128)(2,1)}), bf16[128,512]{1,0:T(8,128)(2,1)}) %reduce-scatter.9.cloned.1.call-update) | async-done | bytes 131088 | tf_op jit(solution)/shard_map/reduce_scatter | solution.py:200
  1340.1 21.4 %reduce-scatter.11.cloned.1.call-done = bf16[128,512]{1,0:T(8,128)(2,1)} async-done(((bf16[128,8192]{1,0:T(8,128)(2,1)}), bf16[128,512]{1,0:T(8,128)(2,1)}) %reduce-scatter.11.cloned.1.call-update) | async-done | bytes 131088 | tf_op jit(solution)/shard_map/reduce_scatter | solution.py:194
  1363.2 66.5 %reduce-scatter.5.cloned.1.call-done = bf16[512,128]{1,0:T(8,128)(2,1)} async-done(((bf16[8192,128]{1,0:T(8,128)(2,1)}), bf16[512,128]{1,0:T(8,128)(2,1)}) %reduce-scatter.5.cloned.1.call-update) | async-done | bytes 131088 | tf_op jit(solution)/shard_map/reduce_scatter | solution.py:191
  (845 shorter events, 1100.0 us)
Async XLA Ops:
  7.2 54.4 %all-gather.12.cloned.1.call-start = ((), (), s32[]{:S(2)}) async-start(), calls=%async_computation.10 | async-start | bytes 2228224 | tf_op jit(solution)/shard_map/all_gather | solution.py:132
  7.9 78.9 %all-gather.10.cloned.1.call-start = ((), (), s32[]{:S(2)}) async-start(), calls=%async_computation.9 | async-start | bytes 2228224 | tf_op jit(solution)/shard_map/all_gather | solution.py:133
  8.7 117.0 %all-gather.8.cloned.1.call-start = ((), (), s32[]{:S(2)}) async-start(), calls=%async_computation.4 | async-start | bytes 2228224 | tf_op jit(solution)/shard_map/all_gather | solution.py:136
  60.7 103.6 %all-gather.14.cloned.1.call-start = ((), (), s32[]{:S(2)}) async-start(), calls=%async_computation.11 | async-start | bytes 2228224 | tf_op jit(solution)/shard_map/all_gather | solution.py:137
  61.3 1163.2 %reduce-scatter.7.cloned.1.call-start = ((), (), s32[]{:S(2)}) async-start(), calls=%async_computation.6 | async-start | bytes 2228224 | tf_op jit(solution)/shard_map/reduce_scatter | solution.py:197
  253.7 24.1 %collective-permute-start = (bf16[8,8192]{1,0:T(8,128)(2,1)S(1)}, bf16[8,8192]{1,0:T(8,128)(2,1)S(1)}, u32[]{:S(2)}, u32[]{:S(2)}) collective-permute-start(bf16[8,8192]{1,0:T(8,128)(2,1)S(1)} %get-tuple-element.853), channel_id=1, source_target_pairs={{16,0},{32,16},{48,32},{64,48},{80,64},{96,80},{112,96},{128,112},... | collective-permute-start | bytes 393224 | tf_op jit(solution)/shard_map/while/body/eval_jaxpr/ppermute | solution.py:16
  275.3 24.8 %collective-permute-start.1 = (bf16[8,8192]{1,0:T(8,128)(2,1)S(1)}, bf16[8,8192]{1,0:T(8,128)(2,1)S(1)}, u32[]{:S(2)}, u32[]{:S(2)}) collective-permute-start(bf16[8,8192]{1,0:T(8,128)(2,1)S(1)} %get-tuple-element.854), channel_id=1, source_target_pairs={{0,16},{16,32},{32,48},{48,64},{64,80},{80,96},{96,112},{112,128},... | collective-permute-start | bytes 393224 | tf_op jit(solution)/shard_map/while/body/eval_jaxpr/ppermute | solution.py:16
  300.1 42.5 %collective-permute-start = (bf16[8,8192]{1,0:T(8,128)(2,1)S(1)}, bf16[8,8192]{1,0:T(8,128)(2,1)S(1)}, u32[]{:S(2)}, u32[]{:S(2)}) collective-permute-start(bf16[8,8192]{1,0:T(8,128)(2,1)S(1)} %get-tuple-element.853), channel_id=1, source_target_pairs={{16,0},{32,16},{48,32},{64,48},{80,64},{96,80},{112,96},{128,112},... | collective-permute-start | bytes 393224 | tf_op jit(solution)/shard_map/while/body/eval_jaxpr/ppermute | solution.py:16
  322.0 26.0 %collective-permute-start.1 = (bf16[8,8192]{1,0:T(8,128)(2,1)S(1)}, bf16[8,8192]{1,0:T(8,128)(2,1)S(1)}, u32[]{:S(2)}, u32[]{:S(2)}) collective-permute-start(bf16[8,8192]{1,0:T(8,128)(2,1)S(1)} %get-tuple-element.854), channel_id=1, source_target_pairs={{0,16},{16,32},{32,48},{48,64},{64,80},{80,96},{96,112},{112,128},... | collective-permute-start | bytes 393224 | tf_op jit(solution)/shard_map/while/body/eval_jaxpr/ppermute | solution.py:16
  370.0 24.8 %collective-permute-start.1 = (bf16[8,8192]{1,0:T(8,128)(2,1)S(1)}, bf16[8,8192]{1,0:T(8,128)(2,1)S(1)}, u32[]{:S(2)}, u32[]{:S(2)}) collective-permute-start(bf16[8,8192]{1,0:T(8,128)(2,1)S(1)} %get-tuple-element.854), channel_id=1, source_target_pairs={{0,16},{16,32},{32,48},{48,64},{64,80},{80,96},{96,112},{112,128},... | collective-permute-start | bytes 393224 | tf_op jit(solution)/shard_map/while/body/eval_jaxpr/ppermute | solution.py:16
  411.4 23.8 %collective-permute-start = (bf16[8,8192]{1,0:T(8,128)(2,1)S(1)}, bf16[8,8192]{1,0:T(8,128)(2,1)S(1)}, u32[]{:S(2)}, u32[]{:S(2)}) collective-permute-start(bf16[8,8192]{1,0:T(8,128)(2,1)S(1)} %get-tuple-element.853), channel_id=1, source_target_pairs={{16,0},{32,16},{48,32},{64,48},{80,64},{96,80},{112,96},{128,112},... | collective-permute-start | bytes 393224 | tf_op jit(solution)/shard_map/while/body/eval_jaxpr/ppermute | solution.py:16
  460.3 23.8 %collective-permute-start = (bf16[8,8192]{1,0:T(8,128)(2,1)S(1)}, bf16[8,8192]{1,0:T(8,128)(2,1)S(1)}, u32[]{:S(2)}, u32[]{:S(2)}) collective-permute-start(bf16[8,8192]{1,0:T(8,128)(2,1)S(1)} %get-tuple-element.853), channel_id=1, source_target_pairs={{16,0},{32,16},{48,32},{64,48},{80,64},{96,80},{112,96},{128,112},... | collective-permute-start | bytes 393224 | tf_op jit(solution)/shard_map/while/body/eval_jaxpr/ppermute | solution.py:16
  507.3 23.8 %collective-permute-start = (bf16[8,8192]{1,0:T(8,128)(2,1)S(1)}, bf16[8,8192]{1,0:T(8,128)(2,1)S(1)}, u32[]{:S(2)}, u32[]{:S(2)}) collective-permute-start(bf16[8,8192]{1,0:T(8,128)(2,1)S(1)} %get-tuple-element.853), channel_id=1, source_target_pairs={{16,0},{32,16},{48,32},{64,48},{80,64},{96,80},{112,96},{128,112},... | collective-permute-start | bytes 393224 | tf_op jit(solution)/shard_map/while/body/eval_jaxpr/ppermute | solution.py:16
  554.3 23.8 %collective-permute-start = (bf16[8,8192]{1,0:T(8,128)(2,1)S(1)}, bf16[8,8192]{1,0:T(8,128)(2,1)S(1)}, u32[]{:S(2)}, u32[]{:S(2)}) collective-permute-start(bf16[8,8192]{1,0:T(8,128)(2,1)S(1)} %get-tuple-element.853), channel_id=1, source_target_pairs={{16,0},{32,16},{48,32},{64,48},{80,64},{96,80},{112,96},{128,112},... | collective-permute-start | bytes 393224 | tf_op jit(solution)/shard_map/while/body/eval_jaxpr/ppermute | solution.py:16
  601.2 23.8 %collective-permute-start = (bf16[8,8192]{1,0:T(8,128)(2,1)S(1)}, bf16[8,8192]{1,0:T(8,128)(2,1)S(1)}, u32[]{:S(2)}, u32[]{:S(2)}) collective-permute-start(bf16[8,8192]{1,0:T(8,128)(2,1)S(1)} %get-tuple-element.853), channel_id=1, source_target_pairs={{16,0},{32,16},{48,32},{64,48},{80,64},{96,80},{112,96},{128,112},... | collective-permute-start | bytes 393224 | tf_op jit(solution)/shard_map/while/body/eval_jaxpr/ppermute | solution.py:16
  648.2 23.8 %collective-permute-start = (bf16[8,8192]{1,0:T(8,128)(2,1)S(1)}, bf16[8,8192]{1,0:T(8,128)(2,1)S(1)}, u32[]{:S(2)}, u32[]{:S(2)}) collective-permute-start(bf16[8,8192]{1,0:T(8,128)(2,1)S(1)} %get-tuple-element.853), channel_id=1, source_target_pairs={{16,0},{32,16},{48,32},{64,48},{80,64},{96,80},{112,96},{128,112},... | collective-permute-start | bytes 393224 | tf_op jit(solution)/shard_map/while/body/eval_jaxpr/ppermute | solution.py:16
  695.2 23.8 %collective-permute-start = (bf16[8,8192]{1,0:T(8,128)(2,1)S(1)}, bf16[8,8192]{1,0:T(8,128)(2,1)S(1)}, u32[]{:S(2)}, u32[]{:S(2)}) collective-permute-start(bf16[8,8192]{1,0:T(8,128)(2,1)S(1)} %get-tuple-element.853), channel_id=1, source_target_pairs={{16,0},{32,16},{48,32},{64,48},{80,64},{96,80},{112,96},{128,112},... | collective-permute-start | bytes 393224 | tf_op jit(solution)/shard_map/while/body/eval_jaxpr/ppermute | solution.py:16
  742.1 23.8 %collective-permute-start = (bf16[8,8192]{1,0:T(8,128)(2,1)S(1)}, bf16[8,8192]{1,0:T(8,128)(2,1)S(1)}, u32[]{:S(2)}, u32[]{:S(2)}) collective-permute-start(bf16[8,8192]{1,0:T(8,128)(2,1)S(1)} %get-tuple-element.853), channel_id=1, source_target_pairs={{16,0},{32,16},{48,32},{64,48},{80,64},{96,80},{112,96},{128,112},... | collective-permute-start | bytes 393224 | tf_op jit(solution)/shard_map/while/body/eval_jaxpr/ppermute | solution.py:16
  913.4 38.0 %collective-permute-start = (bf16[8,8192]{1,0:T(8,128)(2,1)S(1)}, bf16[8,8192]{1,0:T(8,128)(2,1)S(1)}, u32[]{:S(2)}, u32[]{:S(2)}) collective-permute-start(bf16[8,8192]{1,0:T(8,128)(2,1)S(1)} %get-tuple-element.853), channel_id=1, source_target_pairs={{16,0},{32,16},{48,32},{64,48},{80,64},{96,80},{112,96},{128,112},... | collective-permute-start | bytes 393224 | tf_op jit(solution)/shard_map/while/body/eval_jaxpr/ppermute | solution.py:16
  960.0 23.9 %collective-permute-start = (bf16[8,8192]{1,0:T(8,128)(2,1)S(1)}, bf16[8,8192]{1,0:T(8,128)(2,1)S(1)}, u32[]{:S(2)}, u32[]{:S(2)}) collective-permute-start(bf16[8,8192]{1,0:T(8,128)(2,1)S(1)} %get-tuple-element.853), channel_id=1, source_target_pairs={{16,0},{32,16},{48,32},{64,48},{80,64},{96,80},{112,96},{128,112},... | collective-permute-start | bytes 393224 | tf_op jit(solution)/shard_map/while/body/eval_jaxpr/ppermute | solution.py:16
  961.9 24.4 %collective-permute-start.1 = (bf16[8,8192]{1,0:T(8,128)(2,1)S(1)}, bf16[8,8192]{1,0:T(8,128)(2,1)S(1)}, u32[]{:S(2)}, u32[]{:S(2)}) collective-permute-start(bf16[8,8192]{1,0:T(8,128)(2,1)S(1)} %get-tuple-element.854), channel_id=1, source_target_pairs={{0,16},{16,32},{32,48},{48,64},{64,80},{80,96},{96,112},{112,128},... | collective-permute-start | bytes 393224 | tf_op jit(solution)/shard_map/while/body/eval_jaxpr/ppermute | solution.py:16
  1097.6 195.1 %reduce-scatter.9.cloned.1.call-start = ((), (), s32[]{:S(2)}) async-start(), calls=%async_computation.7 | async-start | bytes 2228224 | tf_op jit(solution)/shard_map/reduce_scatter | solution.py:200
  1101.5 260.0 %reduce-scatter.11.cloned.1.call-start = ((), (), s32[]{:S(2)}) async-start(), calls=%async_computation.8 | async-start | bytes 2228224 | tf_op jit(solution)/shard_map/reduce_scatter | solution.py:194
  1105.4 324.3 %reduce-scatter.5.cloned.1.call-start = ((), (), s32[]{:S(2)}) async-start(), calls=%async_computation.5 | async-start | bytes 2228224 | tf_op jit(solution)/shard_map/reduce_scatter | solution.py:191
  (171 other events, 1037.8 us)
Sparse Core Ops, SparseCore 0:
  9.8 38.6 all-gather.11
  50.3 36.4 all-gather.9
  89.3 36.3 all-gather.7
  128.0 36.3 all-gather.13
  1097.8 126.7 reduce-scatter.6
  1226.9 65.8 reduce-scatter.8
  1295.3 66.2 reduce-scatter.10
  1364.1 65.5 reduce-scatter.4
where the time goes:
time: 1440 us
  waiting for transfers between devices  661 us (46%)
  starting transfers between devices  313 us (22%)
  matrix products  199 us (14%)
  local copies, waits for them, and re-layouts  149 us (10%)
  loops' own time  53.4 us (4%)
  other arithmetic  48.8 us (3%)
    ppermute x54, starting transfers between devices, passed_along(): lax.ppermute(value, axis, [(source, source + steps) for source in range(i...  292 us
    ppermute x54, waiting for transfers between devices, passed_along(): lax.ppermute(value, axis, [(source, source + steps) for source in range(i...  211 us
    reduce_scatter x1, waiting for transfers between devices, on_device(): lax.psum_scatter(state_up[0].astype(jnp.bfloat16), 'fsdp', scatter_dimens...  115 us
    cond x240, local copies, waits for them, and re-layouts  81.5 us
    ppermute x8, waiting for transfers between devices, from_partner(): return lax.ppermute(value, axis, pairs)  74.3 us
    dot_general x24, matrix products, active(): lax.dot_general(rows_in, grad_pre, (((0,), (0,)), ((), ())), preferred_el...  73.4 us
    reduce_scatter x1, waiting for transfers between devices, on_device(): lax.psum_scatter(state_up[1].astype(jnp.bfloat16), 'fsdp', scatter_dimens...  67.2 us
    reduce_scatter x1, waiting for transfers between devices, on_device(): lax.psum_scatter(state_down[0].astype(jnp.bfloat16), 'fsdp', scatter_dime...  66.5 us
  transfers between devices with their start and end apart: 70, of which 56 were waited for; matrix products, arithmetic and copies ran while one was open for 12% of the time, Pallas kernels for 0%

commit v1 on v0

v1 whole, which is shorter than its diff:
```python
import jax
import jax.numpy as jnp
from jax import lax
from jax.experimental import pallas as pl
from jax.experimental.pallas import tpu as pltpu
from jax.sharding import PartitionSpec as P

BF16 = jnp.bfloat16
F32 = jnp.float32
ROWS_OF_BOTH = (((0,), (0,)), ((), ()))
COLS_OF_BOTH = (((1,), (1,)), ((), ()))


def dot(left, right, dims=(((1,), (0,)), ((), ()))):
    return lax.dot_general(left, right, dims, preferred_element_type=F32)


def from_above(value, steps):
    count = lax.axis_size("section")
    return lax.ppermute(value, "section", [((k + steps) % count, k) for k in range(count)])


def mirrored(value):
    count = lax.axis_size("section")
    return lax.ppermute(value, "section", [(k, count - 1 - k) for k in range(count)])


def exchanged(parts, axis):
    return lax.all_to_all(parts, axis, 0, 0, tiled=True)


def spread(value, axis):
    return exchanged(jnp.broadcast_to(value[None], (lax.axis_size(axis),) + value.shape), axis)


def vmem():
    return pl.BlockSpec(memory_space=pltpu.VMEM)


def smem():
    return pl.BlockSpec(memory_space=pltpu.SMEM)


def couplings(section, in_t, out_t, near, count):
    units = in_t.shape[0]
    slots = len(near)

    def kernel(section_ref, in_ref, out_ref, *refs):
        dest = refs[slots]
        for slot in range(slots):
            wrapped = section_ref[0] + slot + 1 >= count

            @pl.when(wrapped)
            def _():
                dest[slot] = dot(in_ref[...], refs[slot][...], COLS_OF_BOTH).astype(BF16)

            @pl.when(jnp.logical_not(wrapped))
            def _():
                dest[slot] = dot(refs[slot][...], out_ref[...], COLS_OF_BOTH).astype(BF16)

    return pl.pallas_call(
        kernel,
        out_shape=jax.ShapeDtypeStruct((slots, units, units), BF16),
        in_specs=[smem()] + [vmem()] * (2 + slots),
        out_specs=vmem(),
        name="couplings",
    )(section, in_t, out_t, *near)


def pre_parts(wide, in_t, far_in_t, step):
    blocks, rows, part = wide.shape
    units = in_t.shape[0]
    half = rows // 2

    def kernel(wide_ref, in_ref, far_ref, dest):
        for b in range(step):
            dest[b, :half] = dot(wide_ref[b, :half], in_ref[...], COLS_OF_BOTH).astype(BF16)
            dest[b, half:] = dot(wide_ref[b, half:], far_ref[...], COLS_OF_BOTH).astype(BF16)

    return pl.pallas_call(
        kernel,
        grid=(blocks // step,),
        out_shape=jax.ShapeDtypeStruct((blocks, rows, units), BF16),
        in_specs=[
            pl.BlockSpec((step, rows, part), lambda b: (b, 0, 0)),
            pl.BlockSpec((units, part), lambda b: (0, 0)),
            pl.BlockSpec((units, part), lambda b: (0, 0)),
        ],
        out_specs=pl.BlockSpec((step, rows, units), lambda b: (b, 0, 0)),
        name="pre_parts",
    )(wide, in_t, far_in_t)


def top_products(top, row_weight, head, out_full, place, step):
    blocks, units, part = out_full.shape
    rows = top.shape[0]

    def kernel(top_ref, weight_ref, head_ref, out_ref, place_ref, dest, acc):
        at = pl.program_id(0)

        @pl.when(at == 0)
        def _():
            acc[...] = jnp.zeros_like(acc)

        first = (top_ref[...].astype(F32) + weight_ref[...] * head_ref[...]).astype(BF16)
        total = acc[...]
        for b in range(step):
            total = total + dot(first[:, b * part : (b + 1) * part], out_ref[b], COLS_OF_BOTH)
        acc[...] = total

        @pl.when(at == pl.num_programs(0) - 1)
        def _():
            dest[...] = dot(place_ref[...], acc[...].astype(BF16)).astype(BF16)

    return pl.pallas_call(
        kernel,
        grid=(blocks // step,),
        out_shape=jax.ShapeDtypeStruct((rows, units), BF16),
        in_specs=[
            pl.BlockSpec((rows, step * part), lambda b: (0, b)),
            pl.BlockSpec((rows, 1), lambda b: (0, 0)),
            pl.BlockSpec((1, step * part), lambda b: (0, b)),
            pl.BlockSpec((step, units, part), lambda b: (b, 0, 0)),
            pl.BlockSpec((rows, rows), lambda b: (0, 0)),
        ],
        out_specs=pl.BlockSpec((rows, units), lambda b: (0, 0)),
        scratch_shapes=[pltpu.VMEM((rows, units), F32)],
        name="top_products",
    )(top, row_weight, head, out_full, place)


def first_parts(top, row_weight, head, pre, place, blocks, step):
    rows, width = top.shape
    units = pre.shape[1]
    part = width // blocks

    def kernel(top_ref, weight_ref, head_ref, pre_ref, place_ref, dest):
        value = pre_ref[...].astype(F32)
        hidden = (value * jax.nn.sigmoid(value)).astype(BF16)
        placed = dot(hidden, place_ref[...], ROWS_OF_BOTH).astype(BF16)
        first = (top_ref[...].astype(F32) + weight_ref[...] * head_ref[...]).astype(BF16)
        total = dot(placed, first).astype(BF16)
        for b in range(step):
            dest[b] = total[:, b * part : (b + 1) * part]

    return pl.pallas_call(
        kernel,
        grid=(blocks // step,),
        out_shape=jax.ShapeDtypeStruct((blocks, units, part), BF16),
        in_specs=[
            pl.BlockSpec((rows, step * part), lambda b: (0, b)),
            pl.BlockSpec((rows, 1), lambda b: (0, 0)),
            pl.BlockSpec((1, step * part), lambda b: (0, b)),
            pl.BlockSpec((rows, units), lambda b: (0, 0)),
            pl.BlockSpec((rows, rows), lambda b: (0, 0)),
        ],
        out_specs=pl.BlockSpec((step, units, part), lambda b: (b, 0, 0)),
        name="first_parts",
    )(top, row_weight, head, pre, place)


def chain(section, known, coupled):
    count, tall, units = known.shape
    rows = tall // 2
    half = rows // 2
    blocks, _, piece, _ = coupled.shape
    pieces = units // piece

    def kernel(section_ref, known_ref, coupled_ref, dest, reach, grads):
        def pre_of(layer, other):
            return jnp.concatenate(
                [known_ref[layer, :half], known_ref[other, half:rows]], axis=0
            ).astype(F32)

        def coupling(upper, lower):
            gap = upper - lower
            if gap <= count // 2:
                at, slot = lower, gap - 1
            else:
                at, slot = upper, count - gap - 1
            return jnp.concatenate(
                [coupled_ref[slot * pieces + p, at] for p in range(pieces)], axis=0
            )

        for layer in range(count):
            reach[layer] = known_ref[layer, rows:].astype(F32)
        for layer in range(count - 1, -1, -1):
            pre = pre_of(layer, count - 1 - layer)
            sig = jax.nn.sigmoid(pre)
            grad_pre = (reach[layer] * sig * (1.0 + pre * (1.0 - sig))).astype(BF16)
            grads[layer] = grad_pre
            if layer > 0:
                lower = jnp.concatenate([coupling(layer, low) for low in range(layer)], axis=1)
                update = dot(grad_pre, lower)
                for low in range(layer):
                    reach[low] += update[:, low * units : (low + 1) * units]
        own = section_ref[0]
        far = count - 1 - own
        pre = pre_of(own, far)
        hidden = (pre * jax.nn.sigmoid(pre)).astype(BF16)
        above = jnp.concatenate(
            [grads[jnp.minimum(own + up, count - 1)] for up in range(1, count)], axis=1
        )
        cross = dot(hidden, above, ROWS_OF_BOTH)
        sent = jnp.concatenate([grads[own][:half], grads[far][half:]], axis=0)
        for up in range(count):
            if up == 0:
                dest[up, :units] = jnp.zeros((units, units), BF16)
            else:
                block = cross[:, (up - 1) * units : up * units]
                dest[up, :units] = jnp.where(own + up < count, block, 0.0).astype(BF16)
            dest[up, units:] = sent

    return pl.pallas_call(
        kernel,
        out_shape=jax.ShapeDtypeStruct((count, units + rows, units), BF16),
        in_specs=[smem(), vmem(), vmem()],
        out_specs=vmem(),
        scratch_shapes=[pltpu.VMEM((count, rows, units), F32), pltpu.VMEM((count, rows, units), BF16)],
        name="chain",
    )(section, known, coupled)


def input_grads(wide, shared, step):
    blocks, rows, part = wide.shape
    tall, units = shared.shape[1:]
    half = rows // 2
    skip = tall - rows

    def kernel(wide_ref, shared_ref, own, far, own_acc, far_acc):
        at = pl.program_id(0)

        @pl.when(at == 0)
        def _():
            own_acc[...] = jnp.zeros_like(own_acc)
            far_acc[...] = jnp.zeros_like(far_acc)

        for b in range(step):
            own_acc[...] += dot(
                shared_ref[b, skip : skip + half], wide_ref[b, :half], ROWS_OF_BOTH
            )
            far_acc[...] += dot(shared_ref[b, skip + half :], wide_ref[b, half:], ROWS_OF_BOTH)

        @pl.when(at == pl.num_programs(0) - 1)
        def _():
            own[...] = own_acc[...]
            far[...] = far_acc[...].astype(BF16)

    return pl.pallas_call(
        kernel,
        grid=(blocks // step,),
        out_shape=[
            jax.ShapeDtypeStruct((units, part), F32),
            jax.ShapeDtypeStruct((units, part), BF16),
        ],
        in_specs=[
            pl.BlockSpec((step, rows, part), lambda b: (b, 0, 0)),
            pl.BlockSpec((step, tall, units), lambda b: (b, 0, 0)),
        ],
        out_specs=[
            pl.BlockSpec((units, part), lambda b: (0, 0)),
            pl.BlockSpec((units, part), lambda b: (0, 0)),
        ],
        scratch_shapes=[pltpu.VMEM((units, part), F32), pltpu.VMEM((units, part), F32)],
        name="input_grads",
    )(wide, shared)


def output_grads(cross, firsts, near, far):
    count, units, _ = cross.shape
    blocks, _, part = firsts.shape
    slots = len(near)

    def kernel(cross_ref, first_ref, far_ref, *refs):
        dest = refs[slots]
        total = jnp.zeros((units, part), F32)
        for b in range(blocks):
            total = total + first_ref[b].astype(F32)
        for up in range(1, count):
            other = refs[up - 1][...] if up <= slots else far_ref[up - 1 - slots]
            total = total + dot(cross_ref[up], other)
        dest[...] = total

    return pl.pallas_call(
        kernel,
        out_shape=jax.ShapeDtypeStruct((units, part), F32),
        in_specs=[vmem()] * (3 + slots),
        out_specs=vmem(),
        name="output_grads",
    )(cross, firsts, far, *near)


def on_device(
    branch_in,
    branch_out,
    down_inputs,
    up_inputs,
    top_grads,
    plan,
    reward_pos,
    reward_cot,
    reward_head,
):
    count = lax.axis_size("section")
    blocks = lax.axis_size("fsdp")
    section_idx = lax.axis_index("section")
    fsdp_idx = lax.axis_index("fsdp")
    section = section_idx.astype(jnp.int32).reshape(1)
    _, micro, row_count, width = down_inputs.shape
    units = branch_in.shape[2]
    part = width // blocks
    half = micro * row_count
    rows = 2 * half
    step = 4

    in_t = branch_in[0].T
    out_t = branch_out[0]
    near = [
        from_above(jnp.where(section_idx >= up, in_t, out_t), up) for up in range(1, count // 2 + 1)
    ]
    far_in_t = mirrored(in_t)
    out_full = lax.all_gather(out_t, "fsdp", axis=0)

    narrow = jnp.concatenate(
        [down_inputs[0].reshape(half, width), up_inputs[0].reshape(half, width)], axis=0
    )
    wide = exchanged(jnp.transpose(narrow.reshape(rows, blocks, part), (1, 0, 2)), "fsdp")

    coupled = couplings(section, in_t, out_t, near, count)
    coupled = exchanged(coupled.reshape(blocks, -1, units), "fsdp")
    coupled = jnp.sum(coupled.astype(F32), axis=0).astype(BF16)
    coupled = lax.all_gather(spread(coupled, "section"), "fsdp", axis=0)
    far_near = lax.ppermute(
        jnp.stack(near[: count // 2 - 1]),
        "section",
        [(k + count // 2, k) for k in range(count // 2)],
    )

    micro_ids = jnp.arange(micro, dtype=jnp.int32)
    picked = plan[:, :, None] == micro_ids[None, None, :]
    cot_here = lax.dynamic_index_in_dim(reward_cot, fsdp_idx, 2, keepdims=False)
    pos_here = lax.dynamic_index_in_dim(reward_pos, fsdp_idx, 2, keepdims=False)
    cot_slot = jnp.sum(jnp.where(picked, cot_here[:, None, :], 0.0), axis=2)
    pos_slot = jnp.sum(jnp.where(picked, pos_here[:, None, :], 0), axis=2)
    row_ids = jnp.arange(row_count, dtype=jnp.int32)
    row_weight = jnp.where(pos_slot[:, :, None] == row_ids, cot_slot[:, :, None], 0.0)
    row_weight = row_weight.reshape(rows, 1)
    target = (jnp.arange(2, dtype=jnp.int32)[:, None] * micro + plan)[:, :, None] * row_count
    target = (target + row_ids).reshape(rows)
    place = (jnp.arange(rows, dtype=jnp.int32)[:, None] == target[None, :]).astype(BF16)
    top = top_grads.reshape(rows, width)
    head = reward_head.reshape(1, width)

    reached = top_products(top, row_weight, head, out_full, place, step)
    pre = exchanged(pre_parts(wide, in_t, far_in_t, step), "fsdp")
    pre = jnp.sum(pre.astype(F32), axis=0).astype(BF16)
    known = spread(jnp.concatenate([pre, reached], axis=0), "section")

    mirror_pre = lax.dynamic_index_in_dim(known, count - 1 - section_idx, 0, keepdims=False)
    own_pre = jnp.concatenate([pre[:half], mirror_pre[half:rows]], axis=0)
    firsts = exchanged(
        first_parts(top, row_weight, head, own_pre, place, blocks, step), "fsdp"
    )

    shared = exchanged(chain(section, known, coupled), "fsdp")
    own_in, far_in = input_grads(wide, shared, step)
    back_in = mirrored(far_in)
    cross = jnp.sum(shared[:, :units].astype(F32), axis=0).astype(BF16)
    cross = spread(cross, "fsdp")
    grad_out = output_grads(cross, firsts, near, far_near)
    grad_in = (own_in + back_in.astype(F32)).T
    return (grad_in[None], grad_out[None])


def solution(mesh):
    in_specs = (
        P("section", "fsdp", None),
        P("section", None, "fsdp"),
        P("section", None, "fsdp", None),
        P("section", None, "fsdp", None),
        P(None, None, "fsdp", None),
        P(),
        P(),
        P(),
        P(),
    )
    out_specs = (P("section", "fsdp", None), P("section", None, "fsdp"))
    return jax.shard_map(
        on_device, mesh=mesh, in_specs=in_specs, out_specs=out_specs, check_vma=False
    )
```

time: 1440 us -> 334 us (0.23)
  waiting for transfers between devices: 661 us -> 105 us
  starting transfers between devices: 313 us -> 64.7 us
  matrix products: 199 us -> 0 us
  local copies, waits for them, and re-layouts: 149 us -> 21.2 us
  blocking collectives: 0 us -> 83.4 us
  loops' own time: 53.4 us -> 0 us
  other arithmetic: 48.8 us -> 6.94 us
  Pallas kernels: 0 us -> 34.1 us
    ppermute x62 -> x11, starting transfers between devices: 312 us -> 39.7 us  [the longest x8 25.4 us: from_above(): lax.ppermute(value, 'section', [((k + steps) % count, k) for k in range(c...]
    reduce_scatter x4 -> x0, waiting for transfers between devices: 270 us -> none  [the longest x1 115 us: on_device(): lax.psum_scatter(state_up[0].astype(jnp.bfloat16), 'fsdp', scatter_dimens...]
    ppermute x62 -> x11, waiting for transfers between devices: 285 us -> 24.4 us  [the longest x2 14.1 us: mirrored(): lax.ppermute(value, 'section', [(k, count - 1 - k) for k in range(count)])]
    dot_general x120 -> x0, matrix products: 199 us -> none  [the longest x24 73.4 us: active(): lax.dot_general(rows_in, grad_pre, (((0,), (0,)), ((), ())), preferred_el...]
    all_gather x4 -> x2, waiting for transfers between devices: 103 us -> 0.02 us  [the longest x1 0.02 us: on_device(): out_full = lax.all_gather(out_t, 'fsdp', axis=0)]
    all_to_all x0 -> x3, blocking collectives: none -> 83.4 us  [exchanged(): return lax.all_to_all(parts, axis, 0, 0, tiled=True)]
    cond x240 -> x0, local copies, waits for them, and re-layouts: 81.5 us -> none
    all_to_all x0 -> x5, waiting for transfers between devices: none -> 80.3 us  [exchanged(): return lax.all_to_all(parts, axis, 0, 0, tiled=True)]
  transfers between devices with their start and end apart: 70 -> 18, of which waited for: 56 -> 10; matrix products, arithmetic and copies ran while one was open for 12% -> 7% of each run, Pallas kernels for 0% -> 7%
where the time goes in v1:
time: 334 us; the launch traced here: 330 us
  waiting for transfers between devices  105 us (31%)
  blocking collectives  83.4 us (25%)
  starting transfers between devices  64.7 us (19%)
  Pallas kernels  34.1 us (10%)
  local copies, waits for them, and re-layouts  21.2 us (6%)
  between operations  14.4 us (4%)
  other arithmetic  6.94 us (2%)
    all_to_all x3, blocking collectives, exchanged(): return lax.all_to_all(parts, axis, 0, 0, tiled=True)  83.4 us
    all_to_all x5, waiting for transfers between devices, exchanged(): return lax.all_to_all(parts, axis, 0, 0, tiled=True)  80.3 us
    ppermute x8, starting transfers between devices, from_above(): lax.ppermute(value, 'section', [((k + steps) % count, k) for k in range(c...  25.4 us
    all_to_all x5, starting transfers between devices, exchanged(): return lax.all_to_all(parts, axis, 0, 0, tiled=True)  25 us
    unnamed x55, local copies, waits for them, and re-layouts  15.3 us
    ppermute x2, waiting for transfers between devices, mirrored(): lax.ppermute(value, 'section', [(k, count - 1 - k) for k in range(count)])  14.1 us
    ppermute x8, waiting for transfers between devices, from_above(): lax.ppermute(value, 'section', [((k + steps) % count, k) for k in range(c...  10.3 us
    ppermute x2, starting transfers between devices, mirrored(): lax.ppermute(value, 'section', [(k, count - 1 - k) for k in range(count)])  9.34 us
  transfers between devices with their start and end apart: 18, of which 10 were waited for; matrix products, arithmetic and copies ran while one was open for 7% of the time, Pallas kernels for 7%

profile of v1, /device:TPU:16, one launch (start us, length us, event | category | flops | bytes accessed | tf_op | source)
XLA Modules:
  0.0 330.1 jit_solution(8886498766210287799)
XLA Ops:
  10.0 5.7 %collective-permute-start.1 = (bf16[128,512]{1,0:T(8,128)(2,1)S(1)}, bf16[128,512]{1,0:T(8,128)(2,1)S(1)}, u32[]{:S(2)}, u32[]{:S(2)}) collective-permute-start(bf16[128,512]{1,0:T(8,128)(2,1)S(1)} %get-tuple-element.15), channel_id=1, source_target_pairs={{16,0},{32,16},{48,32},{64,48},{80,64},{96,80},{112,96},{128,112},... | collective-permute-start | bytes 393224 | tf_op jit(solution)/shard_map/ppermute | solution.py:20
  17.6 7.7 %collective-permute-start.4 = (bf16[128,512]{1,0:T(8,128)(2,1)S(1)}, bf16[128,512]{1,0:T(8,128)(2,1)S(1)}, u32[]{:S(2)}, u32[]{:S(2)}) collective-permute-start(bf16[128,512]{1,0:T(8,128)(2,1)S(1)} %get-tuple-element.18), channel_id=1, source_target_pairs={{64,0},{80,16},{96,32},{112,48},{128,64},{144,80},{160,96},{176,11... | collective-permute-start | bytes 393224 | tf_op jit(solution)/shard_map/ppermute | solution.py:20
  27.6 4.5 %collective-permute-start.7 = (bf16[128,512]{1,0:T(8,128)(2,1)S(1)}, bf16[128,512]{1,0:T(8,128)(2,1)S(1)}, u32[]{:S(2)}, u32[]{:S(2)}) collective-permute-start(bf16[128,512]{1,0:T(8,128)(2,1)S(1)} %get-tuple-element.21), channel_id=1, source_target_pairs={{112,0},{128,16},{144,32},{160,48},{176,64},{192,80},{208,96},{224... | collective-permute-start | bytes 393224 | tf_op jit(solution)/shard_map/ppermute | solution.py:20
  32.1 6.1 %collective-permute-done.3.refs_2_ = bf16[128,512]{1,0:T(8,128)(2,1)S(1)} collective-permute-done((bf16[128,512]{1,0:T(8,128)(2,1)S(1)}, bf16[128,512]{1,0:T(8,128)(2,1)S(1)}, u32[]{:S(2)}, u32[]{:S(2)}) %collective-permute-start.3) | collective-permute-done | bytes 131104 | tf_op jit(solution)/shard_map/ppermute | solution.py:20
  50.2 13.7 %all_to_all.40 = bf16[16,64,128]{2,1,0:T(8,128)(2,1)S(1)} all-to-all(bf16[16,64,128]{2,1,0:T(8,128)(2,1)} %bitcast.69), channel_id=1, replica_groups=mesh['section'=16,'fsdp'=16] {'fsdp'}, dimensions={0} | all-to-all | bytes 524288 | tf_op jit(solution)/shard_map/all_to_all | solution.py:29
  63.9 24.3 %all_to_all.41 = bf16[16,64,128]{2,1,0:T(8,128)(2,1)} all-to-all(bf16[16,64,128]{2,1,0:T(8,128)(2,1)S(1)} %broadcast_in_dim.84), channel_id=1, replica_groups=mesh['section'=16,'fsdp'=16] {'section'}, dimensions={0} | all-to-all | bytes 524288 | tf_op jit(solution)/shard_map/all_to_all | solution.py:29
  97.5 4.8 %collective-permute-start = (bf16[128,512]{1,0:T(8,128)(2,1)S(1)}, bf16[128,512]{1,0:T(8,128)(2,1)S(1)}, u32[]{:S(2)}, u32[]{:S(2)}) collective-permute-start(bf16[128,512]{1,0:T(8,128)(2,1)S(1)} %bitcast.65), channel_id=1, source_target_pairs={{0,240},{16,224},{32,208},{48,192},{64,176},{80,160},{96,144},{112... | collective-permute-start | bytes 393224 | tf_op jit(solution)/shard_map/ppermute | solution.py:25
  104.3 6.0 %collective-permute-done.far_ref = bf16[128,512]{1,0:T(8,128)(2,1)S(1)} collective-permute-done((bf16[128,512]{1,0:T(8,128)(2,1)S(1)}, bf16[128,512]{1,0:T(8,128)(2,1)S(1)}, u32[]{:S(2)}, u32[]{:S(2)}) %collective-permute-start) | collective-permute-done | bytes 131104 | tf_op jit(solution)/shard_map/ppermute | solution.py:25
  110.2 40.8 %all-to-all-done.wide_ref = bf16[16,192,512]{2,1,0:T(8,128)(2,1)S(1)} async-done(((bf16[16,192,512]{2,1,0:T(8,128)(2,1)}), bf16[16,192,512]{2,1,0:T(8,128)(2,1)S(1)}, u32[]{:S(2)}, u32[]{:S(2)}) %all-to-all-start) | async-done | bytes 3145760 | tf_op jit(solution)/shard_map/all_to_all | solution.py:29
  152.8 4.7 %pre_parts.1 = bf16[16,192,128]{2,1,0:T(8,128)(2,1)} custom-call(bf16[16,192,512]{2,1,0:T(8,128)(2,1)} %copy-done.1, bf16[128,512]{1,0:T(8,128)(2,1)} %bitcast.64, bf16[128,512]{1,0:T(8,128)(2,1)} %copy-done.19), custom_call_target="tpu_custom_call" | custom-call | tf_op jit(solution)/shard_map/pre_parts/pallas_call | solution.py:80
  157.5 8.1 %all-to-all-start.1 = ((bf16[16,192,128]{2,1,0:T(8,128)(2,1)}), bf16[16,192,128]{2,1,0:T(8,128)(2,1)S(1)}, u32[]{:S(2)}, u32[]{:S(2)}) async-start(bf16[16,192,128]{2,1,0:T(8,128)(2,1)} %pre_parts.1), calls=%async_computation.1 | async-start | bytes 1572864 | tf_op jit(solution)/shard_map/all_to_all | solution.py:29
  166.5 12.7 %all-to-all-done.1 = bf16[16,192,128]{2,1,0:T(8,128)(2,1)S(1)} async-done(((bf16[16,192,128]{2,1,0:T(8,128)(2,1)}), bf16[16,192,128]{2,1,0:T(8,128)(2,1)S(1)}, u32[]{:S(2)}, u32[]{:S(2)}) %all-to-all-start.1) | async-done | bytes 786464 | tf_op jit(solution)/shard_map/all_to_all | solution.py:29
  179.4 4.9 %top_products.1 = bf16[192,128]{1,0:T(8,128)(2,1)} custom-call(bf16[192,8192]{1,0:T(8,128)(2,1)} %bitcast.58, f32[192,1]{1,0:T(8,128)} %select_n.104.weight_ref, f32[1,8192]{1,0:T(1,128)} %bitcast.71, bf16[16,128,512]{2,1,0:T(8,128)(2,1)} %all-gather.4.cloned.1.call-done.out_ref, bf16[192,192]{1,0:T(8,128)(2,1)} %fusion.place_ref), custom_call_target="tpu_custom_call" | custom-call | tf_op jit(solution)/shard_map/top_products/pallas_call | solution.py:115
  185.4 45.5 %all_to_all.42.known_ref = bf16[16,384,128]{2,1,0:T(8,128)(2,1)} all-to-all(bf16[16,384,128]{2,1,0:T(8,128)(2,1)S(1)} %broadcast_in_dim.83), channel_id=1, replica_groups=mesh['section'=16,'fsdp'=16] {'section'}, dimensions={0} | all-to-all | bytes 3145728 | tf_op jit(solution)/shard_map/all_to_all | solution.py:29
  230.8 7.3 %chain.1 = bf16[16,320,128]{2,1,0:T(8,128)(2,1)} custom-call(s32[1]{0:T(128)} %bitcast.1.section_ref, bf16[16,384,128]{2,1,0:T(8,128)(2,1)} %all_to_all.42.known_ref, bf16[16,16,64,128]{3,2,1,0:T(8,128)(2,1)} %bitcast.62), custom_call_target="tpu_custom_call" | custom-call | tf_op jit(solution)/shard_map/chain/pallas_call | solution.py:214
  238.2 4.3 %all-to-all-start.5 = ((bf16[16,320,128]{2,1,0:T(8,128)(2,1)}), bf16[16,320,128]{2,1,0:T(8,128)(2,1)S(1)}, u32[]{:S(2)}, u32[]{:S(2)}) async-start(bf16[16,320,128]{2,1,0:T(8,128)(2,1)} %chain.1), calls=%async_computation.5 | async-start | bytes 2621440 | tf_op jit(solution)/shard_map/all_to_all | solution.py:29
  243.9 5.0 %first_parts.1 = bf16[16,128,512]{2,1,0:T(8,128)(2,1)} custom-call(bf16[192,8192]{1,0:T(8,128)(2,1)} %bitcast.59, f32[192,1]{1,0:T(8,128)} %select_n.104.weight_ref, f32[1,8192]{1,0:T(1,128)} %bitcast.72, bf16[192,128]{1,0:T(8,128)(2,1)} %pad_maximum_fusion.1.pre_ref, bf16[192,192]{1,0:T(8,128)(2,1)} %fusion.place_ref), custom_call_target="tpu_custom_call" | custom-call | tf_op jit(solution)/shard_map/first_parts/pallas_call | solution.py:146
  248.9 12.9 %all-to-all-done.5.shared_ref = bf16[16,320,128]{2,1,0:T(8,128)(2,1)S(1)} async-done(((bf16[16,320,128]{2,1,0:T(8,128)(2,1)}), bf16[16,320,128]{2,1,0:T(8,128)(2,1)S(1)}, u32[]{:S(2)}, u32[]{:S(2)}) %all-to-all-start.5) | async-done | bytes 1310752 | tf_op jit(solution)/shard_map/all_to_all | solution.py:29
  274.7 5.0 %collective-permute-start.10 = (bf16[7,128,512]{2,1,0:T(8,128)(2,1)}, bf16[7,128,512]{2,1,0:T(8,128)(2,1)}, u32[]{:S(2)}, u32[]{:S(2)}) collective-permute-start(bf16[7,128,512]{2,1,0:T(8,128)(2,1)} %bitcast_dynamic-update-slice_fusion), channel_id=1, source_target_pairs={{128,0},{144,16},{160,32},{176,48},{192,64},{208,80},{224,96},{240... | collective-permute-start | bytes 2752520 | tf_op jit(solution)/shard_map/ppermute | solution.py:333
  279.7 13.4 %all-to-all-done.7.first_ref = bf16[16,128,512]{2,1,0:T(8,128)(2,1)S(1)} async-done(((bf16[16,128,512]{2,1,0:T(8,128)(2,1)}), bf16[16,128,512]{2,1,0:T(8,128)(2,1)S(1)}, u32[]{:S(2)}, u32[]{:S(2)}) %all-to-all-start.7) | async-done | bytes 2097184 | tf_op jit(solution)/shard_map/all_to_all | solution.py:29
  294.1 4.9 %all-to-all-start.6 = ((bf16[16,128,128]{2,1,0:T(8,128)(2,1)}), bf16[16,128,128]{2,1,0:T(8,128)(2,1)S(1)}, u32[]{:S(2)}, u32[]{:S(2)}) async-start(bf16[16,128,128]{2,1,0:T(8,128)(2,1)} %broadcast_in_dim.86), calls=%async_computation.6 | async-start | bytes 1048576 | tf_op jit(solution)/shard_map/all_to_all | solution.py:29
  299.1 4.7 %input_grads.1 = (f32[128,512]{1,0:T(8,128)}, bf16[128,512]{1,0:T(8,128)(2,1)}) custom-call(bf16[16,192,512]{2,1,0:T(8,128)(2,1)} %copy-done.1, bf16[16,320,128]{2,1,0:T(8,128)(2,1)} %copy-done.3), custom_call_target="tpu_custom_call" | custom-call | tf_op jit(solution)/shard_map/input_grads/pallas_call | solution.py:249
  303.8 4.5 %collective-permute-start.9 = (bf16[128,512]{1,0:T(8,128)(2,1)}, bf16[128,512]{1,0:T(8,128)(2,1)S(1)}, u32[]{:S(2)}, u32[]{:S(2)}) collective-permute-start(bf16[128,512]{1,0:T(8,128)(2,1)} %get-tuple-element.5), channel_id=1, source_target_pairs={{0,240},{16,224},{32,208},{48,192},{64,176},{80,160},{96,144},{112... | collective-permute-start | bytes 393224 | tf_op jit(solution)/shard_map/ppermute | solution.py:25
  308.3 8.1 %collective-permute-done.9 = bf16[128,512]{1,0:T(8,128)(2,1)S(1)} collective-permute-done((bf16[128,512]{1,0:T(8,128)(2,1)}, bf16[128,512]{1,0:T(8,128)(2,1)S(1)}, u32[]{:S(2)}, u32[]{:S(2)}) %collective-permute-start.9) | collective-permute-done | bytes 131104 | tf_op jit(solution)/shard_map/ppermute | solution.py:25
  (110 shorter events, 56.1 us)
Async XLA Ops:
  7.2 95.1 %copy-start = (f32[2,12,16]{2,0,1:T(2,128)S(1)}, f32[2,12,16]{2,0,1:T(2,128)}, u32[]{:S(2)}) copy-start(f32[2,12,16]{2,0,1:T(2,128)} %param.16) | copy-start | bytes 4612
  7.2 172.2 %all-gather.4.cloned.1.call-start = ((), (), s32[]{:S(2)}) async-start(), calls=%async_computation.8 | async-start | bytes 2228224 | tf_op jit(solution)/shard_map/all_gather | solution.py:322
  7.9 222.9 %all-gather.6.cloned.1.call-start = ((), (), s32[]{:S(2)}) async-start(), calls=%async_computation.9 | async-start | bytes 4456448 | tf_op jit(solution)/shard_map/all_gather | solution.py:332
  9.0 36.8 %copy-start.4 = (bf16[1,512,128]{1,2,0:T(8,128)(2,1)}, bf16[1,512,128]{1,2,0:T(8,128)(2,1)S(1)}, u32[]{:S(2)}) copy-start(bf16[1,512,128]{1,2,0:T(8,128)(2,1)S(1)} %copy.33) | copy-start | bytes 393220
  10.0 15.3 %collective-permute-start.1 = (bf16[128,512]{1,0:T(8,128)(2,1)S(1)}, bf16[128,512]{1,0:T(8,128)(2,1)S(1)}, u32[]{:S(2)}, u32[]{:S(2)}) collective-permute-start(bf16[128,512]{1,0:T(8,128)(2,1)S(1)} %get-tuple-element.15), channel_id=1, source_target_pairs={{16,0},{32,16},{48,32},{64,48},{80,64},{96,80},{112,96},{128,112},... | collective-permute-start | bytes 393224 | tf_op jit(solution)/shard_map/ppermute | solution.py:20
  15.7 11.8 %collective-permute-start.2 = (bf16[128,512]{1,0:T(8,128)(2,1)S(1)}, bf16[128,512]{1,0:T(8,128)(2,1)S(1)}, u32[]{:S(2)}, u32[]{:S(2)}) collective-permute-start(bf16[128,512]{1,0:T(8,128)(2,1)S(1)} %get-tuple-element.16), channel_id=1, source_target_pairs={{32,0},{48,16},{64,32},{80,48},{96,64},{112,80},{128,96},{144,112}... | collective-permute-start | bytes 393224 | tf_op jit(solution)/shard_map/ppermute | solution.py:20
  17.2 21.0 %collective-permute-start.3 = (bf16[128,512]{1,0:T(8,128)(2,1)S(1)}, bf16[128,512]{1,0:T(8,128)(2,1)S(1)}, u32[]{:S(2)}, u32[]{:S(2)}) collective-permute-start(bf16[128,512]{1,0:T(8,128)(2,1)S(1)} %get-tuple-element.17), channel_id=1, source_target_pairs={{48,0},{64,16},{80,32},{96,48},{112,64},{128,80},{144,96},{160,112... | collective-permute-start | bytes 393224 | tf_op jit(solution)/shard_map/ppermute | solution.py:20
  17.6 23.9 %collective-permute-start.4 = (bf16[128,512]{1,0:T(8,128)(2,1)S(1)}, bf16[128,512]{1,0:T(8,128)(2,1)S(1)}, u32[]{:S(2)}, u32[]{:S(2)}) collective-permute-start(bf16[128,512]{1,0:T(8,128)(2,1)S(1)} %get-tuple-element.18), channel_id=1, source_target_pairs={{64,0},{80,16},{96,32},{112,48},{128,64},{144,80},{160,96},{176,11... | collective-permute-start | bytes 393224 | tf_op jit(solution)/shard_map/ppermute | solution.py:20
  25.3 16.2 %collective-permute-start.5 = (bf16[128,512]{1,0:T(8,128)(2,1)S(1)}, bf16[128,512]{1,0:T(8,128)(2,1)S(1)}, u32[]{:S(2)}, u32[]{:S(2)}) collective-permute-start(bf16[128,512]{1,0:T(8,128)(2,1)S(1)} %get-tuple-element.19), channel_id=1, source_target_pairs={{80,0},{96,16},{112,32},{128,48},{144,64},{160,80},{176,96},{192,1... | collective-permute-start | bytes 393224 | tf_op jit(solution)/shard_map/ppermute | solution.py:20
  25.3 20.4 %copy-start.9 = (bf16[128,512]{1,0:T(8,128)(2,1)}, bf16[128,512]{1,0:T(8,128)(2,1)S(1)}, u32[]{:S(2)}) copy-start(bf16[128,512]{1,0:T(8,128)(2,1)S(1)} %collective-permute-done.1.refs_0_) | copy-start | bytes 393220
  25.3 17.4 %collective-permute-start.6 = (bf16[128,512]{1,0:T(8,128)(2,1)S(1)}, bf16[128,512]{1,0:T(8,128)(2,1)S(1)}, u32[]{:S(2)}, u32[]{:S(2)}) collective-permute-start(bf16[128,512]{1,0:T(8,128)(2,1)S(1)} %get-tuple-element.20), channel_id=1, source_target_pairs={{96,0},{112,16},{128,32},{144,48},{160,64},{176,80},{192,96},{208,... | collective-permute-start | bytes 393224 | tf_op jit(solution)/shard_map/ppermute | solution.py:20
  27.6 18.2 %copy-start.11 = (bf16[128,512]{1,0:T(8,128)(2,1)}, bf16[128,512]{1,0:T(8,128)(2,1)S(1)}, u32[]{:S(2)}) copy-start(bf16[128,512]{1,0:T(8,128)(2,1)S(1)} %collective-permute-done.2.refs_1_) | copy-start | bytes 393220
  27.6 18.2 %collective-permute-start.7 = (bf16[128,512]{1,0:T(8,128)(2,1)S(1)}, bf16[128,512]{1,0:T(8,128)(2,1)S(1)}, u32[]{:S(2)}, u32[]{:S(2)}) collective-permute-start(bf16[128,512]{1,0:T(8,128)(2,1)S(1)} %get-tuple-element.21), channel_id=1, source_target_pairs={{112,0},{128,16},{144,32},{160,48},{176,64},{192,80},{208,96},{224... | collective-permute-start | bytes 393224 | tf_op jit(solution)/shard_map/ppermute | solution.py:20
  38.2 7.5 %collective-permute-start.8 = (bf16[128,512]{1,0:T(8,128)(2,1)S(1)}, bf16[128,512]{1,0:T(8,128)(2,1)S(1)}, u32[]{:S(2)}, u32[]{:S(2)}) collective-permute-start(bf16[128,512]{1,0:T(8,128)(2,1)S(1)} %get-tuple-element.14), channel_id=1, source_target_pairs={{128,0},{144,16},{160,32},{176,48},{192,64},{208,80},{224,96},{240... | collective-permute-start | bytes 393224 | tf_op jit(solution)/shard_map/ppermute | solution.py:20
  46.4 41.8 %copy-start.7 = (bf16[1,12,8,8192]{3,2,1,0:T(8,128)(2,1)S(1)}, bf16[1,12,8,8192]{3,2,1,0:T(8,128)(2,1)}, u32[]{:S(2)}) copy-start(bf16[1,12,8,8192]{3,2,1,0:T(8,128)(2,1)} %param.12) | copy-start | bytes 4718596
  93.6 57.5 %all-to-all-start = ((bf16[16,192,512]{2,1,0:T(8,128)(2,1)}), bf16[16,192,512]{2,1,0:T(8,128)(2,1)S(1)}, u32[]{:S(2)}, u32[]{:S(2)}) async-start(bf16[16,192,512]{2,1,0:T(8,128)(2,1)} %maximum_bitcast_fusion), calls=%async_computation | async-start | bytes 6291456 | tf_op jit(solution)/shard_map/all_to_all | solution.py:29
  97.5 12.8 %collective-permute-start = (bf16[128,512]{1,0:T(8,128)(2,1)S(1)}, bf16[128,512]{1,0:T(8,128)(2,1)S(1)}, u32[]{:S(2)}, u32[]{:S(2)}) collective-permute-start(bf16[128,512]{1,0:T(8,128)(2,1)S(1)} %bitcast.65), channel_id=1, source_target_pairs={{0,240},{16,224},{32,208},{48,192},{64,176},{80,160},{96,144},{112... | collective-permute-start | bytes 393224 | tf_op jit(solution)/shard_map/ppermute | solution.py:25
  110.2 40.8 %copy-start.19 = (bf16[128,512]{1,0:T(8,128)(2,1)}, bf16[128,512]{1,0:T(8,128)(2,1)S(1)}, u32[]{:S(2)}) copy-start(bf16[128,512]{1,0:T(8,128)(2,1)S(1)} %collective-permute-done.far_ref) | copy-start | bytes 393220
  157.5 21.8 %all-to-all-start.1 = ((bf16[16,192,128]{2,1,0:T(8,128)(2,1)}), bf16[16,192,128]{2,1,0:T(8,128)(2,1)S(1)}, u32[]{:S(2)}, u32[]{:S(2)}) async-start(bf16[16,192,128]{2,1,0:T(8,128)(2,1)} %pre_parts.1), calls=%async_computation.1 | async-start | bytes 1572864 | tf_op jit(solution)/shard_map/all_to_all | solution.py:29
  238.2 23.6 %all-to-all-start.5 = ((bf16[16,320,128]{2,1,0:T(8,128)(2,1)}), bf16[16,320,128]{2,1,0:T(8,128)(2,1)S(1)}, u32[]{:S(2)}, u32[]{:S(2)}) async-start(bf16[16,320,128]{2,1,0:T(8,128)(2,1)} %chain.1), calls=%async_computation.5 | async-start | bytes 2621440 | tf_op jit(solution)/shard_map/all_to_all | solution.py:29
  261.8 31.4 %all-to-all-start.7 = ((bf16[16,128,512]{2,1,0:T(8,128)(2,1)}), bf16[16,128,512]{2,1,0:T(8,128)(2,1)S(1)}, u32[]{:S(2)}, u32[]{:S(2)}) async-start(bf16[16,128,512]{2,1,0:T(8,128)(2,1)} %first_parts.1), calls=%async_computation.7 | async-start | bytes 4194304 | tf_op jit(solution)/shard_map/all_to_all | solution.py:29
  274.7 43.6 %collective-permute-start.10 = (bf16[7,128,512]{2,1,0:T(8,128)(2,1)}, bf16[7,128,512]{2,1,0:T(8,128)(2,1)}, u32[]{:S(2)}, u32[]{:S(2)}) collective-permute-start(bf16[7,128,512]{2,1,0:T(8,128)(2,1)} %bitcast_dynamic-update-slice_fusion), channel_id=1, source_target_pairs={{128,0},{144,16},{160,32},{176,48},{192,64},{208,80},{224,96},{240... | collective-permute-start | bytes 2752520 | tf_op jit(solution)/shard_map/ppermute | solution.py:333
  294.1 24.6 %all-to-all-start.6 = ((bf16[16,128,128]{2,1,0:T(8,128)(2,1)}), bf16[16,128,128]{2,1,0:T(8,128)(2,1)S(1)}, u32[]{:S(2)}, u32[]{:S(2)}) async-start(bf16[16,128,128]{2,1,0:T(8,128)(2,1)} %broadcast_in_dim.86), calls=%async_computation.6 | async-start | bytes 1048576 | tf_op jit(solution)/shard_map/all_to_all | solution.py:29
  303.8 12.6 %collective-permute-start.9 = (bf16[128,512]{1,0:T(8,128)(2,1)}, bf16[128,512]{1,0:T(8,128)(2,1)S(1)}, u32[]{:S(2)}, u32[]{:S(2)}) collective-permute-start(bf16[128,512]{1,0:T(8,128)(2,1)} %get-tuple-element.5), channel_id=1, source_target_pairs={{0,240},{16,224},{32,208},{48,192},{64,176},{80,160},{96,144},{112... | collective-permute-start | bytes 393224 | tf_op jit(solution)/shard_map/ppermute | solution.py:25
  (16 other events, 100.1 us)
Sparse Core Ops, SparseCore 0:
  9.8 39.1 all-gather.3
  88.4 71.0 all-gather.5

commit v2 on v1

--- a/solution.py
+++ b/solution.py
@@ -5,6 +5,7 @@
 from jax.experimental.pallas import tpu as pltpu
 from jax.sharding import PartitionSpec as P
 
+
 BF16 = jnp.bfloat16
 F32 = jnp.float32
 ROWS_OF_BOTH = (((0,), (0,)), ((), ()))
@@ -25,12 +26,22 @@
     return lax.ppermute(value, "section", [(k, count - 1 - k) for k in range(count)])
 
 
-def exchanged(parts, axis):
-    return lax.all_to_all(parts, axis, 0, 0, tiled=True)
-
-
-def spread(value, axis):
-    return exchanged(jnp.broadcast_to(value[None], (lax.axis_size(axis),) + value.shape), axis)
+def exchanged(parts, axis, groups=None):
+    return lax.all_to_all(parts, axis, 0, 0, axis_index_groups=groups, tiled=True)
+
+
+def crossed(value, mask):
+    count = lax.axis_size("section")
+    return lax.ppermute(value, "section", [(k, k ^ mask) for k in range(count)])
+
+
+def same_core(count):
+    return [list(range(core, count, 2)) for core in range(2)]
+
+
+def from_other_core(value):
+    count = lax.axis_size("fsdp")
+    return lax.ppermute(value, "fsdp", [(f, f ^ 1) for f in range(count)])
 
 
 def vmem():
@@ -46,7 +57,9 @@
     slots = len(near)
 
     def kernel(section_ref, in_ref, out_ref, *refs):
-        dest = refs[slots]
+        dest, packed = refs[slots:]
+        for slot in range(slots - 1):
+            packed[slot] = refs[slot][...]
         for slot in range(slots):
             wrapped = section_ref[0] + slot + 1 >= count
 
@@ -60,11 +73,96 @@
 
     return pl.pallas_call(
         kernel,
-        out_shape=jax.ShapeDtypeStruct((slots, units, units), BF16),
+        out_shape=[
+            jax.ShapeDtypeStruct((slots, units, units), BF16),
+            jax.ShapeDtypeStruct((slots - 1,) + in_t.shape, BF16),
+        ],
         in_specs=[smem()] + [vmem()] * (2 + slots),
-        out_specs=vmem(),
+        out_specs=[vmem(), vmem()],
         name="couplings",
     )(section, in_t, out_t, *near)
+
+
+def laid_out(down, up, blocks, step):
+    half, width = down.shape
+    part = width // blocks
+
+    def kernel(down_ref, up_ref, dest):
+        for b in range(step):
+            dest[b, :half] = down_ref[:, b * part : (b + 1) * part]
+            dest[b, half:] = up_ref[:, b * part : (b + 1) * part]
+
+    return pl.pallas_call(
+        kernel,
+        grid=(blocks // step,),
+        out_shape=jax.ShapeDtypeStruct((blocks, 2 * half, part), BF16),
+        in_specs=[pl.BlockSpec((half, step * part), lambda b: (0, b))] * 2,
+        out_specs=pl.BlockSpec((step, 2 * half, part), lambda b: (b, 0, 0)),
+        name="laid_out",
+    )(down, up)
+
+
+def stacked(pieces):
+    count = len(pieces)
+    length = pieces[0].shape[0]
+
+    def kernel(*refs):
+        for at in range(count):
+            refs[count][at * length : (at + 1) * length] = refs[at][...]
+
+    return pl.pallas_call(
+        kernel,
+        out_shape=jax.ShapeDtypeStruct((count * length,) + pieces[0].shape[1:], BF16),
+        in_specs=[vmem()] * count,
+        out_specs=vmem(),
+        name="stacked",
+    )(*pieces)
+
+
+def folded(parts, copies, used):
+    blocks, _, units = parts.shape
+
+    def kernel(parts_ref, dest):
+        total = parts_ref[0, :used].astype(F32)
+        for b in range(1, blocks):
+            total = total + parts_ref[b, :used].astype(F32)
+        total = total.astype(BF16)
+        for c in range(copies):
+            dest[c] = total
+
+    return pl.pallas_call(
+        kernel,
+        out_shape=jax.ShapeDtypeStruct((copies, used, units), BF16),
+        in_specs=[vmem()],
+        out_specs=vmem(),
+        name="folded",
+    )(parts)
+
+
+def folded_with(parts, below, copies):
+    blocks, rows, units = parts.shape
+
+    def kernel(parts_ref, below_ref, dest, own):
+        total = parts_ref[0].astype(F32)
+        for b in range(1, blocks):
+            total = total + parts_ref[b].astype(F32)
+        total = total.astype(BF16)
+        own[0] = total[: rows // 2]
+        own[1] = total[rows // 2 :]
+        for c in range(copies):
+            dest[c, :rows] = total
+            dest[c, rows:] = below_ref[...]
+
+    return pl.pallas_call(
+        kernel,
+        out_shape=[
+            jax.ShapeDtypeStruct((copies, 2 * rows, units), BF16),
+            jax.ShapeDtypeStruct((2, rows // 2, units), BF16),
+        ],
+        in_specs=[vmem(), vmem()],
+        out_specs=[vmem(), vmem()],
+        name="folded_with",
+    )(parts, below)
 
 
 def pre_parts(wide, in_t, far_in_t, step):
@@ -129,13 +227,13 @@
     )(top, row_weight, head, out_full, place)
 
 
-def first_parts(top, row_weight, head, pre, place, blocks, step):
+def first_parts(top, row_weight, head, pre_down, pre_up, place, blocks, step):
     rows, width = top.shape
-    units = pre.shape[1]
+    half, units = pre_down.shape
     part = width // blocks
 
-    def kernel(top_ref, weight_ref, head_ref, pre_ref, place_ref, dest):
-        value = pre_ref[...].astype(F32)
+    def kernel(top_ref, weight_ref, head_ref, down_ref, up_ref, place_ref, dest):
+        value = jnp.concatenate([down_ref[...], up_ref[...]], axis=0).astype(F32)
         hidden = (value * jax.nn.sigmoid(value)).astype(BF16)
         placed = dot(hidden, place_ref[...], ROWS_OF_BOTH).astype(BF16)
         first = (top_ref[...].astype(F32) + weight_ref[...] * head_ref[...]).astype(BF16)
@@ -151,22 +249,24 @@
             pl.BlockSpec((rows, step * part), lambda b: (0, b)),
             pl.BlockSpec((rows, 1), lambda b: (0, 0)),
             pl.BlockSpec((1, step * part), lambda b: (0, b)),
-            pl.BlockSpec((rows, units), lambda b: (0, 0)),
+            pl.BlockSpec((half, units), lambda b: (0, 0)),
+            pl.BlockSpec((half, units), lambda b: (0, 0)),
             pl.BlockSpec((rows, rows), lambda b: (0, 0)),
         ],
         out_specs=pl.BlockSpec((step, units, part), lambda b: (b, 0, 0)),
         name="first_parts",
-    )(top, row_weight, head, pre, place)
-
-
-def chain(section, known, coupled):
+    )(top, row_weight, head, pre_down, pre_up, place)
+
+
+def chain(section, core, known, same, other):
     count, tall, units = known.shape
     rows = tall // 2
     half = rows // 2
-    blocks, _, piece, _ = coupled.shape
-    pieces = units // piece
-
-    def kernel(section_ref, known_ref, coupled_ref, dest, reach, grads):
+
+    def kernel(section_ref, core_ref, known_ref, same_ref, other_ref, dest, reach, grads):
+        even = core_ref[0] == 0
+        own = section_ref[0]
+
         def pre_of(layer, other):
             return jnp.concatenate(
                 [known_ref[layer, :half], known_ref[other, half:rows]], axis=0
@@ -178,8 +278,10 @@
                 at, slot = lower, gap - 1
             else:
                 at, slot = upper, count - gap - 1
+            place = jnp.bitwise_xor(own, at)
+            mine, theirs = same_ref[slot, place], other_ref[slot, place]
             return jnp.concatenate(
-                [coupled_ref[slot * pieces + p, at] for p in range(pieces)], axis=0
+                [jnp.where(even, mine, theirs), jnp.where(even, theirs, mine)], axis=0
             )
 
         for layer in range(count):
@@ -194,7 +296,6 @@
                 update = dot(grad_pre, lower)
                 for low in range(layer):
                     reach[low] += update[:, low * units : (low + 1) * units]
-        own = section_ref[0]
         far = count - 1 - own
         pre = pre_of(own, far)
         hidden = (pre * jax.nn.sigmoid(pre)).astype(BF16)
@@ -214,11 +315,14 @@
     return pl.pallas_call(
         kernel,
         out_shape=jax.ShapeDtypeStruct((count, units + rows, units), BF16),
-        in_specs=[smem(), vmem(), vmem()],
+        in_specs=[smem(), smem(), vmem(), vmem(), vmem()],
         out_specs=vmem(),
-        scratch_shapes=[pltpu.VMEM((count, rows, units), F32), pltpu.VMEM((count, rows, units), BF16)],
+        scratch_shapes=[
+            pltpu.VMEM((count, rows, units), F32),
+            pltpu.VMEM((count, rows, units), BF16),
+        ],
         name="chain",
-    )(section, known, coupled)
+    )(section, core, known, same, other)
 
 
 def input_grads(wide, shared, step):
@@ -308,32 +412,35 @@
     section = section_idx.astype(jnp.int32).reshape(1)
     _, micro, row_count, width = down_inputs.shape
     units = branch_in.shape[2]
-    part = width // blocks
     half = micro * row_count
     rows = 2 * half
     step = 4
 
+    core = (fsdp_idx % 2).astype(jnp.int32).reshape(1)
+    groups = same_core(blocks)
+
     in_t = branch_in[0].T
     out_t = branch_out[0]
-    near = [
-        from_above(jnp.where(section_idx >= up, in_t, out_t), up) for up in range(1, count // 2 + 1)
-    ]
+    down = down_inputs[0].reshape(half, width)
+    up = up_inputs[0].reshape(half, width)
+    out_full = lax.all_gather(out_t, "fsdp", axis=0)
+    wide = exchanged(laid_out(down, up, blocks, step), "fsdp")
+    near = []
+    for above in range(1, count // 2 + 1):
+        near.append(from_above(jnp.where(section_idx >= above, in_t, out_t), above))
     far_in_t = mirrored(in_t)
-    out_full = lax.all_gather(out_t, "fsdp", axis=0)
-
-    narrow = jnp.concatenate(
-        [down_inputs[0].reshape(half, width), up_inputs[0].reshape(half, width)], axis=0
-    )
-    wide = exchanged(jnp.transpose(narrow.reshape(rows, blocks, part), (1, 0, 2)), "fsdp")
-
-    coupled = couplings(section, in_t, out_t, near, count)
+
+    coupled, packed = couplings(section, in_t, out_t, near, count)
     coupled = exchanged(coupled.reshape(blocks, -1, units), "fsdp")
-    coupled = jnp.sum(coupled.astype(F32), axis=0).astype(BF16)
-    coupled = lax.all_gather(spread(coupled, "section"), "fsdp", axis=0)
+    coupled = folded(coupled, 1, coupled.shape[1])
+    for unit in (1, 4):
+        coupled = stacked(
+            [coupled] + [crossed(coupled, unit * times) for times in range(1, 4)]
+        )
+    coupled_same = lax.all_gather(coupled, "fsdp", axis=0, axis_index_groups=groups)
+    coupled_other = from_other_core(coupled_same)
     far_near = lax.ppermute(
-        jnp.stack(near[: count // 2 - 1]),
-        "section",
-        [(k + count // 2, k) for k in range(count // 2)],
+        packed, "section", [(k + count // 2, k) for k in range(count // 2)]
     )
 
     micro_ids = jnp.arange(micro, dtype=jnp.int32)
@@ -352,21 +459,19 @@
     head = reward_head.reshape(1, width)
 
     reached = top_products(top, row_weight, head, out_full, place, step)
-    pre = exchanged(pre_parts(wide, in_t, far_in_t, step), "fsdp")
-    pre = jnp.sum(pre.astype(F32), axis=0).astype(BF16)
-    known = spread(jnp.concatenate([pre, reached], axis=0), "section")
-
-    mirror_pre = lax.dynamic_index_in_dim(known, count - 1 - section_idx, 0, keepdims=False)
-    own_pre = jnp.concatenate([pre[:half], mirror_pre[half:rows]], axis=0)
-    firsts = exchanged(
-        first_parts(top, row_weight, head, own_pre, place, blocks, step), "fsdp"
-    )
-
-    shared = exchanged(chain(section, known, coupled), "fsdp")
+    parts = pre_parts(wide, in_t, far_in_t, step)
+    parts = exchanged(parts, "fsdp")
+    known, own_pre = folded_with(parts, reached, count)
+    mirror_pre = mirrored(own_pre[1])
+    known = exchanged(known, "section")
+    firsts = first_parts(top, row_weight, head, own_pre[0], mirror_pre, place, blocks, step)
+    firsts = exchanged(firsts, "fsdp")
+
+    shared = chain(section, core, known, coupled_same, coupled_other)
+    shared = exchanged(shared, "fsdp")
     own_in, far_in = input_grads(wide, shared, step)
     back_in = mirrored(far_in)
-    cross = jnp.sum(shared[:, :units].astype(F32), axis=0).astype(BF16)
-    cross = spread(cross, "fsdp")
+    cross = exchanged(folded(shared, blocks, units), "fsdp")
     grad_out = output_grads(cross, firsts, near, far_near)
     grad_in = (own_in + back_in.astype(F32)).T
     return (grad_in[None], grad_out[None])

time: 334 us -> 312 us (0.934)
  blocking collectives: 83.4 us -> 0 us
  starting transfers between devices: 64.7 us -> 111 us
  Pallas kernels: 34.1 us -> 48.2 us
  waiting for transfers between devices: 105 us -> 117 us
  local copies, waits for them, and re-layouts: 21.2 us -> 14.1 us
  other arithmetic: 6.94 us -> 3.42 us
    all_to_all x3 -> x0, blocking collectives: 83.4 us -> none  [exchanged(): return lax.all_to_all(parts, axis, 0, 0, tiled=True)]
    all_to_all x5 -> x7, waiting for transfers between devices: 80.3 us -> 55.3 us  [exchanged(): lax.all_to_all(parts, axis, 0, 0, axis_index_groups=groups, tiled=True)]
    all_to_all x5 -> x7, starting transfers between devices: 25 us -> 48.8 us  [exchanged(): lax.all_to_all(parts, axis, 0, 0, axis_index_groups=groups, tiled=True)]
    ppermute x1 -> x8, starting transfers between devices: 4.98 us -> 22.5 us  [the longest x6 16.1 us: crossed(): return lax.ppermute(value, 'section', [(k, k ^ mask) for k in range(count)])]
    ppermute x1 -> x8, waiting for transfers between devices: 0.01 us -> 17.5 us  [the longest x6 13 us: crossed(): return lax.ppermute(value, 'section', [(k, k ^ mask) for k in range(count)])]
    all_gather x1, waiting for transfers between devices: 0.01 us -> 17.1 us  [on_device(): lax.all_gather(coupled, 'fsdp', axis=0, axis_index_groups=groups)]
    pallas_call x1 -> x7, Pallas kernels: 3.72 us -> 17.7 us  [the longest x1 4.21 us: laid_out(): pl.pallas_call(kernel, grid=(blocks // step,), out_shape=jax.ShapeDtypeSt...]
    ppermute x2 -> x3, starting transfers between devices: 9.34 us -> 14.1 us  [mirrored(): lax.ppermute(value, 'section', [(k, count - 1 - k) for k in range(count)])]
  transfers between devices with their start and end apart: 18 -> 28, of which waited for: 10 -> 18; matrix products, arithmetic and copies ran while one was open for 7% -> 3% of each run, Pallas kernels for 7% -> 12%
where the time goes in v2:
time: 312 us; the launch traced here: 308 us
  waiting for transfers between devices  117 us (38%)
  starting transfers between devices  111 us (36%)
  Pallas kernels  48.2 us (15%)
  between operations  14.3 us (5%)
  local copies, waits for them, and re-layouts  14.1 us (5%)
  other arithmetic  3.42 us (1%)
    all_to_all x7, waiting for transfers between devices, exchanged(): lax.all_to_all(parts, axis, 0, 0, axis_index_groups=groups, tiled=True)  55.3 us
    all_to_all x7, starting transfers between devices, exchanged(): lax.all_to_all(parts, axis, 0, 0, axis_index_groups=groups, tiled=True)  48.8 us
    ppermute x8, starting transfers between devices, from_above(): lax.ppermute(value, 'section', [((k + steps) % count, k) for k in range(c...  25.4 us
    all_gather x1, waiting for transfers between devices, on_device(): lax.all_gather(coupled, 'fsdp', axis=0, axis_index_groups=groups)  17.1 us
    ppermute x3, waiting for transfers between devices, mirrored(): lax.ppermute(value, 'section', [(k, count - 1 - k) for k in range(count)])  16.5 us
    ppermute x6, starting transfers between devices, crossed(): return lax.ppermute(value, 'section', [(k, k ^ mask) for k in range(count)])  16.1 us
    ppermute x3, starting transfers between devices, mirrored(): lax.ppermute(value, 'section', [(k, count - 1 - k) for k in range(count)])  14.1 us
    ppermute x6, waiting for transfers between devices, crossed(): return lax.ppermute(value, 'section', [(k, k ^ mask) for k in range(count)])  13 us
  transfers between devices with their start and end apart: 28, of which 18 were waited for; matrix products, arithmetic and copies ran while one was open for 3% of the time, Pallas kernels for 12%

profile of v2, /device:TPU:16, one launch (start us, length us, event | category | flops | bytes accessed | tf_op | source)
XLA Modules:
  0.0 308.3 jit_solution(10845423632651063103)
XLA Ops:
  10.0 5.7 %collective-permute-start.1 = (bf16[128,512]{1,0:T(8,128)(2,1)S(1)}, bf16[128,512]{1,0:T(8,128)(2,1)S(1)}, u32[]{:S(2)}, u32[]{:S(2)}) collective-permute-start(bf16[128,512]{1,0:T(8,128)(2,1)S(1)} %get-tuple-element.23), channel_id=1, source_target_pairs={{16,0},{32,16},{48,32},{64,48},{80,64},{96,80},{112,96},{128,112},... | collective-permute-start | bytes 393224 | tf_op jit(solution)/shard_map/ppermute | solution.py:21
  17.6 7.7 %collective-permute-start.4 = (bf16[128,512]{1,0:T(8,128)(2,1)S(1)}, bf16[128,512]{1,0:T(8,128)(2,1)S(1)}, u32[]{:S(2)}, u32[]{:S(2)}) collective-permute-start(bf16[128,512]{1,0:T(8,128)(2,1)S(1)} %get-tuple-element.26), channel_id=1, source_target_pairs={{64,0},{80,16},{96,32},{112,48},{128,64},{144,80},{160,96},{176,11... | collective-permute-start | bytes 393224 | tf_op jit(solution)/shard_map/ppermute | solution.py:21
  27.5 4.5 %collective-permute-start.7 = (bf16[128,512]{1,0:T(8,128)(2,1)S(1)}, bf16[128,512]{1,0:T(8,128)(2,1)S(1)}, u32[]{:S(2)}, u32[]{:S(2)}) collective-permute-start(bf16[128,512]{1,0:T(8,128)(2,1)S(1)} %get-tuple-element.29), channel_id=1, source_target_pairs={{112,0},{128,16},{144,32},{160,48},{176,64},{192,80},{208,96},{224... | collective-permute-start | bytes 393224 | tf_op jit(solution)/shard_map/ppermute | solution.py:21
  32.1 6.1 %collective-permute-done.3.refs_2_ = bf16[128,512]{1,0:T(8,128)(2,1)S(1)} collective-permute-done((bf16[128,512]{1,0:T(8,128)(2,1)S(1)}, bf16[128,512]{1,0:T(8,128)(2,1)S(1)}, u32[]{:S(2)}, u32[]{:S(2)}) %collective-permute-start.3) | collective-permute-done | bytes 131104 | tf_op jit(solution)/shard_map/ppermute | solution.py:21
  50.4 6.0 %all-to-all-start.3 = ((bf16[16,64,128]{2,1,0:T(8,128)(2,1)}), bf16[16,64,128]{2,1,0:T(8,128)(2,1)S(1)}, u32[]{:S(2)}, u32[]{:S(2)}) async-start(bf16[16,64,128]{2,1,0:T(8,128)(2,1)} %bitcast.50), calls=%async_computation.3 | async-start | bytes 524288 | tf_op jit(solution)/shard_map/all_to_all | solution.py:30
  84.5 5.4 %collective-permute-start.12 = (bf16[4,64,128]{2,1,0:T(8,128)(2,1)}, bf16[4,64,128]{2,1,0:T(8,128)(2,1)S(1)}, u32[]{:S(2)}, u32[]{:S(2)}) collective-permute-start(bf16[4,64,128]{2,1,0:T(8,128)(2,1)} %stacked.2.refs_0_), channel_id=1, source_target_pairs={{0,64},{16,80},{32,96},{48,112},{64,0},{80,16},{96,32},{112,48},{1... | collective-permute-start | bytes 196616 | tf_op jit(solution)/shard_map/ppermute | solution.py:35
  93.4 7.1 %collective-permute-done.13.refs_2_ = bf16[4,64,128]{2,1,0:T(8,128)(2,1)S(1)} collective-permute-done((bf16[4,64,128]{2,1,0:T(8,128)(2,1)}, bf16[4,64,128]{2,1,0:T(8,128)(2,1)S(1)}, u32[]{:S(2)}, u32[]{:S(2)}) %collective-permute-start.13) | collective-permute-done | bytes 65568 | tf_op jit(solution)/shard_map/ppermute | solution.py:35
  103.6 7.6 %collective-permute-start = (bf16[128,512]{1,0:T(8,128)(2,1)S(1)}, bf16[128,512]{1,0:T(8,128)(2,1)S(1)}, u32[]{:S(2)}, u32[]{:S(2)}) collective-permute-start(bf16[128,512]{1,0:T(8,128)(2,1)S(1)} %bitcast.43), channel_id=1, source_target_pairs={{0,240},{16,224},{32,208},{48,192},{64,176},{80,160},{96,144},{112... | collective-permute-start | bytes 393224 | tf_op jit(solution)/shard_map/ppermute | solution.py:26
  119.3 4.7 %pre_parts.1 = bf16[16,192,128]{2,1,0:T(8,128)(2,1)} custom-call(bf16[16,192,512]{2,1,0:T(8,128)(2,1)} %copy-done.1, bf16[128,512]{1,0:T(8,128)(2,1)} %bitcast.42, bf16[128,512]{1,0:T(8,128)(2,1)} %copy-done.18), custom_call_target="tpu_custom_call" | custom-call | tf_op jit(solution)/shard_map/pre_parts/pallas_call | solution.py:178
  124.0 13.6 %all-to-all-start.1 = ((bf16[16,192,128]{2,1,0:T(8,128)(2,1)}), bf16[16,192,128]{2,1,0:T(8,128)(2,1)S(1)}, u32[]{:S(2)}, u32[]{:S(2)}) async-start(bf16[16,192,128]{2,1,0:T(8,128)(2,1)} %pre_parts.1), calls=%async_computation.1 | async-start | bytes 1572864 | tf_op jit(solution)/shard_map/all_to_all | solution.py:30
  138.5 4.9 %top_products.1.below_ref = bf16[192,128]{1,0:T(8,128)(2,1)} custom-call(bf16[192,8192]{1,0:T(8,128)(2,1)} %bitcast.39, f32[192,1]{1,0:T(8,128)} %select_n.107.weight_ref, f32[1,8192]{1,0:T(1,128)} %bitcast.51, bf16[16,128,512]{2,1,0:T(8,128)(2,1)} %all-gather.4.cloned.1.call-done.out_ref, bf16[192,192]{1,0:T(8,128)(2,1)} %fusion.place_ref), custom_call_target="tpu_custom_call" | custom-call | tf_op jit(solution)/shard_map/top_products/pallas_call | solution.py:213
  143.4 10.6 %all-to-all-done.1.parts_ref = bf16[16,192,128]{2,1,0:T(8,128)(2,1)S(1)} async-done(((bf16[16,192,128]{2,1,0:T(8,128)(2,1)}), bf16[16,192,128]{2,1,0:T(8,128)(2,1)S(1)}, u32[]{:S(2)}, u32[]{:S(2)}) %all-to-all-start.1) | async-done | bytes 786464 | tf_op jit(solution)/shard_map/all_to_all | solution.py:30
  157.5 11.5 %all-to-all-start.2 = ((bf16[16,384,128]{2,1,0:T(8,128)(2,1)}), bf16[16,384,128]{2,1,0:T(8,128)(2,1)S(1)}, u32[]{:S(2)}, u32[]{:S(2)}) async-start(bf16[16,384,128]{2,1,0:T(8,128)(2,1)} %get-tuple-element.8), calls=%async_computation.2 | async-start | bytes 3145728 | tf_op jit(solution)/shard_map/all_to_all | solution.py:30
  169.0 17.1 %all-gather.6.cloned.1.call-done = bf16[128,64,128]{2,1,0:T(8,128)(2,1)} async-done(((bf16[16,64,128]{2,1,0:T(8,128)(2,1)}), bf16[128,64,128]{2,1,0:T(8,128)(2,1)}) %all-gather.6.cloned.1.call-update) | async-done | bytes 2097168 | tf_op jit(solution)/shard_map/all_gather | solution.py:440
  190.5 15.3 %all-to-all-done.2.known_ref = bf16[16,384,128]{2,1,0:T(8,128)(2,1)S(1)} async-done(((bf16[16,384,128]{2,1,0:T(8,128)(2,1)}), bf16[16,384,128]{2,1,0:T(8,128)(2,1)S(1)}, u32[]{:S(2)}, u32[]{:S(2)}) %all-to-all-start.2) | async-done | bytes 1572896 | tf_op jit(solution)/shard_map/all_to_all | solution.py:30
  207.1 7.4 %chain.1 = bf16[16,320,128]{2,1,0:T(8,128)(2,1)} custom-call(s32[1]{0:T(128)} %bitcast.2.section_ref, s32[1]{0:T(128)} %bitcast.3.core_ref, bf16[16,384,128]{2,1,0:T(8,128)(2,1)} %copy-done.4, bf16[8,16,64,128]{3,2,1,0:T(8,128)(2,1)} %bitcast.45, bf16[8,16,64,128]{3,2,1,0:T(8,128)(2,1)} %collective-permute-done.15.other_ref), custom_call_target="tpu_custom_call" | custom-call | tf_op jit(solution)/shard_map/chain/pallas_call | solution.py:315
  214.5 4.8 %all-to-all-start.4 = ((bf16[16,320,128]{2,1,0:T(8,128)(2,1)}), bf16[16,320,128]{2,1,0:T(8,128)(2,1)S(1)}, u32[]{:S(2)}, u32[]{:S(2)}) async-start(bf16[16,320,128]{2,1,0:T(8,128)(2,1)} %chain.1), calls=%async_computation.4 | async-start | bytes 2621440 | tf_op jit(solution)/shard_map/all_to_all | solution.py:30
  228.0 5.0 %first_parts.1 = bf16[16,128,512]{2,1,0:T(8,128)(2,1)} custom-call(bf16[192,8192]{1,0:T(8,128)(2,1)} %bitcast.40, f32[192,1]{1,0:T(8,128)} %select_n.107.weight_ref, f32[1,8192]{1,0:T(1,128)} %bitcast.52, bf16[96,128]{1,0:T(8,128)(2,1)} %get-tuple-element.31.down_ref, bf16[96,128]{1,0:T(8,128)(2,1)} %copy-done.23, bf16[192,192]{1,0:T(8,128)(2,1)} %fusion.place_ref), custom_call_target="tpu_custom_call" | custom-call | tf_op jit(solution)/shard_map/first_parts/pallas_call | solution.py:244
  233.0 5.6 %all-to-all-done.4.shared_ref.parts_ref = bf16[16,320,128]{2,1,0:T(8,128)(2,1)S(1)} async-done(((bf16[16,320,128]{2,1,0:T(8,128)(2,1)}), bf16[16,320,128]{2,1,0:T(8,128)(2,1)S(1)}, u32[]{:S(2)}, u32[]{:S(2)}) %all-to-all-start.4) | async-done | bytes 1310752 | tf_op jit(solution)/shard_map/all_to_all | solution.py:30
  243.6 6.4 %collective-permute-start.18 = (bf16[7,128,512]{2,1,0:T(8,128)(2,1)}, bf16[7,128,512]{2,1,0:T(8,128)(2,1)}, u32[]{:S(2)}, u32[]{:S(2)}) collective-permute-start(bf16[7,128,512]{2,1,0:T(8,128)(2,1)} %get-tuple-element.13), channel_id=1, source_target_pairs={{128,0},{144,16},{160,32},{176,48},{192,64},{208,80},{224,96},{240... | collective-permute-start | bytes 2752520 | tf_op jit(solution)/shard_map/ppermute | solution.py:442
  252.2 19.0 %all-to-all-done.6.first_ref = bf16[16,128,512]{2,1,0:T(8,128)(2,1)S(1)} async-done(((bf16[16,128,512]{2,1,0:T(8,128)(2,1)}), bf16[16,128,512]{2,1,0:T(8,128)(2,1)S(1)}, u32[]{:S(2)}, u32[]{:S(2)}) %all-to-all-start.6) | async-done | bytes 2097184 | tf_op jit(solution)/shard_map/all_to_all | solution.py:30
  271.3 5.3 %all-to-all-start.5 = ((bf16[16,128,128]{2,1,0:T(8,128)(2,1)}), bf16[16,128,128]{2,1,0:T(8,128)(2,1)S(1)}, u32[]{:S(2)}, u32[]{:S(2)}) async-start(bf16[16,128,128]{2,1,0:T(8,128)(2,1)} %folded.3), calls=%async_computation.5 | async-start | bytes 1048576 | tf_op jit(solution)/shard_map/all_to_all | solution.py:30
  276.5 4.7 %input_grads.1 = (f32[128,512]{1,0:T(8,128)}, bf16[128,512]{1,0:T(8,128)(2,1)}) custom-call(bf16[16,192,512]{2,1,0:T(8,128)(2,1)} %copy-done.1, bf16[16,320,128]{2,1,0:T(8,128)(2,1)} %copy-done.2), custom_call_target="tpu_custom_call" | custom-call | tf_op jit(solution)/shard_map/input_grads/pallas_call | solution.py:353
  284.3 9.5 %collective-permute-done.16 = bf16[128,512]{1,0:T(8,128)(2,1)S(1)} collective-permute-done((bf16[128,512]{1,0:T(8,128)(2,1)}, bf16[128,512]{1,0:T(8,128)(2,1)S(1)}, u32[]{:S(2)}, u32[]{:S(2)}) %collective-permute-start.16) | collective-permute-done | bytes 131104 | tf_op jit(solution)/shard_map/ppermute | solution.py:26
  (124 shorter events, 98.5 us)
Async XLA Ops:
  7.2 131.3 %all-gather.4.cloned.1.call-start = ((), (), s32[]{:S(2)}) async-start(), calls=%async_computation.7 | async-start | bytes 2228224 | tf_op jit(solution)/shard_map/all_gather | solution.py:426
  10.0 15.3 %collective-permute-start.1 = (bf16[128,512]{1,0:T(8,128)(2,1)S(1)}, bf16[128,512]{1,0:T(8,128)(2,1)S(1)}, u32[]{:S(2)}, u32[]{:S(2)}) collective-permute-start(bf16[128,512]{1,0:T(8,128)(2,1)S(1)} %get-tuple-element.23), channel_id=1, source_target_pairs={{16,0},{32,16},{48,32},{64,48},{80,64},{96,80},{112,96},{128,112},... | collective-permute-start | bytes 393224 | tf_op jit(solution)/shard_map/ppermute | solution.py:21
  15.7 11.8 %collective-permute-start.2 = (bf16[128,512]{1,0:T(8,128)(2,1)S(1)}, bf16[128,512]{1,0:T(8,128)(2,1)S(1)}, u32[]{:S(2)}, u32[]{:S(2)}) collective-permute-start(bf16[128,512]{1,0:T(8,128)(2,1)S(1)} %get-tuple-element.24), channel_id=1, source_target_pairs={{32,0},{48,16},{64,32},{80,48},{96,64},{112,80},{128,96},{144,112}... | collective-permute-start | bytes 393224 | tf_op jit(solution)/shard_map/ppermute | solution.py:21
  17.2 21.0 %collective-permute-start.3 = (bf16[128,512]{1,0:T(8,128)(2,1)S(1)}, bf16[128,512]{1,0:T(8,128)(2,1)S(1)}, u32[]{:S(2)}, u32[]{:S(2)}) collective-permute-start(bf16[128,512]{1,0:T(8,128)(2,1)S(1)} %get-tuple-element.25), channel_id=1, source_target_pairs={{48,0},{64,16},{80,32},{96,48},{112,64},{128,80},{144,96},{160,112... | collective-permute-start | bytes 393224 | tf_op jit(solution)/shard_map/ppermute | solution.py:21
  17.6 23.9 %collective-permute-start.4 = (bf16[128,512]{1,0:T(8,128)(2,1)S(1)}, bf16[128,512]{1,0:T(8,128)(2,1)S(1)}, u32[]{:S(2)}, u32[]{:S(2)}) collective-permute-start(bf16[128,512]{1,0:T(8,128)(2,1)S(1)} %get-tuple-element.26), channel_id=1, source_target_pairs={{64,0},{80,16},{96,32},{112,48},{128,64},{144,80},{160,96},{176,11... | collective-permute-start | bytes 393224 | tf_op jit(solution)/shard_map/ppermute | solution.py:21
  25.3 16.2 %collective-permute-start.5 = (bf16[128,512]{1,0:T(8,128)(2,1)S(1)}, bf16[128,512]{1,0:T(8,128)(2,1)S(1)}, u32[]{:S(2)}, u32[]{:S(2)}) collective-permute-start(bf16[128,512]{1,0:T(8,128)(2,1)S(1)} %get-tuple-element.27), channel_id=1, source_target_pairs={{80,0},{96,16},{112,32},{128,48},{144,64},{160,80},{176,96},{192,1... | collective-permute-start | bytes 393224 | tf_op jit(solution)/shard_map/ppermute | solution.py:21
  25.3 17.4 %collective-permute-start.6 = (bf16[128,512]{1,0:T(8,128)(2,1)S(1)}, bf16[128,512]{1,0:T(8,128)(2,1)S(1)}, u32[]{:S(2)}, u32[]{:S(2)}) collective-permute-start(bf16[128,512]{1,0:T(8,128)(2,1)S(1)} %get-tuple-element.28), channel_id=1, source_target_pairs={{96,0},{112,16},{128,32},{144,48},{160,64},{176,80},{192,96},{208,... | collective-permute-start | bytes 393224 | tf_op jit(solution)/shard_map/ppermute | solution.py:21
  27.5 18.2 %collective-permute-start.7 = (bf16[128,512]{1,0:T(8,128)(2,1)S(1)}, bf16[128,512]{1,0:T(8,128)(2,1)S(1)}, u32[]{:S(2)}, u32[]{:S(2)}) collective-permute-start(bf16[128,512]{1,0:T(8,128)(2,1)S(1)} %get-tuple-element.29), channel_id=1, source_target_pairs={{112,0},{128,16},{144,32},{160,48},{176,64},{192,80},{208,96},{224... | collective-permute-start | bytes 393224 | tf_op jit(solution)/shard_map/ppermute | solution.py:21
  38.2 7.5 %collective-permute-start.8 = (bf16[128,512]{1,0:T(8,128)(2,1)S(1)}, bf16[128,512]{1,0:T(8,128)(2,1)S(1)}, u32[]{:S(2)}, u32[]{:S(2)}) collective-permute-start(bf16[128,512]{1,0:T(8,128)(2,1)S(1)} %get-tuple-element.22), channel_id=1, source_target_pairs={{128,0},{144,16},{160,32},{176,48},{192,64},{208,80},{224,96},{240... | collective-permute-start | bytes 393224 | tf_op jit(solution)/shard_map/ppermute | solution.py:21
  50.4 13.7 %all-to-all-start.3 = ((bf16[16,64,128]{2,1,0:T(8,128)(2,1)}), bf16[16,64,128]{2,1,0:T(8,128)(2,1)S(1)}, u32[]{:S(2)}, u32[]{:S(2)}) async-start(bf16[16,64,128]{2,1,0:T(8,128)(2,1)} %bitcast.50), calls=%async_computation.3 | async-start | bytes 524288 | tf_op jit(solution)/shard_map/all_to_all | solution.py:30
  64.8 52.3 %all-to-all-start = ((bf16[16,192,512]{2,1,0:T(8,128)(2,1)}), bf16[16,192,512]{2,1,0:T(8,128)(2,1)S(1)}, u32[]{:S(2)}, u32[]{:S(2)}) async-start(bf16[16,192,512]{2,1,0:T(8,128)(2,1)} %laid_out.1), calls=%async_computation | async-start | bytes 6291456 | tf_op jit(solution)/shard_map/all_to_all | solution.py:30
  68.5 117.5 %all-gather.6.cloned.1.call-start = ((), (), s32[]{:S(2)}) async-start(), calls=%async_computation.8 | async-start | bytes 2359296 | tf_op jit(solution)/shard_map/all_gather | solution.py:440
  84.5 8.9 %collective-permute-start.12 = (bf16[4,64,128]{2,1,0:T(8,128)(2,1)}, bf16[4,64,128]{2,1,0:T(8,128)(2,1)S(1)}, u32[]{:S(2)}, u32[]{:S(2)}) collective-permute-start(bf16[4,64,128]{2,1,0:T(8,128)(2,1)} %stacked.2.refs_0_), channel_id=1, source_target_pairs={{0,64},{16,80},{32,96},{48,112},{64,0},{80,16},{96,32},{112,48},{1... | collective-permute-start | bytes 196616 | tf_op jit(solution)/shard_map/ppermute | solution.py:35
  89.8 10.7 %collective-permute-start.13 = (bf16[4,64,128]{2,1,0:T(8,128)(2,1)}, bf16[4,64,128]{2,1,0:T(8,128)(2,1)S(1)}, u32[]{:S(2)}, u32[]{:S(2)}) collective-permute-start(bf16[4,64,128]{2,1,0:T(8,128)(2,1)} %stacked.2.refs_0_), channel_id=1, source_target_pairs={{0,128},{16,144},{32,160},{48,176},{64,192},{80,208},{96,224},{112... | collective-permute-start | bytes 196616 | tf_op jit(solution)/shard_map/ppermute | solution.py:35
  90.5 10.8 %collective-permute-start.14 = (bf16[4,64,128]{2,1,0:T(8,128)(2,1)}, bf16[4,64,128]{2,1,0:T(8,128)(2,1)S(1)}, u32[]{:S(2)}, u32[]{:S(2)}) collective-permute-start(bf16[4,64,128]{2,1,0:T(8,128)(2,1)} %stacked.2.refs_0_), channel_id=1, source_target_pairs={{0,192},{16,208},{32,224},{48,240},{64,128},{80,144},{96,160},{112... | collective-permute-start | bytes 196616 | tf_op jit(solution)/shard_map/ppermute | solution.py:35
  103.6 13.4 %collective-permute-start = (bf16[128,512]{1,0:T(8,128)(2,1)S(1)}, bf16[128,512]{1,0:T(8,128)(2,1)S(1)}, u32[]{:S(2)}, u32[]{:S(2)}) collective-permute-start(bf16[128,512]{1,0:T(8,128)(2,1)S(1)} %bitcast.43), channel_id=1, source_target_pairs={{0,240},{16,224},{32,208},{48,192},{64,176},{80,160},{96,144},{112... | collective-permute-start | bytes 393224 | tf_op jit(solution)/shard_map/ppermute | solution.py:26
  124.0 30.0 %all-to-all-start.1 = ((bf16[16,192,128]{2,1,0:T(8,128)(2,1)}), bf16[16,192,128]{2,1,0:T(8,128)(2,1)S(1)}, u32[]{:S(2)}, u32[]{:S(2)}) async-start(bf16[16,192,128]{2,1,0:T(8,128)(2,1)} %pre_parts.1), calls=%async_computation.1 | async-start | bytes 1572864 | tf_op jit(solution)/shard_map/all_to_all | solution.py:30
  157.5 48.4 %all-to-all-start.2 = ((bf16[16,384,128]{2,1,0:T(8,128)(2,1)}), bf16[16,384,128]{2,1,0:T(8,128)(2,1)S(1)}, u32[]{:S(2)}, u32[]{:S(2)}) async-start(bf16[16,384,128]{2,1,0:T(8,128)(2,1)} %get-tuple-element.8), calls=%async_computation.2 | async-start | bytes 3145728 | tf_op jit(solution)/shard_map/all_to_all | solution.py:30
  214.5 24.1 %all-to-all-start.4 = ((bf16[16,320,128]{2,1,0:T(8,128)(2,1)}), bf16[16,320,128]{2,1,0:T(8,128)(2,1)S(1)}, u32[]{:S(2)}, u32[]{:S(2)}) async-start(bf16[16,320,128]{2,1,0:T(8,128)(2,1)} %chain.1), calls=%async_computation.4 | async-start | bytes 2621440 | tf_op jit(solution)/shard_map/all_to_all | solution.py:30
  219.9 7.4 %collective-permute-start.17 = (bf16[96,128]{1,0:T(8,128)(2,1)S(1)}, bf16[96,128]{1,0:T(8,128)(2,1)S(1)}, u32[]{:S(2)}, u32[]{:S(2)}) collective-permute-start(bf16[96,128]{1,0:T(8,128)(2,1)S(1)} %get-tuple-element.30), channel_id=1, source_target_pairs={{0,240},{16,224},{32,208},{48,192},{64,176},{80,160},{96,144},{112... | collective-permute-start | bytes 73736 | tf_op jit(solution)/shard_map/ppermute | solution.py:26
  239.7 31.6 %all-to-all-start.6 = ((bf16[16,128,512]{2,1,0:T(8,128)(2,1)}), bf16[16,128,512]{2,1,0:T(8,128)(2,1)S(1)}, u32[]{:S(2)}, u32[]{:S(2)}) async-start(bf16[16,128,512]{2,1,0:T(8,128)(2,1)} %first_parts.1), calls=%async_computation.6 | async-start | bytes 4194304 | tf_op jit(solution)/shard_map/all_to_all | solution.py:30
  243.6 52.0 %collective-permute-start.18 = (bf16[7,128,512]{2,1,0:T(8,128)(2,1)}, bf16[7,128,512]{2,1,0:T(8,128)(2,1)}, u32[]{:S(2)}, u32[]{:S(2)}) collective-permute-start(bf16[7,128,512]{2,1,0:T(8,128)(2,1)} %get-tuple-element.13), channel_id=1, source_target_pairs={{128,0},{144,16},{160,32},{176,48},{192,64},{208,80},{224,96},{240... | collective-permute-start | bytes 2752520 | tf_op jit(solution)/shard_map/ppermute | solution.py:442
  271.3 25.6 %all-to-all-start.5 = ((bf16[16,128,128]{2,1,0:T(8,128)(2,1)}), bf16[16,128,128]{2,1,0:T(8,128)(2,1)S(1)}, u32[]{:S(2)}, u32[]{:S(2)}) async-start(bf16[16,128,128]{2,1,0:T(8,128)(2,1)} %folded.3), calls=%async_computation.5 | async-start | bytes 1048576 | tf_op jit(solution)/shard_map/all_to_all | solution.py:30
  281.3 12.5 %collective-permute-start.16 = (bf16[128,512]{1,0:T(8,128)(2,1)}, bf16[128,512]{1,0:T(8,128)(2,1)S(1)}, u32[]{:S(2)}, u32[]{:S(2)}) collective-permute-start(bf16[128,512]{1,0:T(8,128)(2,1)} %get-tuple-element.11), channel_id=1, source_target_pairs={{0,240},{16,224},{32,208},{48,192},{64,176},{80,160},{96,144},{112... | collective-permute-start | bytes 393224 | tf_op jit(solution)/shard_map/ppermute | solution.py:26
  (32 other events, 357.9 us)
Sparse Core Ops, SparseCore 0:
  9.8 39.1 all-gather.3
  103.7 82.2 all-gather.5

commit v3 on v2

v3 whole, which is shorter than its diff:
```python
import jax
import jax.numpy as jnp
from jax import lax
from jax.experimental import pallas as pl
from jax.experimental.pallas import tpu as pltpu
from jax.sharding import PartitionSpec as P


BF16 = jnp.bfloat16
F32 = jnp.float32
ROWS_OF_BOTH = (((0,), (0,)), ((), ()))
COLS_OF_BOTH = (((1,), (1,)), ((), ()))


def dot(left, right, dims=(((1,), (0,)), ((), ()))):
    return lax.dot_general(left, right, dims, preferred_element_type=F32)


def from_above(value, steps):
    count = lax.axis_size("section")
    return lax.ppermute(value, "section", [((k + steps) % count, k) for k in range(count)])


def mirrored(value):
    count = lax.axis_size("section")
    return lax.ppermute(value, "section", [(k, count - 1 - k) for k in range(count)])


def exchanged(parts, axis, groups=None):
    return lax.all_to_all(parts, axis, 0, 0, axis_index_groups=groups, tiled=True)


def same_core(count):
    return [list(range(core, count, 2)) for core in range(2)]


def from_other_core(value):
    count = lax.axis_size("fsdp")
    return lax.ppermute(value, "fsdp", [(f, f ^ 1) for f in range(count)])


def vmem():
    return pl.BlockSpec(memory_space=pltpu.VMEM)


def smem():
    return pl.BlockSpec(memory_space=pltpu.SMEM)


def couplings(section, in_t, out_t, near, count):
    units = in_t.shape[0]
    slots = len(near)

    def kernel(section_ref, in_ref, out_ref, *refs):
        dest = refs[slots]
        for slot in range(slots):
            wrapped = section_ref[0] + slot + 1 >= count

            @pl.when(wrapped)
            def _():
                dest[slot] = dot(in_ref[...], refs[slot][...], COLS_OF_BOTH).astype(BF16)

            @pl.when(jnp.logical_not(wrapped))
            def _():
                dest[slot] = dot(refs[slot][...], out_ref[...], COLS_OF_BOTH).astype(BF16)

    return pl.pallas_call(
        kernel,
        out_shape=jax.ShapeDtypeStruct((slots, units, units), BF16),
        in_specs=[smem()] + [vmem()] * (2 + slots),
        out_specs=vmem(),
        name="couplings",
    )(section, in_t, out_t, *near)


def laid_out(down, up, blocks, step):
    half, width = down.shape
    part = width // blocks

    def kernel(down_ref, up_ref, dest):
        for b in range(step):
            dest[b, :half] = down_ref[:, b * part : (b + 1) * part]
            dest[b, half:] = up_ref[:, b * part : (b + 1) * part]

    return pl.pallas_call(
        kernel,
        grid=(blocks // step,),
        out_shape=jax.ShapeDtypeStruct((blocks, 2 * half, part), BF16),
        in_specs=[pl.BlockSpec((half, step * part), lambda b: (0, b))] * 2,
        out_specs=pl.BlockSpec((step, 2 * half, part), lambda b: (b, 0, 0)),
        name="laid_out",
    )(down, up)


def folded(parts, copies, used):
    blocks, _, units = parts.shape

    def kernel(parts_ref, dest):
        total = parts_ref[0, :used].astype(F32)
        for b in range(1, blocks):
            total = total + parts_ref[b, :used].astype(F32)
        total = total.astype(BF16)
        for c in range(copies):
            dest[c] = total

    return pl.pallas_call(
        kernel,
        out_shape=jax.ShapeDtypeStruct((copies, used, units), BF16),
        in_specs=[vmem()],
        out_specs=vmem(),
        name="folded",
    )(parts)


def folded_with(parts, below, copies, lead):
    blocks, rows, units = parts.shape
    half = (rows - lead) // 2

    def kernel(parts_ref, below_ref, dest, own):
        total = parts_ref[0].astype(F32)
        for b in range(1, blocks):
            total = total + parts_ref[b].astype(F32)
        total = total.astype(BF16)
        own[0] = total[lead : lead + half]
        own[1] = total[lead + half :]
        for c in range(copies):
            dest[c, :rows] = total
            dest[c, rows:] = below_ref[...]

    return pl.pallas_call(
        kernel,
        out_shape=[
            jax.ShapeDtypeStruct((copies, rows + below.shape[0], units), BF16),
            jax.ShapeDtypeStruct((2, half, units), BF16),
        ],
        in_specs=[vmem(), vmem()],
        out_specs=[vmem(), vmem()],
        name="folded_with",
    )(parts, below)


def row_setup(fsdp, plan, reward_pos, reward_cot, row_count):
    directions, micro = plan.shape
    rows = directions * micro * row_count

    def kernel(fsdp_ref, plan_ref, pos_ref, cot_ref, weight, place):
        at = fsdp_ref[0]
        row = lax.broadcasted_iota(jnp.int32, (row_count, 128), 0)
        wide_row = lax.broadcasted_iota(jnp.int32, (row_count, rows), 0)
        wide_col = lax.broadcasted_iota(jnp.int32, (row_count, rows), 1)
        for d in range(directions):
            for j in range(micro):
                ident = plan_ref[d, j]
                base = (d * micro + j) * row_count
                spot = (d * micro + ident) * row_count
                value = jnp.where(row == pos_ref[d, ident, at], cot_ref[d, ident, at], 0.0)
                weight[base : base + row_count] = value
                place[base : base + row_count] = jnp.where(
                    wide_col == wide_row + spot, 1.0, 0.0
                )

    return pl.pallas_call(
        kernel,
        out_shape=[
            jax.ShapeDtypeStruct((rows, 128), F32),
            jax.ShapeDtypeStruct((rows, rows), F32),
        ],
        in_specs=[smem()] * 4,
        out_specs=[vmem(), vmem()],
        name="row_setup",
    )(fsdp, plan, reward_pos, reward_cot)


def pre_parts(wide, coupled, in_t, far_in_t, step):
    blocks, rows, part = wide.shape
    units = in_t.shape[0]
    lead = coupled.shape[1]
    half = rows // 2

    def kernel(wide_ref, coupled_ref, in_ref, far_ref, dest):
        for b in range(step):
            dest[b, :lead] = coupled_ref[b]
            dest[b, lead : lead + half] = dot(
                wide_ref[b, :half], in_ref[...], COLS_OF_BOTH
            ).astype(BF16)
            dest[b, lead + half :] = dot(
                wide_ref[b, half:], far_ref[...], COLS_OF_BOTH
            ).astype(BF16)

    return pl.pallas_call(
        kernel,
        grid=(blocks // step,),
        out_shape=jax.ShapeDtypeStruct((blocks, lead + rows, units), BF16),
        in_specs=[
            pl.BlockSpec((step, rows, part), lambda b: (b, 0, 0)),
            pl.BlockSpec((step, lead, units), lambda b: (b, 0, 0)),
            pl.BlockSpec((units, part), lambda b: (0, 0)),
            pl.BlockSpec((units, part), lambda b: (0, 0)),
        ],
        out_specs=pl.BlockSpec((step, lead + rows, units), lambda b: (b, 0, 0)),
        name="pre_parts",
    )(wide, coupled, in_t, far_in_t)


def top_products(top, row_weight, head, out_full, place, step):
    blocks, units, part = out_full.shape
    rows = top.shape[0]

    def kernel(top_ref, weight_ref, head_ref, out_ref, place_ref, dest, acc):
        at = pl.program_id(0)

        @pl.when(at == 0)
        def _():
            acc[...] = jnp.zeros_like(acc)

        first = top_ref[...].astype(F32) + weight_ref[:, :1] * head_ref[...]
        first = first.astype(BF16)
        total = acc[...]
        for b in range(step):
            total = total + dot(first[:, b * part : (b + 1) * part], out_ref[b], COLS_OF_BOTH)
        acc[...] = total

        @pl.when(at == pl.num_programs(0) - 1)
        def _():
            dest[...] = dot(
                place_ref[...].astype(BF16), acc[...].astype(BF16), ROWS_OF_BOTH
            ).astype(BF16)

    return pl.pallas_call(
        kernel,
        grid=(blocks // step,),
        out_shape=jax.ShapeDtypeStruct((rows, units), BF16),
        in_specs=[
            pl.BlockSpec((rows, step * part), lambda b: (0, b)),
            pl.BlockSpec((rows, 128), lambda b: (0, 0)),
            pl.BlockSpec((1, step * part), lambda b: (0, b)),
            pl.BlockSpec((step, units, part), lambda b: (b, 0, 0)),
            pl.BlockSpec((rows, rows), lambda b: (0, 0)),
        ],
        out_specs=pl.BlockSpec((rows, units), lambda b: (0, 0)),
        scratch_shapes=[pltpu.VMEM((rows, units), F32)],
        name="top_products",
    )(top, row_weight, head, out_full, place)


def first_parts(top, row_weight, head, pre_down, pre_up, place, blocks, step):
    rows, width = top.shape
    half, units = pre_down.shape
    part = width // blocks

    def kernel(top_ref, weight_ref, head_ref, down_ref, up_ref, place_ref, dest):
        value = jnp.concatenate([down_ref[...], up_ref[...]], axis=0).astype(F32)
        hidden = (value * jax.nn.sigmoid(value)).astype(BF16)
        placed = dot(place_ref[...].astype(BF16), hidden).astype(BF16)
        first = top_ref[...].astype(F32) + weight_ref[:, :1] * head_ref[...]
        first = first.astype(BF16)
        total = dot(placed, first, ROWS_OF_BOTH).astype(BF16)
        for b in range(step):
            dest[b] = total[:, b * part : (b + 1) * part]

    return pl.pallas_call(
        kernel,
        grid=(blocks // step,),
        out_shape=jax.ShapeDtypeStruct((blocks, units, part), BF16),
        in_specs=[
            pl.BlockSpec((rows, step * part), lambda b: (0, b)),
            pl.BlockSpec((rows, 128), lambda b: (0, 0)),
            pl.BlockSpec((1, step * part), lambda b: (0, b)),
            pl.BlockSpec((half, units), lambda b: (0, 0)),
            pl.BlockSpec((half, units), lambda b: (0, 0)),
            pl.BlockSpec((rows, rows), lambda b: (0, 0)),
        ],
        out_specs=pl.BlockSpec((step, units, part), lambda b: (b, 0, 0)),
        name="first_parts",
    )(top, row_weight, head, pre_down, pre_up, place)


def chain(section, core, known, same, other):
    count, tall, units = known.shape
    lead = same.shape[2]
    rows = (tall - lead) // 2
    half = rows // 2

    def kernel(section_ref, core_ref, known_ref, same_ref, other_ref, dest, reach, grads):
        even = core_ref[0] == 0
        own = section_ref[0]

        def pre_of(layer, other):
            return jnp.concatenate(
                [
                    known_ref[layer, lead : lead + half],
                    known_ref[other, lead + half : lead + rows],
                ],
                axis=0,
            ).astype(F32)

        def coupling(upper, lower):
            gap = upper - lower
            if gap <= count // 2:
                at, slot = lower, gap - 1
            else:
                at, slot = upper, count - gap - 1
            mine, theirs = same_ref[slot, at], other_ref[slot, at]
            return jnp.concatenate(
                [jnp.where(even, mine, theirs), jnp.where(even, theirs, mine)], axis=0
            )

        for layer in range(count):
            reach[layer] = known_ref[layer, lead + rows :].astype(F32)
        for layer in range(count - 1, -1, -1):
            pre = pre_of(layer, count - 1 - layer)
            sig = jax.nn.sigmoid(pre)
            grad_pre = (reach[layer] * sig * (1.0 + pre * (1.0 - sig))).astype(BF16)
            grads[layer] = grad_pre
            if layer > 0:
                lower = jnp.concatenate([coupling(layer, low) for low in range(layer)], axis=1)
                update = dot(grad_pre, lower)
                for low in range(layer):
                    reach[low] += update[:, low * units : (low + 1) * units]
        far = count - 1 - own
        pre = pre_of(own, far)
        hidden = (pre * jax.nn.sigmoid(pre)).astype(BF16)
        above = jnp.concatenate(
            [grads[jnp.minimum(own + up, count - 1)] for up in range(1, count)], axis=1
        )
        cross = dot(hidden, above, ROWS_OF_BOTH)
        sent = jnp.concatenate([grads[own][:half], grads[far][half:]], axis=0)
        for up in range(count):
            if up == 0:
                dest[up, :units] = jnp.zeros((units, units), BF16)
            else:
                block = cross[:, (up - 1) * units : up * units]
                dest[up, :units] = jnp.where(own + up < count, block, 0.0).astype(BF16)
            dest[up, units:] = sent

    return pl.pallas_call(
        kernel,
        out_shape=jax.ShapeDtypeStruct((count, units + rows, units), BF16),
        in_specs=[smem(), smem(), vmem(), vmem(), vmem()],
        out_specs=vmem(),
        scratch_shapes=[
            pltpu.VMEM((count, rows, units), F32),
            pltpu.VMEM((count, rows, units), BF16),
        ],
        name="chain",
    )(section, core, known, same, other)


def input_grads(wide, shared, step, side, kind):
    blocks, rows, part = wide.shape
    tall, units = shared.shape[1:]
    half = rows // 2
    skip = tall - rows + side * half

    def kernel(wide_ref, shared_ref, dest, acc):
        at = pl.program_id(0)

        @pl.when(at == 0)
        def _():
            acc[...] = jnp.zeros_like(acc)

        total = acc[...]
        for b in range(step):
            total = total + dot(shared_ref[b, skip : skip + half], wide_ref[b], ROWS_OF_BOTH)
        acc[...] = total

        @pl.when(at == pl.num_programs(0) - 1)
        def _():
            dest[...] = acc[...].astype(kind)

    return pl.pallas_call(
        kernel,
        grid=(blocks // step,),
        out_shape=jax.ShapeDtypeStruct((units, part), kind),
        in_specs=[
            pl.BlockSpec((step, half, part), lambda b: (b, side, 0)),
            pl.BlockSpec((step, tall, units), lambda b: (b, 0, 0)),
        ],
        out_specs=pl.BlockSpec((units, part), lambda b: (0, 0)),
        scratch_shapes=[pltpu.VMEM((units, part), F32)],
    )(wide, shared)


def output_grads(section, cross, first, near, far):
    count, units, _ = cross.shape
    part = first.shape[1]
    slots = len(near)
    upper = count // 2

    def kernel(section_ref, cross_ref, first_ref, far_ref, *refs):
        dest = refs[slots]
        own = section_ref[0]
        total = first_ref[...].astype(F32)
        for up in range(1, slots + 1):
            total = total + dot(cross_ref[up], refs[up - 1][...])
        dest[...] = total
        for at in range(1, count - upper):

            @pl.when(at > own)
            def _():
                dest[...] += dot(cross_ref[at + upper - own], far_ref[at])

    return pl.pallas_call(
        kernel,
        out_shape=jax.ShapeDtypeStruct((units, part), F32),
        in_specs=[smem()] + [vmem()] * (3 + slots),
        out_specs=vmem(),
        name="output_grads",
    )(section, cross, first, far, *near)


def on_device(
    branch_in,
    branch_out,
    down_inputs,
    up_inputs,
    top_grads,
    plan,
    reward_pos,
    reward_cot,
    reward_head,
):
    count = lax.axis_size("section")
    blocks = lax.axis_size("fsdp")
    section_idx = lax.axis_index("section")
    fsdp_idx = lax.axis_index("fsdp")
    section = section_idx.astype(jnp.int32).reshape(1)
    _, micro, row_count, width = down_inputs.shape
    units = branch_in.shape[2]
    part = width // blocks
    half = micro * row_count
    rows = 2 * half
    step = 4

    core = (fsdp_idx % 2).astype(jnp.int32).reshape(1)
    groups = same_core(blocks)

    in_t = branch_in[0].T
    out_t = branch_out[0]
    down = down_inputs[0].reshape(half, width)
    up = up_inputs[0].reshape(half, width)
    out_full = lax.all_gather(out_t, "fsdp", axis=0)
    wide = exchanged(laid_out(down, up, blocks, step), "fsdp")
    near = []
    for above in range(1, count // 2 + 1):
        near.append(from_above(jnp.where(section_idx >= above, in_t, out_t), above))
    far_in_t = mirrored(in_t)

    partner = lax.ppermute(
        in_t, "section", [(k + count // 2, k) for k in range(count // 2)]
    )
    far_all = lax.all_gather(
        partner,
        "section",
        axis=0,
        axis_index_groups=[list(range(count // 2)), list(range(count // 2, count))],
    )

    coupled = couplings(section, in_t, out_t, near, count).reshape(blocks, -1, units)
    lead = coupled.shape[1]
    row_weight, place = row_setup(
        fsdp_idx.astype(jnp.int32).reshape(1), plan, reward_pos, reward_cot, row_count
    )
    top = top_grads.reshape(rows, width)
    head = reward_head.reshape(1, width)
    parts = pre_parts(wide, coupled, in_t, far_in_t, step)
    parts = exchanged(parts, "fsdp")
    reached = top_products(top, row_weight, head, out_full, place, step)
    known, own_pre = folded_with(parts, reached, count, lead)
    mirror_pre = mirrored(own_pre[1])
    known = exchanged(known, "section")
    firsts = first_parts(top, row_weight, head, own_pre[0], mirror_pre, place, blocks, step)
    first = lax.psum_scatter(
        firsts.reshape(blocks * units, part), "fsdp", scatter_dimension=0, tiled=True
    )
    coupled = known[:, :lead]
    coupled_same = exchanged(
        jnp.broadcast_to(coupled[None], (blocks // 2,) + coupled.shape), "fsdp", groups
    )
    coupled_other = from_other_core(coupled_same)

    shared = chain(section, core, known, coupled_same, coupled_other)
    shared = exchanged(shared, "fsdp")
    far_in = input_grads(wide, shared, step, 1, BF16)
    back_in = mirrored(far_in)
    cross = exchanged(folded(shared, blocks, units), "fsdp")
    own_in = input_grads(wide, shared, step, 0, F32)
    grad_out = output_grads(section, cross, first, near, far_all)
    grad_in = (own_in + back_in.astype(F32)).T
    return (grad_in[None], grad_out[None])


def solution(mesh):
    in_specs = (
        P("section", "fsdp", None),
        P("section", None, "fsdp"),
        P("section", None, "fsdp", None),
        P("section", None, "fsdp", None),
        P(None, None, "fsdp", None),
        P(),
        P(),
        P(),
        P(),
    )
    out_specs = (P("section", "fsdp", None), P("section", None, "fsdp"))
    return jax.shard_map(
        on_device, mesh=mesh, in_specs=in_specs, out_specs=out_specs, check_vma=False
    )
```

time: 312 us -> 295 us (0.946)
  waiting for transfers between devices: 117 us -> 90.1 us
  blocking collectives: 0 us -> 25.3 us
  starting transfers between devices: 111 us -> 98.9 us
    all_to_all x0 -> x1, blocking collectives: none -> 25.3 us  [exchanged(): lax.all_to_all(parts, axis, 0, 0, axis_index_groups=groups, tiled=True)]
    ppermute x7 -> x1, starting transfers between devices: 22.5 us -> 2.01 us  [on_device(): lax.ppermute(in_t, 'section', [(k + count // 2, k) for k in range(count /...]
    all_gather x1, waiting for transfers between devices: 17.1 us -> 0.01 us  [on_device(): lax.all_gather(partner, 'section', axis=0, axis_index_groups=[list(range(...]
    all_to_all x7 -> x5, starting transfers between devices: 48.8 us -> 56.9 us  [exchanged(): lax.all_to_all(parts, axis, 0, 0, axis_index_groups=groups, tiled=True)]
    ppermute x8, waiting for transfers between devices: 10.3 us -> 4.65 us  [from_above(): lax.ppermute(value, 'section', [((k + steps) % count, k) for k in range(c...]
    ppermute x7 -> x1, waiting for transfers between devices: 13 us -> 7.53 us  [on_device(): lax.ppermute(in_t, 'section', [(k + count // 2, k) for k in range(count /...]
    all_to_all x7 -> x5, waiting for transfers between devices: 55.3 us -> 59.5 us  [exchanged(): lax.all_to_all(parts, axis, 0, 0, axis_index_groups=groups, tiled=True)]
    ppermute x3, starting transfers between devices: 14.1 us -> 17.9 us  [mirrored(): lax.ppermute(value, 'section', [(k, count - 1 - k) for k in range(count)])]
  transfers between devices with their start and end apart: 28 -> 21, of which waited for: 18 -> 9; matrix products, arithmetic and copies ran while one was open for 3% -> 2% of each run, Pallas kernels for 12% -> 15%
where the time goes in v3:
time: 295 us; the launch traced here: 291 us
  starting transfers between devices  98.9 us (34%)
  waiting for transfers between devices  90.1 us (31%)
  Pallas kernels  48 us (16%)
  blocking collectives  25.3 us (9%)
  between operations  15.7 us (5%)
  local copies, waits for them, and re-layouts  12.2 us (4%)
    all_to_all x5, waiting for transfers between devices, exchanged(): lax.all_to_all(parts, axis, 0, 0, axis_index_groups=groups, tiled=True)  59.5 us
    all_to_all x5, starting transfers between devices, exchanged(): lax.all_to_all(parts, axis, 0, 0, axis_index_groups=groups, tiled=True)  56.9 us
    all_to_all x1, blocking collectives, exchanged(): lax.all_to_all(parts, axis, 0, 0, axis_index_groups=groups, tiled=True)  25.3 us
    ppermute x8, starting transfers between devices, from_above(): lax.ppermute(value, 'section', [((k + steps) % count, k) for k in range(c...  22.1 us
    ppermute x3, starting transfers between devices, mirrored(): lax.ppermute(value, 'section', [(k, count - 1 - k) for k in range(count)])  17.9 us
    ppermute x3, waiting for transfers between devices, mirrored(): lax.ppermute(value, 'section', [(k, count - 1 - k) for k in range(count)])  13.2 us
    unnamed x40, local copies, waits for them, and re-layouts  9.58 us
    pallas_call x2, Pallas kernels, input_grads(): pl.pallas_call(kernel, grid=(blocks // step,), out_shape=jax.ShapeDtypeSt...  7.93 us
  transfers between devices with their start and end apart: 21, of which 9 were waited for; matrix products, arithmetic and copies ran while one was open for 2% of the time, Pallas kernels for 15%

profile of v3, /device:TPU:16, one launch (start us, length us, event | category | flops | bytes accessed | tf_op | source)
XLA Modules:
  0.0 291.2 jit_solution(8589254051761654029)
XLA Ops:
  8.7 4.2 %laid_out.1 = bf16[16,192,512]{2,1,0:T(8,128)(2,1)} custom-call(bf16[96,8192]{1,0:T(8,128)(2,1)} %bitcast.46, bf16[96,8192]{1,0:T(8,128)(2,1)} %bitcast.47), custom_call_target="tpu_custom_call" | custom-call | tf_op jit(solution)/shard_map/laid_out/pallas_call | solution.py:85
  12.9 5.3 %all-to-all-start = ((bf16[16,192,512]{2,1,0:T(8,128)(2,1)}), bf16[16,192,512]{2,1,0:T(8,128)(2,1)S(1)}, u32[]{:S(2)}, u32[]{:S(2)}) async-start(bf16[16,192,512]{2,1,0:T(8,128)(2,1)} %laid_out.1), calls=%async_computation | async-start | bytes 6291456 | tf_op jit(solution)/shard_map/all_to_all | solution.py:30
  18.4 6.0 %collective-permute-start = (bf16[128,512]{1,0:T(8,128)(2,1)S(1)}, bf16[128,512]{1,0:T(8,128)(2,1)S(1)}, u32[]{:S(2)}, u32[]{:S(2)}) collective-permute-start(bf16[128,512]{1,0:T(8,128)(2,1)S(1)} %get-tuple-element.15), channel_id=1, source_target_pairs={{16,0},{32,16},{48,32},{64,48},{80,64},{96,80},{112,96},{128,112},... | collective-permute-start | bytes 393224 | tf_op jit(solution)/shard_map/ppermute | solution.py:21
  26.3 7.4 %collective-permute-start.3 = (bf16[128,512]{1,0:T(8,128)(2,1)S(1)}, bf16[128,512]{1,0:T(8,128)(2,1)S(1)}, u32[]{:S(2)}, u32[]{:S(2)}) collective-permute-start(bf16[128,512]{1,0:T(8,128)(2,1)S(1)} %get-tuple-element.18), channel_id=1, source_target_pairs={{64,0},{80,16},{96,32},{112,48},{128,64},{144,80},{160,96},{176,11... | collective-permute-start | bytes 393224 | tf_op jit(solution)/shard_map/ppermute | solution.py:21
  36.3 4.3 %collective-permute-start.6 = (bf16[128,512]{1,0:T(8,128)(2,1)S(1)}, bf16[128,512]{1,0:T(8,128)(2,1)}, u32[]{:S(2)}, u32[]{:S(2)}) collective-permute-start(bf16[128,512]{1,0:T(8,128)(2,1)S(1)} %get-tuple-element.21), channel_id=1, source_target_pairs={{112,0},{128,16},{144,32},{160,48},{176,64},{192,80},{208,96},{224... | collective-permute-start | bytes 393224 | tf_op jit(solution)/shard_map/ppermute | solution.py:21
  40.5 4.6 %collective-permute-done.2.refs_2_ = bf16[128,512]{1,0:T(8,128)(2,1)S(1)} collective-permute-done((bf16[128,512]{1,0:T(8,128)(2,1)S(1)}, bf16[128,512]{1,0:T(8,128)(2,1)S(1)}, u32[]{:S(2)}, u32[]{:S(2)}) %collective-permute-start.2) | collective-permute-done | bytes 131104 | tf_op jit(solution)/shard_map/ppermute | solution.py:21
  46.5 12.7 %collective-permute-start.8 = (bf16[128,512]{1,0:T(8,128)(2,1)S(1)}, bf16[128,512]{1,0:T(8,128)(2,1)}, u32[]{:S(2)}, u32[]{:S(2)}) collective-permute-start(bf16[128,512]{1,0:T(8,128)(2,1)S(1)} %bitcast.42), channel_id=1, source_target_pairs={{0,240},{16,224},{32,208},{48,192},{64,176},{80,160},{96,144},{112... | collective-permute-start | bytes 393224 | tf_op jit(solution)/shard_map/ppermute | solution.py:26
  66.4 4.8 %pre_parts.1 = bf16[16,256,128]{2,1,0:T(8,128)(2,1)} custom-call(bf16[16,192,512]{2,1,0:T(8,128)(2,1)} %copy-done, bf16[16,64,128]{2,1,0:T(8,128)(2,1)} %bitcast.50, bf16[128,512]{1,0:T(8,128)(2,1)} %bitcast.44, bf16[128,512]{1,0:T(8,128)(2,1)} %collective-permute-done.8.far_ref), custom_call_target="tpu_custom_call" | custom-call | tf_op jit(solution)/shard_map/pre_parts/pallas_call | solution.py:190
  71.1 9.5 %all-to-all-start.1 = ((bf16[16,256,128]{2,1,0:T(8,128)(2,1)}), bf16[16,256,128]{2,1,0:T(8,128)(2,1)S(1)}, u32[]{:S(2)}, u32[]{:S(2)}) async-start(bf16[16,256,128]{2,1,0:T(8,128)(2,1)} %pre_parts.1), calls=%async_computation.1 | async-start | bytes 2097152 | tf_op jit(solution)/shard_map/all_to_all | solution.py:30
  83.8 4.9 %top_products.1.below_ref = bf16[192,128]{1,0:T(8,128)(2,1)} custom-call(bf16[192,8192]{1,0:T(8,128)(2,1)} %bitcast.39, f32[192,128]{1,0:T(8,128)} %get-tuple-element.6.weight_ref, f32[1,8192]{1,0:T(1,128)} %bitcast.52, bf16[16,128,512]{2,1,0:T(8,128)(2,1)} %all-gather.4.cloned.1.call-done.out_ref, f32[192,192]{1,0:T(8,128)} %get-tuple-element.7.place_ref), custom_call_target="tpu_custom_call" | custom-call | tf_op jit(solution)/shard_map/top_products/pallas_call | solution.py:229
  88.8 8.3 %all-to-all-done.1.parts_ref = bf16[16,256,128]{2,1,0:T(8,128)(2,1)S(1)} async-done(((bf16[16,256,128]{2,1,0:T(8,128)(2,1)}), bf16[16,256,128]{2,1,0:T(8,128)(2,1)S(1)}, u32[]{:S(2)}, u32[]{:S(2)}) %all-to-all-start.1) | async-done | bytes 1048608 | tf_op jit(solution)/shard_map/all_to_all | solution.py:30
  100.9 32.6 %all-to-all-start.2 = ((bf16[16,448,128]{2,1,0:T(8,128)(2,1)}), bf16[16,448,128]{2,1,0:T(8,128)(2,1)S(1)}, u32[]{:S(2)}, u32[]{:S(2)}) async-start(bf16[16,448,128]{2,1,0:T(8,128)(2,1)} %get-tuple-element.8), calls=%async_computation.2 | async-start | bytes 3670016 | tf_op jit(solution)/shard_map/all_to_all | solution.py:30
  135.5 7.5 %collective-permute-done.12 = bf16[128,512]{1,0:T(8,128)(2,1)S(1)} collective-permute-done((bf16[128,512]{1,0:T(8,128)(2,1)S(1)}, bf16[128,512]{1,0:T(8,128)(2,1)S(1)}, u32[]{:S(2)}, u32[]{:S(2)}) %collective-permute-start.12) | collective-permute-done | bytes 131104 | tf_op jit(solution)/shard_map/ppermute | solution.py:449
  143.7 38.9 %all-to-all-done.2.known_ref = bf16[16,448,128]{2,1,0:T(8,128)(2,1)S(1)} async-done(((bf16[16,448,128]{2,1,0:T(8,128)(2,1)}), bf16[16,448,128]{2,1,0:T(8,128)(2,1)S(1)}, u32[]{:S(2)}, u32[]{:S(2)}) %all-to-all-start.2) | async-done | bytes 1835040 | tf_op jit(solution)/shard_map/all_to_all | solution.py:30
  184.6 4.5 %all-to-all-start.3 = ((bf16[8,16,64,128]{3,2,1,0:T(8,128)(2,1)}), bf16[8,16,64,128]{3,2,1,0:T(8,128)(2,1)}, u32[]{:S(2)}, u32[]{:S(2)}) async-start(bf16[8,16,64,128]{3,2,1,0:T(8,128)(2,1)} %broadcast_in_dim.12), calls=%async_computation.3 | async-start | bytes 4194304 | tf_op jit(solution)/shard_map/all_to_all | solution.py:30
  191.1 6.7 %collective-permute-done.11.up_ref = bf16[96,128]{1,0:T(8,128)(2,1)S(1)} collective-permute-done((bf16[96,128]{1,0:T(8,128)(2,1)S(1)}, bf16[96,128]{1,0:T(8,128)(2,1)S(1)}, u32[]{:S(2)}, u32[]{:S(2)}) %collective-permute-start.11) | collective-permute-done | bytes 24608 | tf_op jit(solution)/shard_map/ppermute | solution.py:26
  198.4 5.2 %first_parts.1 = bf16[16,128,512]{2,1,0:T(8,128)(2,1)} custom-call(bf16[192,8192]{1,0:T(8,128)(2,1)} %bitcast.40, f32[192,128]{1,0:T(8,128)} %get-tuple-element.6.weight_ref, f32[1,8192]{1,0:T(1,128)} %bitcast.53, bf16[96,128]{1,0:T(8,128)(2,1)} %get-tuple-element.23.down_ref, bf16[96,128]{1,0:T(8,128)(2,1)} %copy-done.15, f32[192,192]{1,0:T(8,128)} %get-tuple-element.7.place_ref), custom_call_target="tpu_custom_call" | custom-call | tf_op jit(solution)/shard_map/first_parts/pallas_call | solution.py:261
  203.6 12.3 %all-to-all-done.3.same_ref = bf16[8,16,64,128]{3,2,1,0:T(8,128)(2,1)} async-done(((bf16[8,16,64,128]{3,2,1,0:T(8,128)(2,1)}), bf16[8,16,64,128]{3,2,1,0:T(8,128)(2,1)}, u32[]{:S(2)}, u32[]{:S(2)}) %all-to-all-start.3) | async-done | bytes 2097184 | tf_op jit(solution)/shard_map/all_to_all | solution.py:30
  215.9 4.5 %collective-permute-done.9.other_ref = bf16[8,16,64,128]{3,2,1,0:T(8,128)(2,1)S(1)} collective-permute-done((bf16[8,16,64,128]{3,2,1,0:T(8,128)(2,1)}, bf16[8,16,64,128]{3,2,1,0:T(8,128)(2,1)S(1)}, u32[]{:S(2)}, u32[]{:S(2)}) %collective-permute-start.9) | collective-permute-done | bytes 2097184 | tf_op jit(solution)/shard_map/ppermute | solution.py:39
  221.7 7.6 %chain.1 = bf16[16,320,128]{2,1,0:T(8,128)(2,1)} custom-call(s32[1]{0:T(128)} %bitcast.2.section_ref, s32[1]{0:T(128)} %bitcast.3.core_ref, bf16[16,448,128]{2,1,0:T(8,128)(2,1)} %copy-done.1, bf16[8,16,64,128]{3,2,1,0:T(8,128)(2,1)} %all-to-all-done.3.same_ref, bf16[8,16,64,128]{3,2,1,0:T(8,128)(2,1)} %copy-done.6), custom_call_target="tpu_custom_call" | custom-call | tf_op jit(solution)/shard_map/chain/pallas_call | solution.py:336
  229.3 25.3 %all_to_all.30.shared_ref.parts_ref = bf16[16,320,128]{2,1,0:T(8,128)(2,1)} all-to-all(bf16[16,320,128]{2,1,0:T(8,128)(2,1)} %chain.1), channel_id=1, replica_groups=mesh['section'=16,'fsdp'=16] {'fsdp'}, dimensions={0} | all-to-all | bytes 2621440 | tf_op jit(solution)/shard_map/all_to_all | solution.py:30
  256.8 5.0 %all-to-all-start.5 = ((bf16[16,128,128]{2,1,0:T(8,128)(2,1)}), bf16[16,128,128]{2,1,0:T(8,128)(2,1)S(1)}, u32[]{:S(2)}, u32[]{:S(2)}) async-start(bf16[16,128,128]{2,1,0:T(8,128)(2,1)} %folded.1), calls=%async_computation.5 | async-start | bytes 1048576 | tf_op jit(solution)/shard_map/all_to_all | solution.py:30
  269.6 4.0 %shard_map.104 = f32[128,512]{1,0:T(8,128)} custom-call(bf16[16,192,512]{2,1,0:T(8,128)(2,1)} %copy-done, bf16[16,320,128]{2,1,0:T(8,128)(2,1)} %all_to_all.30.shared_ref.parts_ref), custom_call_target="tpu_custom_call" | custom-call | tf_op jit(solution)/shard_map/pallas_call | solution.py:371
  273.6 4.6 %collective-permute-done.10 = bf16[128,512]{1,0:T(8,128)(2,1)S(1)} collective-permute-done((bf16[128,512]{1,0:T(8,128)(2,1)}, bf16[128,512]{1,0:T(8,128)(2,1)S(1)}, u32[]{:S(2)}, u32[]{:S(2)}) %collective-permute-start.10) | collective-permute-done | bytes 131104 | tf_op jit(solution)/shard_map/ppermute | solution.py:26
  (79 shorter events, 45.1 us)
Async XLA Ops:
  8.0 75.8 %all-gather.4.cloned.1.call-start = ((), (), s32[]{:S(2)}) async-start(), calls=%async_computation.7 | async-start | bytes 2228224 | tf_op jit(solution)/shard_map/all_gather | solution.py:442
  12.9 51.8 %all-to-all-start = ((bf16[16,192,512]{2,1,0:T(8,128)(2,1)}), bf16[16,192,512]{2,1,0:T(8,128)(2,1)S(1)}, u32[]{:S(2)}, u32[]{:S(2)}) async-start(bf16[16,192,512]{2,1,0:T(8,128)(2,1)} %laid_out.1), calls=%async_computation | async-start | bytes 6291456 | tf_op jit(solution)/shard_map/all_to_all | solution.py:30
  18.3 40.8 %copy-start.3 = (bf16[1,512,128]{1,2,0:T(8,128)(2,1)}, bf16[1,512,128]{1,2,0:T(8,128)(2,1)S(1)}, u32[]{:S(2)}) copy-start(bf16[1,512,128]{1,2,0:T(8,128)(2,1)S(1)} %copy.15) | copy-start | bytes 393220
  18.4 15.3 %collective-permute-start = (bf16[128,512]{1,0:T(8,128)(2,1)S(1)}, bf16[128,512]{1,0:T(8,128)(2,1)S(1)}, u32[]{:S(2)}, u32[]{:S(2)}) collective-permute-start(bf16[128,512]{1,0:T(8,128)(2,1)S(1)} %get-tuple-element.15), channel_id=1, source_target_pairs={{16,0},{32,16},{48,32},{64,48},{80,64},{96,80},{112,96},{128,112},... | collective-permute-start | bytes 393224 | tf_op jit(solution)/shard_map/ppermute | solution.py:21
  24.4 11.8 %collective-permute-start.1 = (bf16[128,512]{1,0:T(8,128)(2,1)S(1)}, bf16[128,512]{1,0:T(8,128)(2,1)S(1)}, u32[]{:S(2)}, u32[]{:S(2)}) collective-permute-start(bf16[128,512]{1,0:T(8,128)(2,1)S(1)} %get-tuple-element.16), channel_id=1, source_target_pairs={{32,0},{48,16},{64,32},{80,48},{96,64},{112,80},{128,96},{144,112}... | collective-permute-start | bytes 393224 | tf_op jit(solution)/shard_map/ppermute | solution.py:21
  25.9 19.3 %collective-permute-start.2 = (bf16[128,512]{1,0:T(8,128)(2,1)S(1)}, bf16[128,512]{1,0:T(8,128)(2,1)S(1)}, u32[]{:S(2)}, u32[]{:S(2)}) collective-permute-start(bf16[128,512]{1,0:T(8,128)(2,1)S(1)} %get-tuple-element.17), channel_id=1, source_target_pairs={{48,0},{64,16},{80,32},{96,48},{112,64},{128,80},{144,96},{160,112... | collective-permute-start | bytes 393224 | tf_op jit(solution)/shard_map/ppermute | solution.py:21
  26.3 18.8 %collective-permute-start.3 = (bf16[128,512]{1,0:T(8,128)(2,1)S(1)}, bf16[128,512]{1,0:T(8,128)(2,1)S(1)}, u32[]{:S(2)}, u32[]{:S(2)}) collective-permute-start(bf16[128,512]{1,0:T(8,128)(2,1)S(1)} %get-tuple-element.18), channel_id=1, source_target_pairs={{64,0},{80,16},{96,32},{112,48},{128,64},{144,80},{160,96},{176,11... | collective-permute-start | bytes 393224 | tf_op jit(solution)/shard_map/ppermute | solution.py:21
  33.7 25.4 %collective-permute-start.4 = (bf16[128,512]{1,0:T(8,128)(2,1)S(1)}, bf16[128,512]{1,0:T(8,128)(2,1)}, u32[]{:S(2)}, u32[]{:S(2)}) collective-permute-start(bf16[128,512]{1,0:T(8,128)(2,1)S(1)} %get-tuple-element.19), channel_id=1, source_target_pairs={{80,0},{96,16},{112,32},{128,48},{144,64},{160,80},{176,96},{192,1... | collective-permute-start | bytes 393224 | tf_op jit(solution)/shard_map/ppermute | solution.py:21
  33.7 25.4 %copy-start.8 = (bf16[128,512]{1,0:T(8,128)(2,1)}, bf16[128,512]{1,0:T(8,128)(2,1)S(1)}, u32[]{:S(2)}) copy-start(bf16[128,512]{1,0:T(8,128)(2,1)S(1)} %collective-permute-done.refs_0_) | copy-start | bytes 393220
  33.7 25.4 %collective-permute-start.5 = (bf16[128,512]{1,0:T(8,128)(2,1)S(1)}, bf16[128,512]{1,0:T(8,128)(2,1)}, u32[]{:S(2)}, u32[]{:S(2)}) collective-permute-start(bf16[128,512]{1,0:T(8,128)(2,1)S(1)} %get-tuple-element.20), channel_id=1, source_target_pairs={{96,0},{112,16},{128,32},{144,48},{160,64},{176,80},{192,96},{208,... | collective-permute-start | bytes 393224 | tf_op jit(solution)/shard_map/ppermute | solution.py:21
  36.3 22.9 %collective-permute-start.6 = (bf16[128,512]{1,0:T(8,128)(2,1)S(1)}, bf16[128,512]{1,0:T(8,128)(2,1)}, u32[]{:S(2)}, u32[]{:S(2)}) collective-permute-start(bf16[128,512]{1,0:T(8,128)(2,1)S(1)} %get-tuple-element.21), channel_id=1, source_target_pairs={{112,0},{128,16},{144,32},{160,48},{176,64},{192,80},{208,96},{224... | collective-permute-start | bytes 393224 | tf_op jit(solution)/shard_map/ppermute | solution.py:21
  45.1 14.0 %collective-permute-start.7 = (bf16[128,512]{1,0:T(8,128)(2,1)S(1)}, bf16[128,512]{1,0:T(8,128)(2,1)}, u32[]{:S(2)}, u32[]{:S(2)}) collective-permute-start(bf16[128,512]{1,0:T(8,128)(2,1)S(1)} %get-tuple-element.14), channel_id=1, source_target_pairs={{128,0},{144,16},{160,32},{176,48},{192,64},{208,80},{224,96},{240... | collective-permute-start | bytes 393224 | tf_op jit(solution)/shard_map/ppermute | solution.py:21
  46.5 18.3 %collective-permute-start.8 = (bf16[128,512]{1,0:T(8,128)(2,1)S(1)}, bf16[128,512]{1,0:T(8,128)(2,1)}, u32[]{:S(2)}, u32[]{:S(2)}) collective-permute-start(bf16[128,512]{1,0:T(8,128)(2,1)S(1)} %bitcast.42), channel_id=1, source_target_pairs={{0,240},{16,224},{32,208},{48,192},{64,176},{80,160},{96,144},{112... | collective-permute-start | bytes 393224 | tf_op jit(solution)/shard_map/ppermute | solution.py:26
  71.1 26.0 %all-to-all-start.1 = ((bf16[16,256,128]{2,1,0:T(8,128)(2,1)}), bf16[16,256,128]{2,1,0:T(8,128)(2,1)S(1)}, u32[]{:S(2)}, u32[]{:S(2)}) async-start(bf16[16,256,128]{2,1,0:T(8,128)(2,1)} %pre_parts.1), calls=%async_computation.1 | async-start | bytes 2097152 | tf_op jit(solution)/shard_map/all_to_all | solution.py:30
  100.9 32.6 %copy-start.4 = (bf16[1,512,128]{1,2,0:T(8,128)(2,1)S(1)}, bf16[1,512,128]{1,2,0:T(8,128)(2,1)}, u32[]{:S(2)}) copy-start(bf16[1,512,128]{1,2,0:T(8,128)(2,1)} %copy-done.3) | copy-start | bytes 393220
  100.9 81.8 %all-to-all-start.2 = ((bf16[16,448,128]{2,1,0:T(8,128)(2,1)}), bf16[16,448,128]{2,1,0:T(8,128)(2,1)S(1)}, u32[]{:S(2)}, u32[]{:S(2)}) async-start(bf16[16,448,128]{2,1,0:T(8,128)(2,1)} %get-tuple-element.8), calls=%async_computation.2 | async-start | bytes 3670016 | tf_op jit(solution)/shard_map/all_to_all | solution.py:30
  133.5 146.6 %all-gather.6.cloned.1.call-start = ((), (), s32[]{:S(2)}) async-start(), calls=%async_computation.9 | async-start | bytes 1179648 | tf_op jit(solution)/shard_map/all_gather | solution.py:452
  133.5 9.5 %collective-permute-start.12 = (bf16[128,512]{1,0:T(8,128)(2,1)S(1)}, bf16[128,512]{1,0:T(8,128)(2,1)S(1)}, u32[]{:S(2)}, u32[]{:S(2)}) collective-permute-start(bf16[128,512]{1,0:T(8,128)(2,1)S(1)} %bitcast.45), channel_id=1, source_target_pairs={{128,0},{144,16},{160,32},{176,48},{192,64},{208,80},{224,96},{240... | collective-permute-start | bytes 393224 | tf_op jit(solution)/shard_map/ppermute | solution.py:449
  184.6 31.3 %all-to-all-start.3 = ((bf16[8,16,64,128]{3,2,1,0:T(8,128)(2,1)}), bf16[8,16,64,128]{3,2,1,0:T(8,128)(2,1)}, u32[]{:S(2)}, u32[]{:S(2)}) async-start(bf16[8,16,64,128]{3,2,1,0:T(8,128)(2,1)} %broadcast_in_dim.12), calls=%async_computation.3 | async-start | bytes 4194304 | tf_op jit(solution)/shard_map/all_to_all | solution.py:30
  189.1 90.9 %reduce-scatter.2.cloned.1.call-start = ((), (), s32[]{:S(2)}) async-start(), calls=%async_computation.8 | async-start | bytes 2228224 | tf_op jit(solution)/shard_map/reduce_scatter | solution.py:473
  189.8 8.0 %collective-permute-start.11 = (bf16[96,128]{1,0:T(8,128)(2,1)S(1)}, bf16[96,128]{1,0:T(8,128)(2,1)S(1)}, u32[]{:S(2)}, u32[]{:S(2)}) collective-permute-start(bf16[96,128]{1,0:T(8,128)(2,1)S(1)} %get-tuple-element.22), channel_id=1, source_target_pairs={{0,240},{16,224},{32,208},{48,192},{64,176},{80,160},{96,144},{112... | collective-permute-start | bytes 73736 | tf_op jit(solution)/shard_map/ppermute | solution.py:26
  215.9 4.5 %collective-permute-start.9 = (bf16[8,16,64,128]{3,2,1,0:T(8,128)(2,1)}, bf16[8,16,64,128]{3,2,1,0:T(8,128)(2,1)S(1)}, u32[]{:S(2)}, u32[]{:S(2)}) collective-permute-start(bf16[8,16,64,128]{3,2,1,0:T(8,128)(2,1)} %all-to-all-done.3.same_ref), channel_id=1, source_target_pairs={{0,1},{1,0},{2,3},{3,2},{4,5},{5,4},{6,7},{7,6},{8,9},{9,8},{10,11... | collective-permute-start | bytes 6291464 | tf_op jit(solution)/shard_map/ppermute | solution.py:39
  256.8 23.2 %all-to-all-start.5 = ((bf16[16,128,128]{2,1,0:T(8,128)(2,1)}), bf16[16,128,128]{2,1,0:T(8,128)(2,1)S(1)}, u32[]{:S(2)}, u32[]{:S(2)}) async-start(bf16[16,128,128]{2,1,0:T(8,128)(2,1)} %folded.1), calls=%async_computation.5 | async-start | bytes 1048576 | tf_op jit(solution)/shard_map/all_to_all | solution.py:30
  265.7 12.4 %collective-permute-start.10 = (bf16[128,512]{1,0:T(8,128)(2,1)}, bf16[128,512]{1,0:T(8,128)(2,1)S(1)}, u32[]{:S(2)}, u32[]{:S(2)}) collective-permute-start(bf16[128,512]{1,0:T(8,128)(2,1)} %shard_map.105), channel_id=1, source_target_pairs={{0,240},{16,224},{32,208},{48,192},{64,176},{80,160},{96,144},{112... | collective-permute-start | bytes 393224 | tf_op jit(solution)/shard_map/ppermute | solution.py:26
  (15 other events, 67.2 us)
Sparse Core Ops, SparseCore 0:
  10.7 71.1 all-gather.3
  203.7 75.5 reduce-scatter.1
Sparse Core Ops, SparseCore 1:
  143.8 47.6 all-gather.5

commit v4 on v3

--- a/solution.py
+++ b/solution.py
@@ -16,9 +16,25 @@
     return lax.dot_general(left, right, dims, preferred_element_type=F32)
 
 
-def from_above(value, steps):
-    count = lax.axis_size("section")
-    return lax.ppermute(value, "section", [((k + steps) % count, k) for k in range(count)])
+LOWER_OFFSETS = (0, -3, -1, 4)
+UPPER_OFFSETS = (1, 2, 3, -2)
+
+
+def inside_half(value, steps, ends):
+    ring = lax.axis_size("section") // 2
+    pairs = []
+    for base in (0, ring):
+        pairs += [(base + (z + steps) % ring, base + z) for z in range(ends)]
+    return lax.ppermute(value, "section", pairs)
+
+
+def across(value, slot):
+    ring = lax.axis_size("section") // 2
+    low, high = LOWER_OFFSETS[slot], UPPER_OFFSETS[slot]
+    pairs = [(ring + (z - high) % ring, ring + z) for z in range(ring)]
+    if low:
+        pairs += [((z + low) % ring, z) for z in range(ring)]
+    return lax.ppermute(value, "section", pairs)
 
 
 def mirrored(value):
@@ -47,30 +63,49 @@
     return pl.BlockSpec(memory_space=pltpu.SMEM)
 
 
-def couplings(section, in_t, out_t, near, count):
+def couplings(section, in_t, out_t, partner, inner, outer, count):
     units = in_t.shape[0]
-    slots = len(near)
-
-    def kernel(section_ref, in_ref, out_ref, *refs):
-        dest = refs[slots]
+    ring = count // 2
+    slots = len(inner)
+
+    def kernel(section_ref, in_ref, out_ref, partner_ref, *refs):
+        dest = refs[2 * slots]
+        own = section_ref[0]
+        upper = own >= ring
+
+        def store(slot, other, as_lower):
+            @pl.when(as_lower)
+            def _():
+                dest[slot] = dot(other[...], out_ref[...], COLS_OF_BOTH).astype(BF16)
+
+            @pl.when(jnp.logical_not(as_lower))
+            def _():
+                dest[slot] = dot(in_ref[...], other[...], COLS_OF_BOTH).astype(BF16)
+
         for slot in range(slots):
-            wrapped = section_ref[0] + slot + 1 >= count
-
-            @pl.when(wrapped)
-            def _():
-                dest[slot] = dot(in_ref[...], refs[slot][...], COLS_OF_BOTH).astype(BF16)
-
-            @pl.when(jnp.logical_not(wrapped))
-            def _():
-                dest[slot] = dot(refs[slot][...], out_ref[...], COLS_OF_BOTH).astype(BF16)
-
-    return pl.pallas_call(
-        kernel,
-        out_shape=jax.ShapeDtypeStruct((slots, units, units), BF16),
-        in_specs=[smem()] + [vmem()] * (2 + slots),
+            store(slot, refs[slot], jnp.where(upper, own - ring, own) + slot + 1 < ring)
+        for slot in range(slots):
+            other = refs[slots + slot]
+            if LOWER_OFFSETS[slot] == 0:
+
+                @pl.when(upper)
+                def _():
+                    dest[slots + slot] = dot(in_ref[...], other[...], COLS_OF_BOTH).astype(BF16)
+
+                @pl.when(jnp.logical_not(upper))
+                def _():
+                    value = dot(partner_ref[...], out_ref[...], COLS_OF_BOTH)
+                    dest[slots + slot] = value.astype(BF16)
+            else:
+                store(slots + slot, other, jnp.logical_not(upper))
+
+    return pl.pallas_call(
+        kernel,
+        out_shape=jax.ShapeDtypeStruct((2 * slots, units, units), BF16),
+        in_specs=[smem()] + [vmem()] * (3 + 2 * slots),
         out_specs=vmem(),
         name="couplings",
-    )(section, in_t, out_t, *near)
+    )(section, in_t, out_t, partner, *inner, *outer)
 
 
 def laid_out(down, up, blocks, step):
@@ -121,8 +156,7 @@
         for b in range(1, blocks):
             total = total + parts_ref[b].astype(F32)
         total = total.astype(BF16)
-        own[0] = total[lead : lead + half]
-        own[1] = total[lead + half :]
+        own[...] = total[lead : lead + half]
         for c in range(copies):
             dest[c, :rows] = total
             dest[c, rows:] = below_ref[...]
@@ -131,7 +165,7 @@
         kernel,
         out_shape=[
             jax.ShapeDtypeStruct((copies, rows + below.shape[0], units), BF16),
-            jax.ShapeDtypeStruct((2, half, units), BF16),
+            jax.ShapeDtypeStruct((half, units), BF16),
         ],
         in_specs=[vmem(), vmem()],
         out_specs=[vmem(), vmem()],
@@ -275,6 +309,19 @@
     )(top, row_weight, head, pre_down, pre_up, place)
 
 
+def held_at(upper, lower, count):
+    ring = count // 2
+    if upper // ring == lower // ring:
+        gap = upper - lower
+        return (lower, gap - 1) if gap <= ring // 2 else (upper, ring - gap - 1)
+    gap = (upper - lower) % ring
+    for slot in range(ring // 2):
+        if LOWER_OFFSETS[slot] % ring == gap:
+            return lower, ring // 2 + slot
+        if UPPER_OFFSETS[slot] % ring == gap:
+            return upper, ring // 2 + slot
+
+
 def chain(section, core, known, same, other):
     count, tall, units = known.shape
     lead = same.shape[2]
@@ -295,11 +342,7 @@
             ).astype(F32)
 
         def coupling(upper, lower):
-            gap = upper - lower
-            if gap <= count // 2:
-                at, slot = lower, gap - 1
-            else:
-                at, slot = upper, count - gap - 1
+            at, slot = held_at(upper, lower, count)
             mine, theirs = same_ref[slot, at], other_ref[slot, at]
             return jnp.concatenate(
                 [jnp.where(even, mine, theirs), jnp.where(even, theirs, mine)], axis=0
@@ -381,32 +424,33 @@
     )(wide, shared)
 
 
-def output_grads(section, cross, first, near, far):
+def output_grads(section, cross, first, weights):
     count, units, _ = cross.shape
     part = first.shape[1]
-    slots = len(near)
-    upper = count // 2
-
-    def kernel(section_ref, cross_ref, first_ref, far_ref, *refs):
-        dest = refs[slots]
+    ring = count // 2
+
+    def kernel(section_ref, cross_ref, first_ref, weights_ref, dest):
         own = section_ref[0]
-        total = first_ref[...].astype(F32)
-        for up in range(1, slots + 1):
-            total = total + dot(cross_ref[up], refs[up - 1][...])
-        dest[...] = total
-        for at in range(1, count - upper):
-
-            @pl.when(at > own)
+        upper = own >= ring
+        place = jnp.where(upper, own - ring, own)
+        dest[...] = first_ref[...].astype(F32)
+        for z in range(ring):
+
+            @pl.when(z > place)
             def _():
-                dest[...] += dot(cross_ref[at + upper - own], far_ref[at])
+                dest[...] += dot(cross_ref[z - place], weights_ref[z, 0])
+
+            @pl.when(jnp.logical_not(upper))
+            def _():
+                dest[...] += dot(cross_ref[jnp.minimum(ring + z - place, count - 1)], weights_ref[z, 1])
 
     return pl.pallas_call(
         kernel,
         out_shape=jax.ShapeDtypeStruct((units, part), F32),
-        in_specs=[smem()] + [vmem()] * (3 + slots),
+        in_specs=[smem()] + [vmem()] * 3,
         out_specs=vmem(),
         name="output_grads",
-    )(section, cross, first, far, *near)
+    )(section, cross, first, weights)
 
 
 def on_device(
@@ -441,22 +485,35 @@
     up = up_inputs[0].reshape(half, width)
     out_full = lax.all_gather(out_t, "fsdp", axis=0)
     wide = exchanged(laid_out(down, up, blocks, step), "fsdp")
-    near = []
-    for above in range(1, count // 2 + 1):
-        near.append(from_above(jnp.where(section_idx >= above, in_t, out_t), above))
+    ring = count // 2
+    place_idx = section_idx % ring
+    partner = lax.ppermute(
+        jnp.where(section_idx >= ring, in_t, out_t),
+        "section",
+        [(k, (k + ring) % count) for k in range(count)],
+    )
+    inner, outer = [], []
+    for slot in range(ring // 2):
+        steps = slot + 1
+        inner.append(
+            inside_half(
+                jnp.where(place_idx >= steps, in_t, out_t),
+                steps,
+                ring // 2 if 2 * steps == ring else ring,
+            )
+        )
     far_in_t = mirrored(in_t)
-
-    partner = lax.ppermute(
-        in_t, "section", [(k + count // 2, k) for k in range(count // 2)]
-    )
-    far_all = lax.all_gather(
-        partner,
+    for slot in range(ring // 2):
+        outer.append(across(partner, slot))
+    weights = lax.all_gather(
+        jnp.stack([in_t, partner]),
         "section",
         axis=0,
-        axis_index_groups=[list(range(count // 2)), list(range(count // 2, count))],
-    )
-
-    coupled = couplings(section, in_t, out_t, near, count).reshape(blocks, -1, units)
+        axis_index_groups=[list(range(ring)), list(range(ring, count))],
+    )
+
+    coupled = couplings(section, in_t, out_t, partner, inner, outer, count)
+    coupled = coupled.reshape(blocks, -1, units)
     lead = coupled.shape[1]
     row_weight, place = row_setup(
         fsdp_idx.astype(jnp.int32).reshape(1), plan, reward_pos, reward_cot, row_count
@@ -467,9 +524,10 @@
     parts = exchanged(parts, "fsdp")
     reached = top_products(top, row_weight, head, out_full, place, step)
     known, own_pre = folded_with(parts, reached, count, lead)
-    mirror_pre = mirrored(own_pre[1])
     known = exchanged(known, "section")
-    firsts = first_parts(top, row_weight, head, own_pre[0], mirror_pre, place, blocks, step)
+    mirror_pre = lax.dynamic_slice_in_dim(known, count - 1 - section_idx, 1, 0)
+    mirror_pre = mirror_pre[0, lead + half : lead + rows]
+    firsts = first_parts(top, row_weight, head, own_pre, mirror_pre, place, blocks, step)
     first = lax.psum_scatter(
         firsts.reshape(blocks * units, part), "fsdp", scatter_dimension=0, tiled=True
     )
@@ -485,7 +543,7 @@
     back_in = mirrored(far_in)
     cross = exchanged(folded(shared, blocks, units), "fsdp")
     own_in = input_grads(wide, shared, step, 0, F32)
-    grad_out = output_grads(section, cross, first, near, far_all)
+    grad_out = output_grads(section, cross, first, weights)
     grad_in = (own_in + back_in.astype(F32)).T
     return (grad_in[None], grad_out[None])
 

time: 295 us -> 305 us (1.034)
  the two profiles are of different devices: /device:TPU:16 before, /device:TPU:1 now
where the time goes in v4:
time: 305 us; the launch traced here: 304 us
  waiting for transfers between devices  121 us (40%)
  starting transfers between devices  79.1 us (26%)
  Pallas kernels  50 us (16%)
  blocking collectives  26.5 us (9%)
  between operations  15.7 us (5%)
  local copies, waits for them, and re-layouts  10.1 us (3%)
    all_to_all x5, waiting for transfers between devices, exchanged(): lax.all_to_all(parts, axis, 0, 0, axis_index_groups=groups, tiled=True)  82.8 us
    all_to_all x5, starting transfers between devices, exchanged(): lax.all_to_all(parts, axis, 0, 0, axis_index_groups=groups, tiled=True)  35.5 us
    all_to_all x1, blocking collectives, exchanged(): lax.all_to_all(parts, axis, 0, 0, axis_index_groups=groups, tiled=True)  26.5 us
    ppermute x4, starting transfers between devices, across(): return lax.ppermute(value, 'section', pairs)  24.1 us
    ppermute x4, waiting for transfers between devices, across(): return lax.ppermute(value, 'section', pairs)  18 us
    ppermute x1, waiting for transfers between devices, on_device(): lax.ppermute(jnp.where(section_idx >= ring, in_t, out_t), 'section', [(k,...  10.2 us
    ppermute x4, starting transfers between devices, inside_half(): return lax.ppermute(value, 'section', pairs)  8.48 us
    pallas_call x2, Pallas kernels, input_grads(): pl.pallas_call(kernel, grid=(blocks // step,), out_shape=jax.ShapeDtypeSt...  7.93 us
  transfers between devices with their start and end apart: 20, of which 8 were waited for; matrix products, arithmetic and copies ran while one was open for 2% of the time, Pallas kernels for 14%

profile of v4, /device:TPU:1, one launch (start us, length us, event | category | flops | bytes accessed | tf_op | source)
XLA Modules:
  0.0 303.8 jit_solution(15999077379678817335)
XLA Ops:
  8.7 4.2 %laid_out.1 = bf16[16,192,512]{2,1,0:T(8,128)(2,1)} custom-call(bf16[96,8192]{1,0:T(8,128)(2,1)} %bitcast.42, bf16[96,8192]{1,0:T(8,128)(2,1)} %bitcast.43), custom_call_target="tpu_custom_call" | custom-call | tf_op jit(solution)/shard_map/laid_out/pallas_call | solution.py:120
  12.9 6.9 %all-to-all-start = ((bf16[16,192,512]{2,1,0:T(8,128)(2,1)}), bf16[16,192,512]{2,1,0:T(8,128)(2,1)S(1)}, u32[]{:S(2)}, u32[]{:S(2)}) async-start(bf16[16,192,512]{2,1,0:T(8,128)(2,1)} %laid_out.1), calls=%async_computation | async-start | bytes 6291456 | tf_op jit(solution)/shard_map/all_to_all | solution.py:46
  22.8 5.6 %collective-permute-start.1 = (bf16[128,512]{1,0:T(8,128)(2,1)S(1)}, bf16[128,512]{1,0:T(8,128)(2,1)S(1)}, u32[]{:S(2)}, u32[]{:S(2)}) collective-permute-start(bf16[128,512]{1,0:T(8,128)(2,1)S(1)} %get-tuple-element.16), channel_id=1, source_target_pairs={{16,0},{32,16},{48,32},{64,48},{80,64},{96,80},{112,96},{0,112},{1... | collective-permute-start | bytes 393224 | tf_op jit(solution)/shard_map/ppermute | solution.py:28
  31.3 10.2 %collective-permute-done.partner_ref = bf16[128,512]{1,0:T(8,128)(2,1)S(1)} collective-permute-done((bf16[128,512]{1,0:T(8,128)(2,1)S(1)}, bf16[128,512]{1,0:T(8,128)(2,1)S(1)}, u32[]{:S(2)}, u32[]{:S(2)}) %collective-permute-start) | collective-permute-done | bytes 131104 | tf_op jit(solution)/shard_map/ppermute | solution.py:490
  42.2 17.0 %collective-permute-start.6 = (bf16[128,512]{1,0:T(8,128)(2,1)S(1)}, bf16[128,512]{1,0:T(8,128)(2,1)S(1)}, u32[]{:S(2)}, u32[]{:S(2)}) collective-permute-start(bf16[128,512]{1,0:T(8,128)(2,1)S(1)} %collective-permute-done.partner_ref), channel_id=1, source_target_pairs={{224,128},{240,144},{128,160},{144,176},{160,192},{176,208},{192,2... | collective-permute-start | bytes 393224 | tf_op jit(solution)/shard_map/ppermute | solution.py:37
  67.4 7.1 %collective-permute-done.7.refs_6_ = bf16[128,512]{1,0:T(8,128)(2,1)S(1)} collective-permute-done((bf16[128,512]{1,0:T(8,128)(2,1)S(1)}, bf16[128,512]{1,0:T(8,128)(2,1)S(1)}, u32[]{:S(2)}, u32[]{:S(2)}) %collective-permute-start.7) | collective-permute-done | bytes 131104 | tf_op jit(solution)/shard_map/ppermute | solution.py:37
  74.4 11.0 %collective-permute-done.8.refs_7_ = bf16[128,512]{1,0:T(8,128)(2,1)S(1)} collective-permute-done((bf16[128,512]{1,0:T(8,128)(2,1)S(1)}, bf16[128,512]{1,0:T(8,128)(2,1)S(1)}, u32[]{:S(2)}, u32[]{:S(2)}) %collective-permute-start.8) | collective-permute-done | bytes 131104 | tf_op jit(solution)/shard_map/ppermute | solution.py:37
  91.2 4.8 %pre_parts.1 = bf16[16,256,128]{2,1,0:T(8,128)(2,1)} custom-call(bf16[16,192,512]{2,1,0:T(8,128)(2,1)} %copy-done, bf16[16,64,128]{2,1,0:T(8,128)(2,1)} %bitcast.45, bf16[128,512]{1,0:T(8,128)(2,1)} %bitcast.39, bf16[128,512]{1,0:T(8,128)(2,1)} %collective-permute-done.9.far_ref), custom_call_target="tpu_custom_call" | custom-call | tf_op jit(solution)/shard_map/pre_parts/pallas_call | solution.py:224
  95.9 12.0 %all-to-all-start.1 = ((bf16[16,256,128]{2,1,0:T(8,128)(2,1)}), bf16[16,256,128]{2,1,0:T(8,128)(2,1)S(1)}, u32[]{:S(2)}, u32[]{:S(2)}) async-start(bf16[16,256,128]{2,1,0:T(8,128)(2,1)} %pre_parts.1), calls=%async_computation.1 | async-start | bytes 2097152 | tf_op jit(solution)/shard_map/all_to_all | solution.py:46
  111.1 4.9 %top_products.1.below_ref = bf16[192,128]{1,0:T(8,128)(2,1)} custom-call(bf16[192,8192]{1,0:T(8,128)(2,1)} %bitcast.34, f32[192,128]{1,0:T(8,128)} %get-tuple-element.6.weight_ref, f32[1,8192]{1,0:T(1,128)} %bitcast.48, bf16[16,128,512]{2,1,0:T(8,128)(2,1)} %all-gather.4.cloned.1.call-done.out_ref, f32[192,192]{1,0:T(8,128)} %get-tuple-element.7.place_ref), custom_call_target="tpu_custom_call" | custom-call | tf_op jit(solution)/shard_map/top_products/pallas_call | solution.py:263
  116.1 7.3 %all-to-all-done.1.parts_ref = bf16[16,256,128]{2,1,0:T(8,128)(2,1)S(1)} async-done(((bf16[16,256,128]{2,1,0:T(8,128)(2,1)}), bf16[16,256,128]{2,1,0:T(8,128)(2,1)S(1)}, u32[]{:S(2)}, u32[]{:S(2)}) %all-to-all-start.1) | async-done | bytes 1048608 | tf_op jit(solution)/shard_map/all_to_all | solution.py:46
  127.1 8.1 %all-to-all-start.2 = ((bf16[16,448,128]{2,1,0:T(8,128)(2,1)}), bf16[16,448,128]{2,1,0:T(8,128)(2,1)S(1)}, u32[]{:S(2)}, u32[]{:S(2)}) async-start(bf16[16,448,128]{2,1,0:T(8,128)(2,1)} %get-tuple-element.8), calls=%async_computation.2 | async-start | bytes 3670016 | tf_op jit(solution)/shard_map/all_to_all | solution.py:46
  136.0 54.6 %all-to-all-done.2.known_ref = bf16[16,448,128]{2,1,0:T(8,128)(2,1)S(1)} async-done(((bf16[16,448,128]{2,1,0:T(8,128)(2,1)}), bf16[16,448,128]{2,1,0:T(8,128)(2,1)S(1)}, u32[]{:S(2)}, u32[]{:S(2)}) %all-to-all-start.2) | async-done | bytes 1835040 | tf_op jit(solution)/shard_map/all_to_all | solution.py:46
  192.6 4.4 %all-to-all-start.3 = ((bf16[8,16,64,128]{3,2,1,0:T(8,128)(2,1)}), bf16[8,16,64,128]{3,2,1,0:T(8,128)(2,1)}, u32[]{:S(2)}, u32[]{:S(2)}) async-start(bf16[8,16,64,128]{3,2,1,0:T(8,128)(2,1)} %broadcast_in_dim.12), calls=%async_computation.3 | async-start | bytes 4194304 | tf_op jit(solution)/shard_map/all_to_all | solution.py:46
  197.6 5.1 %first_parts.1 = bf16[16,128,512]{2,1,0:T(8,128)(2,1)} custom-call(bf16[192,8192]{1,0:T(8,128)(2,1)} %bitcast.35, f32[192,128]{1,0:T(8,128)} %get-tuple-element.6.weight_ref, f32[1,8192]{1,0:T(1,128)} %bitcast.49, bf16[96,128]{1,0:T(8,128)(2,1)} %get-tuple-element.9.down_ref, bf16[96,128]{1,0:T(8,128)(2,1)} %dynamic-slice_bitcast_fusion.up_ref, ...), custom_call_target="tpu_custom_call" | custom-call | tf_op jit(solution)/shard_map/first_parts/pallas_call | solution.py:295
  202.8 20.8 %all-to-all-done.3.same_ref = bf16[8,16,64,128]{3,2,1,0:T(8,128)(2,1)} async-done(((bf16[8,16,64,128]{3,2,1,0:T(8,128)(2,1)}), bf16[8,16,64,128]{3,2,1,0:T(8,128)(2,1)}, u32[]{:S(2)}, u32[]{:S(2)}) %all-to-all-start.3) | async-done | bytes 2097184 | tf_op jit(solution)/shard_map/all_to_all | solution.py:46
  226.9 4.0 %collective-permute-done.10.other_ref = bf16[8,16,64,128]{3,2,1,0:T(8,128)(2,1)S(1)} collective-permute-done((bf16[8,16,64,128]{3,2,1,0:T(8,128)(2,1)}, bf16[8,16,64,128]{3,2,1,0:T(8,128)(2,1)S(1)}, u32[]{:S(2)}, u32[]{:S(2)}) %collective-permute-start.10) | collective-permute-done | bytes 2097184 | tf_op jit(solution)/shard_map/ppermute | solution.py:55
  232.2 7.5 %chain.1 = bf16[16,320,128]{2,1,0:T(8,128)(2,1)} custom-call(s32[1]{0:T(128)} %bitcast.2.section_ref, s32[1]{0:T(128)} %bitcast.3.core_ref, bf16[16,448,128]{2,1,0:T(8,128)(2,1)} %copy-done.1, bf16[8,16,64,128]{3,2,1,0:T(8,128)(2,1)} %all-to-all-done.3.same_ref, bf16[8,16,64,128]{3,2,1,0:T(8,128)(2,1)} %copy-done.6), custom_call_target="tpu_custom_call" | custom-call | tf_op jit(solution)/shard_map/chain/pallas_call | solution.py:379
  239.8 26.5 %all_to_all.30.shared_ref.parts_ref = bf16[16,320,128]{2,1,0:T(8,128)(2,1)} all-to-all(bf16[16,320,128]{2,1,0:T(8,128)(2,1)} %chain.1), channel_id=1, replica_groups=mesh['section'=16,'fsdp'=16] {'fsdp'}, dimensions={0} | all-to-all | bytes 2621440 | tf_op jit(solution)/shard_map/all_to_all | solution.py:46
  268.5 4.1 %all-to-all-start.5 = ((bf16[16,128,128]{2,1,0:T(8,128)(2,1)}), bf16[16,128,128]{2,1,0:T(8,128)(2,1)S(1)}, u32[]{:S(2)}, u32[]{:S(2)}) async-start(bf16[16,128,128]{2,1,0:T(8,128)(2,1)} %folded.1), calls=%async_computation.5 | async-start | bytes 1048576 | tf_op jit(solution)/shard_map/all_to_all | solution.py:46
  272.6 3.9 %shard_map.105 = bf16[128,512]{1,0:T(8,128)(2,1)} custom-call(bf16[16,192,512]{2,1,0:T(8,128)(2,1)} %copy-done, bf16[16,320,128]{2,1,0:T(8,128)(2,1)} %all_to_all.30.shared_ref.parts_ref), custom_call_target="tpu_custom_call" | custom-call | tf_op jit(solution)/shard_map/pallas_call | solution.py:414
  279.8 4.0 %shard_map.104 = f32[128,512]{1,0:T(8,128)} custom-call(bf16[16,192,512]{2,1,0:T(8,128)(2,1)} %copy-done, bf16[16,320,128]{2,1,0:T(8,128)(2,1)} %all_to_all.30.shared_ref.parts_ref), custom_call_target="tpu_custom_call" | custom-call | tf_op jit(solution)/shard_map/pallas_call | solution.py:414
  283.8 4.8 %collective-permute-done.11 = bf16[128,512]{1,0:T(8,128)(2,1)S(1)} collective-permute-done((bf16[128,512]{1,0:T(8,128)(2,1)}, bf16[128,512]{1,0:T(8,128)(2,1)S(1)}, u32[]{:S(2)}, u32[]{:S(2)}) %collective-permute-start.11) | collective-permute-done | bytes 131104 | tf_op jit(solution)/shard_map/ppermute | solution.py:42
  291.2 5.2 %output_grads.1 = f32[128,512]{1,0:T(8,128)} custom-call(s32[1]{0:T(128)} %bitcast.2.section_ref, bf16[16,128,128]{2,1,0:T(8,128)(2,1)} %copy-done.5, bf16[128,512]{1,0:T(8,128)(2,1)} %reduce-scatter.2.cloned.1.call-done.first_ref, bf16[8,2,128,512]{3,2,1,0:T(8,128)(2,1)} %bitcast.41), custom_call_target="tpu_custom_call" | custom-call | tf_op jit(solution)/shard_map/output_grads/pallas_call | solution.py:447
  (84 shorter events, 44.0 us)
Async XLA Ops:
  8.0 103.1 %all-gather.4.cloned.1.call-start = ((), (), s32[]{:S(2)}) async-start(), calls=%async_computation.7 | async-start | bytes 2228224 | tf_op jit(solution)/shard_map/all_gather | solution.py:486
  12.9 76.6 %all-to-all-start = ((bf16[16,192,512]{2,1,0:T(8,128)(2,1)}), bf16[16,192,512]{2,1,0:T(8,128)(2,1)S(1)}, u32[]{:S(2)}, u32[]{:S(2)}) async-start(bf16[16,192,512]{2,1,0:T(8,128)(2,1)} %laid_out.1), calls=%async_computation | async-start | bytes 6291456 | tf_op jit(solution)/shard_map/all_to_all | solution.py:46
  20.0 66.1 %copy-start.3 = (bf16[1,512,128]{1,2,0:T(8,128)(2,1)}, bf16[1,512,128]{1,2,0:T(8,128)(2,1)S(1)}, u32[]{:S(2)}) copy-start(bf16[1,512,128]{1,2,0:T(8,128)(2,1)S(1)} %copy.15) | copy-start | bytes 393220
  20.1 21.4 %collective-permute-start = (bf16[128,512]{1,0:T(8,128)(2,1)S(1)}, bf16[128,512]{1,0:T(8,128)(2,1)S(1)}, u32[]{:S(2)}, u32[]{:S(2)}) collective-permute-start(bf16[128,512]{1,0:T(8,128)(2,1)S(1)} %get-tuple-element.15), channel_id=1, source_target_pairs={{0,128},{16,144},{32,160},{48,176},{64,192},{80,208},{96,224},{112... | collective-permute-start | bytes 393224 | tf_op jit(solution)/shard_map/ppermute | solution.py:490
  22.8 19.4 %collective-permute-start.1 = (bf16[128,512]{1,0:T(8,128)(2,1)S(1)}, bf16[128,512]{1,0:T(8,128)(2,1)S(1)}, u32[]{:S(2)}, u32[]{:S(2)}) collective-permute-start(bf16[128,512]{1,0:T(8,128)(2,1)S(1)} %get-tuple-element.16), channel_id=1, source_target_pairs={{16,0},{32,16},{48,32},{64,48},{80,64},{96,80},{112,96},{0,112},{1... | collective-permute-start | bytes 393224 | tf_op jit(solution)/shard_map/ppermute | solution.py:28
  28.4 30.8 %collective-permute-start.2 = (bf16[128,512]{1,0:T(8,128)(2,1)S(1)}, bf16[128,512]{1,0:T(8,128)(2,1)S(1)}, u32[]{:S(2)}, u32[]{:S(2)}) collective-permute-start(bf16[128,512]{1,0:T(8,128)(2,1)S(1)} %get-tuple-element.17), channel_id=1, source_target_pairs={{32,0},{48,16},{64,32},{80,48},{96,64},{112,80},{0,96},{16,112},{1... | collective-permute-start | bytes 393224 | tf_op jit(solution)/shard_map/ppermute | solution.py:28
  29.5 33.1 %collective-permute-start.3 = (bf16[128,512]{1,0:T(8,128)(2,1)S(1)}, bf16[128,512]{1,0:T(8,128)(2,1)S(1)}, u32[]{:S(2)}, u32[]{:S(2)}) collective-permute-start(bf16[128,512]{1,0:T(8,128)(2,1)S(1)} %get-tuple-element.18), channel_id=1, source_target_pairs={{48,0},{64,16},{80,32},{96,48},{112,64},{0,80},{16,96},{32,112},{1... | collective-permute-start | bytes 393224 | tf_op jit(solution)/shard_map/ppermute | solution.py:28
  30.0 35.7 %collective-permute-start.4 = (bf16[128,512]{1,0:T(8,128)(2,1)S(1)}, bf16[128,512]{1,0:T(8,128)(2,1)S(1)}, u32[]{:S(2)}, u32[]{:S(2)}) collective-permute-start(bf16[128,512]{1,0:T(8,128)(2,1)S(1)} %get-tuple-element.14), channel_id=1, source_target_pairs={{64,0},{80,16},{96,32},{112,48},{192,128},{208,144},{224,160},{240... | collective-permute-start | bytes 393224 | tf_op jit(solution)/shard_map/ppermute | solution.py:28
  41.5 44.6 %copy-start.8 = (bf16[128,512]{1,0:T(8,128)(2,1)}, bf16[128,512]{1,0:T(8,128)(2,1)S(1)}, u32[]{:S(2)}) copy-start(bf16[128,512]{1,0:T(8,128)(2,1)S(1)} %collective-permute-done.partner_ref) | copy-start | bytes 393220
  41.5 25.8 %collective-permute-start.5 = (bf16[128,512]{1,0:T(8,128)(2,1)S(1)}, bf16[128,512]{1,0:T(8,128)(2,1)S(1)}, u32[]{:S(2)}, u32[]{:S(2)}) collective-permute-start(bf16[128,512]{1,0:T(8,128)(2,1)S(1)} %collective-permute-done.partner_ref), channel_id=1, source_target_pairs={{240,128},{128,144},{144,160},{160,176},{176,192},{192,208},{208,2... | collective-permute-start | bytes 393224 | tf_op jit(solution)/shard_map/ppermute | solution.py:37
  42.2 43.9 %copy-start.10 = (bf16[128,512]{1,0:T(8,128)(2,1)}, bf16[128,512]{1,0:T(8,128)(2,1)S(1)}, u32[]{:S(2)}) copy-start(bf16[128,512]{1,0:T(8,128)(2,1)S(1)} %collective-permute-done.1.refs_0_) | copy-start | bytes 393220
  42.2 25.2 %collective-permute-start.6 = (bf16[128,512]{1,0:T(8,128)(2,1)S(1)}, bf16[128,512]{1,0:T(8,128)(2,1)S(1)}, u32[]{:S(2)}, u32[]{:S(2)}) collective-permute-start(bf16[128,512]{1,0:T(8,128)(2,1)S(1)} %collective-permute-done.partner_ref), channel_id=1, source_target_pairs={{224,128},{240,144},{128,160},{144,176},{160,192},{176,208},{192,2... | collective-permute-start | bytes 393224 | tf_op jit(solution)/shard_map/ppermute | solution.py:37
  59.2 26.2 %copy-start.11 = (bf16[128,512]{1,0:T(8,128)(2,1)}, bf16[128,512]{1,0:T(8,128)(2,1)S(1)}, u32[]{:S(2)}) copy-start(bf16[128,512]{1,0:T(8,128)(2,1)S(1)} %collective-permute-done.2.refs_1_) | copy-start | bytes 393220
  59.2 15.3 %collective-permute-start.7 = (bf16[128,512]{1,0:T(8,128)(2,1)S(1)}, bf16[128,512]{1,0:T(8,128)(2,1)S(1)}, u32[]{:S(2)}, u32[]{:S(2)}) collective-permute-start(bf16[128,512]{1,0:T(8,128)(2,1)S(1)} %collective-permute-done.partner_ref), channel_id=1, source_target_pairs={{208,128},{224,144},{240,160},{128,176},{144,192},{160,208},{176,2... | collective-permute-start | bytes 393224 | tf_op jit(solution)/shard_map/ppermute | solution.py:37
  62.7 22.7 %collective-permute-start.8 = (bf16[128,512]{1,0:T(8,128)(2,1)S(1)}, bf16[128,512]{1,0:T(8,128)(2,1)S(1)}, u32[]{:S(2)}, u32[]{:S(2)}) collective-permute-start(bf16[128,512]{1,0:T(8,128)(2,1)S(1)} %collective-permute-done.partner_ref), channel_id=1, source_target_pairs={{160,128},{176,144},{192,160},{208,176},{224,192},{240,208},{128,2... | collective-permute-start | bytes 393224 | tf_op jit(solution)/shard_map/ppermute | solution.py:37
  65.6 23.9 %collective-permute-start.9 = (bf16[128,512]{1,0:T(8,128)(2,1)S(1)}, bf16[128,512]{1,0:T(8,128)(2,1)}, u32[]{:S(2)}, u32[]{:S(2)}) collective-permute-start(bf16[128,512]{1,0:T(8,128)(2,1)S(1)} %bitcast.37), channel_id=1, source_target_pairs={{0,240},{16,224},{32,208},{48,192},{64,176},{80,160},{96,144},{112... | collective-permute-start | bytes 393224 | tf_op jit(solution)/shard_map/ppermute | solution.py:42
  95.9 27.4 %all-to-all-start.1 = ((bf16[16,256,128]{2,1,0:T(8,128)(2,1)}), bf16[16,256,128]{2,1,0:T(8,128)(2,1)S(1)}, u32[]{:S(2)}, u32[]{:S(2)}) async-start(bf16[16,256,128]{2,1,0:T(8,128)(2,1)} %pre_parts.1), calls=%async_computation.1 | async-start | bytes 2097152 | tf_op jit(solution)/shard_map/all_to_all | solution.py:46
  127.1 63.5 %all-to-all-start.2 = ((bf16[16,448,128]{2,1,0:T(8,128)(2,1)}), bf16[16,448,128]{2,1,0:T(8,128)(2,1)S(1)}, u32[]{:S(2)}, u32[]{:S(2)}) async-start(bf16[16,448,128]{2,1,0:T(8,128)(2,1)} %get-tuple-element.8), calls=%async_computation.2 | async-start | bytes 3670016 | tf_op jit(solution)/shard_map/all_to_all | solution.py:46
  135.2 155.3 %all-gather.6.cloned.1.call-start = ((), (), s32[]{:S(2)}) async-start(), calls=%async_computation.9 | async-start | bytes 2359296 | tf_op jit(solution)/shard_map/all_gather | solution.py:508
  192.6 31.1 %all-to-all-start.3 = ((bf16[8,16,64,128]{3,2,1,0:T(8,128)(2,1)}), bf16[8,16,64,128]{3,2,1,0:T(8,128)(2,1)}, u32[]{:S(2)}, u32[]{:S(2)}) async-start(bf16[8,16,64,128]{3,2,1,0:T(8,128)(2,1)} %broadcast_in_dim.12), calls=%async_computation.3 | async-start | bytes 4194304 | tf_op jit(solution)/shard_map/all_to_all | solution.py:46
  196.9 93.5 %reduce-scatter.2.cloned.1.call-start = ((), (), s32[]{:S(2)}) async-start(), calls=%async_computation.8 | async-start | bytes 2228224 | tf_op jit(solution)/shard_map/reduce_scatter | solution.py:531
  223.6 7.3 %collective-permute-start.10 = (bf16[8,16,64,128]{3,2,1,0:T(8,128)(2,1)}, bf16[8,16,64,128]{3,2,1,0:T(8,128)(2,1)S(1)}, u32[]{:S(2)}, u32[]{:S(2)}) collective-permute-start(bf16[8,16,64,128]{3,2,1,0:T(8,128)(2,1)} %all-to-all-done.3.same_ref), channel_id=1, source_target_pairs={{0,1},{1,0},{2,3},{3,2},{4,5},{5,4},{6,7},{7,6},{8,9},{9,8},{10,11... | collective-permute-start | bytes 6291464 | tf_op jit(solution)/shard_map/ppermute | solution.py:55
  268.5 22.0 %all-to-all-start.5 = ((bf16[16,128,128]{2,1,0:T(8,128)(2,1)}), bf16[16,128,128]{2,1,0:T(8,128)(2,1)S(1)}, u32[]{:S(2)}, u32[]{:S(2)}) async-start(bf16[16,128,128]{2,1,0:T(8,128)(2,1)} %folded.1), calls=%async_computation.5 | async-start | bytes 1048576 | tf_op jit(solution)/shard_map/all_to_all | solution.py:46
  276.6 12.0 %collective-permute-start.11 = (bf16[128,512]{1,0:T(8,128)(2,1)}, bf16[128,512]{1,0:T(8,128)(2,1)S(1)}, u32[]{:S(2)}, u32[]{:S(2)}) collective-permute-start(bf16[128,512]{1,0:T(8,128)(2,1)} %shard_map.105), channel_id=1, source_target_pairs={{0,240},{16,224},{32,208},{48,192},{64,176},{80,160},{96,144},{112... | collective-permute-start | bytes 393224 | tf_op jit(solution)/shard_map/ppermute | solution.py:42
  (17 other events, 156.3 us)
Sparse Core Ops, SparseCore 0:
  10.7 69.9 all-gather.3
  202.9 77.2 reduce-scatter.1
Sparse Core Ops, SparseCore 1:
  137.4 62.0 all-gather.5

commit v5 on v4

--- a/solution.py
+++ b/solution.py
@@ -149,26 +149,29 @@
 
 def folded_with(parts, below, copies, lead):
     blocks, rows, units = parts.shape
-    half = (rows - lead) // 2
-
-    def kernel(parts_ref, below_ref, dest, own):
+    kept = rows - lead
+    half = kept // 2
+
+    def kernel(parts_ref, below_ref, coupled, known, far):
         total = parts_ref[0].astype(F32)
         for b in range(1, blocks):
             total = total + parts_ref[b].astype(F32)
         total = total.astype(BF16)
-        own[...] = total[lead : lead + half]
         for c in range(copies):
-            dest[c, :rows] = total
-            dest[c, rows:] = below_ref[...]
+            coupled[c] = total[:lead]
+        known[:kept] = total[lead:]
+        known[kept:] = below_ref[...]
+        far[...] = total[lead + half :]
 
     return pl.pallas_call(
         kernel,
         out_shape=[
-            jax.ShapeDtypeStruct((copies, rows + below.shape[0], units), BF16),
+            jax.ShapeDtypeStruct((copies, lead, units), BF16),
+            jax.ShapeDtypeStruct((kept + below.shape[0], units), BF16),
             jax.ShapeDtypeStruct((half, units), BF16),
         ],
         in_specs=[vmem(), vmem()],
-        out_specs=[vmem(), vmem()],
+        out_specs=[vmem(), vmem(), vmem()],
         name="folded_with",
     )(parts, below)
 
@@ -279,11 +282,11 @@
 
 def first_parts(top, row_weight, head, pre_down, pre_up, place, blocks, step):
     rows, width = top.shape
-    half, units = pre_down.shape
+    half, units = pre_up.shape
     part = width // blocks
 
     def kernel(top_ref, weight_ref, head_ref, down_ref, up_ref, place_ref, dest):
-        value = jnp.concatenate([down_ref[...], up_ref[...]], axis=0).astype(F32)
+        value = jnp.concatenate([down_ref[:half], up_ref[...]], axis=0).astype(F32)
         hidden = (value * jax.nn.sigmoid(value)).astype(BF16)
         placed = dot(place_ref[...].astype(BF16), hidden).astype(BF16)
         first = top_ref[...].astype(F32) + weight_ref[:, :1] * head_ref[...]
@@ -300,7 +303,7 @@
             pl.BlockSpec((rows, step * part), lambda b: (0, b)),
             pl.BlockSpec((rows, 128), lambda b: (0, 0)),
             pl.BlockSpec((1, step * part), lambda b: (0, b)),
-            pl.BlockSpec((half, units), lambda b: (0, 0)),
+            pl.BlockSpec((2 * rows, units), lambda b: (0, 0)),
             pl.BlockSpec((half, units), lambda b: (0, 0)),
             pl.BlockSpec((rows, rows), lambda b: (0, 0)),
         ],
@@ -322,21 +325,27 @@
             return upper, ring // 2 + slot
 
 
-def chain(section, core, known, same, other):
-    count, tall, units = known.shape
-    lead = same.shape[2]
-    rows = (tall - lead) // 2
+def chain(section, core, held, same, other, count):
+    ring = count // 2
+    _, tall, units = held[0].shape
+    rows = tall // 2
     half = rows // 2
 
-    def kernel(section_ref, core_ref, known_ref, same_ref, other_ref, dest, reach, grads):
+    def kernel(section_ref, core_ref, same_ref, other_ref, *refs):
+        dest, known_ref, reach, grads = refs[ring:]
         even = core_ref[0] == 0
         own = section_ref[0]
+        base = jnp.where(own >= ring, ring, 0)
+        for steps in range(ring):
+            at = lax.rem(own - base + steps, ring)
+            known_ref[base + at] = refs[steps][0]
+            known_ref[ring - base + at] = refs[steps][1]
 
         def pre_of(layer, other):
             return jnp.concatenate(
                 [
-                    known_ref[layer, lead : lead + half],
-                    known_ref[other, lead + half : lead + rows],
+                    known_ref[layer, :half],
+                    known_ref[other, half:rows],
                 ],
                 axis=0,
             ).astype(F32)
@@ -349,7 +358,7 @@
             )
 
         for layer in range(count):
-            reach[layer] = known_ref[layer, lead + rows :].astype(F32)
+            reach[layer] = known_ref[layer, rows:].astype(F32)
         for layer in range(count - 1, -1, -1):
             pre = pre_of(layer, count - 1 - layer)
             sig = jax.nn.sigmoid(pre)
@@ -379,14 +388,15 @@
     return pl.pallas_call(
         kernel,
         out_shape=jax.ShapeDtypeStruct((count, units + rows, units), BF16),
-        in_specs=[smem(), smem(), vmem(), vmem(), vmem()],
+        in_specs=[smem(), smem()] + [vmem()] * (2 + ring),
         out_specs=vmem(),
         scratch_shapes=[
+            pltpu.VMEM((count, tall, units), BF16),
             pltpu.VMEM((count, rows, units), F32),
             pltpu.VMEM((count, rows, units), BF16),
         ],
         name="chain",
-    )(section, core, known, same, other)
+    )(section, core, same, other, *held)
 
 
 def input_grads(wide, shared, step, side, kind):
@@ -523,21 +533,23 @@
     parts = pre_parts(wide, coupled, in_t, far_in_t, step)
     parts = exchanged(parts, "fsdp")
     reached = top_products(top, row_weight, head, out_full, place, step)
-    known, own_pre = folded_with(parts, reached, count, lead)
-    known = exchanged(known, "section")
-    mirror_pre = lax.dynamic_slice_in_dim(known, count - 1 - section_idx, 1, 0)
-    mirror_pre = mirror_pre[0, lead + half : lead + rows]
-    firsts = first_parts(top, row_weight, head, own_pre, mirror_pre, place, blocks, step)
+    coupled, known, far_pre = folded_with(parts, reached, count, lead)
+    coupled = exchanged(coupled, "section")
+    mirror_pre = mirrored(far_pre)
+    known_partner = lax.ppermute(known, "section", [(k, (k + ring) % count) for k in range(count)])
+    held = [jnp.stack([known, known_partner])]
+    for steps in range(1, ring):
+        held.append(inside_half(held[0], steps, ring))
+    firsts = first_parts(top, row_weight, head, known, mirror_pre, place, blocks, step)
     first = lax.psum_scatter(
         firsts.reshape(blocks * units, part), "fsdp", scatter_dimension=0, tiled=True
     )
-    coupled = known[:, :lead]
     coupled_same = exchanged(
         jnp.broadcast_to(coupled[None], (blocks // 2,) + coupled.shape), "fsdp", groups
     )
     coupled_other = from_other_core(coupled_same)
 
-    shared = chain(section, core, known, coupled_same, coupled_other)
+    shared = chain(section, core, held, coupled_same, coupled_other, count)
     shared = exchanged(shared, "fsdp")
     far_in = input_grads(wide, shared, step, 1, BF16)
     back_in = mirrored(far_in)

time: 305 us -> 317 us (1.039)
  the two profiles are of different devices: /device:TPU:1 before, /device:TPU:16 now
where the time goes in v5:
time: 317 us; the launch traced here: 311 us
  waiting for transfers between devices  99.9 us (32%)
  starting transfers between devices  99.3 us (31%)
  Pallas kernels  48.1 us (15%)
  blocking collectives  37.9 us (12%)
  between operations  14 us (4%)
  local copies, waits for them, and re-layouts  8.91 us (3%)
    ppermute x11, starting transfers between devices, inside_half(): return lax.ppermute(value, 'section', pairs)  42.9 us
    all_to_all x2, blocking collectives, exchanged(): lax.all_to_all(parts, axis, 0, 0, axis_index_groups=groups, tiled=True)  37.9 us
    all_to_all x4, starting transfers between devices, exchanged(): lax.all_to_all(parts, axis, 0, 0, axis_index_groups=groups, tiled=True)  31.6 us
    ppermute x1, waiting for transfers between devices, on_device(): lax.ppermute(jnp.where(section_idx >= ring, in_t, out_t), 'section', [(k,...  30.5 us
    all_to_all x4, waiting for transfers between devices, exchanged(): lax.all_to_all(parts, axis, 0, 0, axis_index_groups=groups, tiled=True)  22.2 us
    ppermute x11, waiting for transfers between devices, inside_half(): return lax.ppermute(value, 'section', pairs)  19.8 us
    ppermute x3, waiting for transfers between devices, mirrored(): lax.ppermute(value, 'section', [(k, count - 1 - k) for k in range(count)])  18.1 us
    ppermute x4, starting transfers between devices, across(): return lax.ppermute(value, 'section', pairs)  11.3 us
  transfers between devices with their start and end apart: 28, of which 14 were waited for; matrix products, arithmetic and copies ran while one was open for 2% of the time, Pallas kernels for 14%

profile of v5, /device:TPU:16, one launch (start us, length us, event | category | flops | bytes accessed | tf_op | source)
XLA Modules:
  0.0 310.8 jit_solution(7185988718647566402)
XLA Ops:
  7.9 4.2 %laid_out.1 = bf16[16,192,512]{2,1,0:T(8,128)(2,1)} custom-call(bf16[96,8192]{1,0:T(8,128)(2,1)} %bitcast.42, bf16[96,8192]{1,0:T(8,128)(2,1)} %bitcast.43), custom_call_target="tpu_custom_call" | custom-call | tf_op jit(solution)/shard_map/laid_out/pallas_call | solution.py:120
  12.1 5.3 %all-to-all-start = ((bf16[16,192,512]{2,1,0:T(8,128)(2,1)}), bf16[16,192,512]{2,1,0:T(8,128)(2,1)S(1)}, u32[]{:S(2)}, u32[]{:S(2)}) async-start(bf16[16,192,512]{2,1,0:T(8,128)(2,1)} %laid_out.1), calls=%async_computation | async-start | bytes 6291456 | tf_op jit(solution)/shard_map/all_to_all | solution.py:46
  19.1 30.5 %collective-permute-done.partner_ref = bf16[128,512]{1,0:T(8,128)(2,1)S(1)} collective-permute-done((bf16[128,512]{1,0:T(8,128)(2,1)S(1)}, bf16[128,512]{1,0:T(8,128)(2,1)S(1)}, u32[]{:S(2)}, u32[]{:S(2)}) %collective-permute-start) | collective-permute-done | bytes 131104 | tf_op jit(solution)/shard_map/ppermute | solution.py:500
  50.3 9.0 %collective-permute-start.1 = (bf16[128,512]{1,0:T(8,128)(2,1)}, bf16[128,512]{1,0:T(8,128)(2,1)S(1)}, u32[]{:S(2)}, u32[]{:S(2)}) collective-permute-start(bf16[128,512]{1,0:T(8,128)(2,1)} %get-tuple-element.18), channel_id=1, source_target_pairs={{16,0},{32,16},{48,32},{64,48},{80,64},{96,80},{112,96},{0,112},{1... | collective-permute-start | bytes 393224 | tf_op jit(solution)/shard_map/ppermute | solution.py:28
  79.0 5.4 %collective-permute-start.9 = (bf16[128,512]{1,0:T(8,128)(2,1)S(1)}, bf16[128,512]{1,0:T(8,128)(2,1)S(1)}, u32[]{:S(2)}, u32[]{:S(2)}) collective-permute-start(bf16[128,512]{1,0:T(8,128)(2,1)S(1)} %bitcast.38), channel_id=1, source_target_pairs={{0,240},{16,224},{32,208},{48,192},{64,176},{80,160},{96,144},{112... | collective-permute-start | bytes 393224 | tf_op jit(solution)/shard_map/ppermute | solution.py:42
  91.3 8.0 %collective-permute-done.9.far_ref = bf16[128,512]{1,0:T(8,128)(2,1)S(1)} collective-permute-done((bf16[128,512]{1,0:T(8,128)(2,1)S(1)}, bf16[128,512]{1,0:T(8,128)(2,1)S(1)}, u32[]{:S(2)}, u32[]{:S(2)}) %collective-permute-start.9) | collective-permute-done | bytes 131104 | tf_op jit(solution)/shard_map/ppermute | solution.py:42
  101.0 4.8 %pre_parts.1 = bf16[16,256,128]{2,1,0:T(8,128)(2,1)} custom-call(bf16[16,192,512]{2,1,0:T(8,128)(2,1)} %copy-done, bf16[16,64,128]{2,1,0:T(8,128)(2,1)} %bitcast.45, bf16[128,512]{1,0:T(8,128)(2,1)} %bitcast.40, bf16[128,512]{1,0:T(8,128)(2,1)} %copy-done.22), custom_call_target="tpu_custom_call" | custom-call | tf_op jit(solution)/shard_map/pre_parts/pallas_call | solution.py:227
  105.8 18.9 %all-to-all-start.1 = ((bf16[16,256,128]{2,1,0:T(8,128)(2,1)}), bf16[16,256,128]{2,1,0:T(8,128)(2,1)S(1)}, u32[]{:S(2)}, u32[]{:S(2)}) async-start(bf16[16,256,128]{2,1,0:T(8,128)(2,1)} %pre_parts.1), calls=%async_computation.1 | async-start | bytes 2097152 | tf_op jit(solution)/shard_map/all_to_all | solution.py:46
  127.9 4.9 %top_products.1.below_ref = bf16[192,128]{1,0:T(8,128)(2,1)} custom-call(bf16[192,8192]{1,0:T(8,128)(2,1)} %bitcast.34, f32[192,128]{1,0:T(8,128)} %get-tuple-element.7.weight_ref, f32[1,8192]{1,0:T(1,128)} %bitcast.49, bf16[16,128,512]{2,1,0:T(8,128)(2,1)} %all-gather.4.cloned.1.call-done.out_ref, f32[192,192]{1,0:T(8,128)} %get-tuple-element.8.place_ref), custom_call_target="tpu_custom_call" | custom-call | tf_op jit(solution)/shard_map/top_products/pallas_call | solution.py:266
  132.8 8.3 %all-to-all-done.1.parts_ref = bf16[16,256,128]{2,1,0:T(8,128)(2,1)S(1)} async-done(((bf16[16,256,128]{2,1,0:T(8,128)(2,1)}), bf16[16,256,128]{2,1,0:T(8,128)(2,1)S(1)}, u32[]{:S(2)}, u32[]{:S(2)}) %all-to-all-start.1) | async-done | bytes 1048608 | tf_op jit(solution)/shard_map/all_to_all | solution.py:46
  144.2 14.6 %all_to_all.30 = bf16[16,64,128]{2,1,0:T(8,128)(2,1)S(1)} all-to-all(bf16[16,64,128]{2,1,0:T(8,128)(2,1)} %get-tuple-element.9), channel_id=1, replica_groups=mesh['section'=16,'fsdp'=16] {'section'}, dimensions={0} | all-to-all | bytes 524288 | tf_op jit(solution)/shard_map/all_to_all | solution.py:46
  164.7 4.3 %collective-permute-start.20 = (bf16[96,128]{1,0:T(8,128)(2,1)S(1)}, bf16[96,128]{1,0:T(8,128)(2,1)S(1)}, u32[]{:S(2)}, u32[]{:S(2)}) collective-permute-start(bf16[96,128]{1,0:T(8,128)(2,1)S(1)} %copy-done.28), channel_id=1, source_target_pairs={{0,240},{16,224},{32,208},{48,192},{64,176},{80,160},{96,144},{112... | collective-permute-start | bytes 73736 | tf_op jit(solution)/shard_map/ppermute | solution.py:42
  168.9 5.0 %collective-permute-done.20.up_ref = bf16[96,128]{1,0:T(8,128)(2,1)S(1)} collective-permute-done((bf16[96,128]{1,0:T(8,128)(2,1)S(1)}, bf16[96,128]{1,0:T(8,128)(2,1)S(1)}, u32[]{:S(2)}, u32[]{:S(2)}) %collective-permute-start.20) | collective-permute-done | bytes 24608 | tf_op jit(solution)/shard_map/ppermute | solution.py:42
  174.5 5.2 %first_parts.1 = bf16[16,128,512]{2,1,0:T(8,128)(2,1)} custom-call(bf16[192,8192]{1,0:T(8,128)(2,1)} %bitcast.35, f32[192,128]{1,0:T(8,128)} %get-tuple-element.7.weight_ref, f32[1,8192]{1,0:T(1,128)} %bitcast.50, bf16[384,128]{1,0:T(8,128)(2,1)} %get-tuple-element.10.down_ref, bf16[96,128]{1,0:T(8,128)(2,1)} %copy-done.25, ...), custom_call_target="tpu_custom_call" | custom-call | tf_op jit(solution)/shard_map/first_parts/pallas_call | solution.py:298
  179.7 13.9 %all-to-all-done.3.same_ref = bf16[8,16,64,128]{3,2,1,0:T(8,128)(2,1)S(1)} async-done(((bf16[8,16,64,128]{3,2,1,0:T(8,128)(2,1)}), bf16[8,16,64,128]{3,2,1,0:T(8,128)(2,1)S(1)}, u32[]{:S(2)}, u32[]{:S(2)}) %all-to-all-start.3) | async-done | bytes 2097184 | tf_op jit(solution)/shard_map/all_to_all | solution.py:46
  196.3 6.1 %collective-permute-done.11 = bf16[384,128]{1,0:T(8,128)(2,1)S(1)} collective-permute-done((bf16[384,128]{1,0:T(8,128)(2,1)S(1)}, bf16[384,128]{1,0:T(8,128)(2,1)S(1)}, u32[]{:S(2)}, u32[]{:S(2)}) %collective-permute-start.11) | collective-permute-done | bytes 98336 | tf_op jit(solution)/shard_map/ppermute | solution.py:539
  213.1 4.6 %collective-permute-start.16 = (bf16[2,384,128]{2,1,0:T(8,128)(2,1)S(1)}, bf16[2,384,128]{2,1,0:T(8,128)(2,1)S(1)}, u32[]{:S(2)}, u32[]{:S(2)}) collective-permute-start(bf16[2,384,128]{2,1,0:T(8,128)(2,1)S(1)} %pad_maximum_fusion.1.refs_0_), channel_id=1, source_target_pairs={{80,0},{96,16},{112,32},{0,48},{16,64},{32,80},{48,96},{64,112},{2... | collective-permute-start | bytes 589832 | tf_op jit(solution)/shard_map/ppermute | solution.py:28
  217.7 8.7 %collective-permute-done.13.refs_2_ = bf16[2,384,128]{2,1,0:T(8,128)(2,1)S(1)} collective-permute-done((bf16[2,384,128]{2,1,0:T(8,128)(2,1)S(1)}, bf16[2,384,128]{2,1,0:T(8,128)(2,1)S(1)}, u32[]{:S(2)}, u32[]{:S(2)}) %collective-permute-start.13) | collective-permute-done | bytes 196640 | tf_op jit(solution)/shard_map/ppermute | solution.py:28
  226.5 5.2 %collective-permute-start.17 = (bf16[2,384,128]{2,1,0:T(8,128)(2,1)S(1)}, bf16[2,384,128]{2,1,0:T(8,128)(2,1)S(1)}, u32[]{:S(2)}, u32[]{:S(2)}) collective-permute-start(bf16[2,384,128]{2,1,0:T(8,128)(2,1)S(1)} %pad_maximum_fusion.1.refs_0_), channel_id=1, source_target_pairs={{96,0},{112,16},{0,32},{16,48},{32,64},{48,80},{64,96},{80,112},{2... | collective-permute-start | bytes 589832 | tf_op jit(solution)/shard_map/ppermute | solution.py:28
  232.5 12.1 %collective-permute-start.18 = (bf16[2,384,128]{2,1,0:T(8,128)(2,1)S(1)}, bf16[2,384,128]{2,1,0:T(8,128)(2,1)}, u32[]{:S(2)}, u32[]{:S(2)}) collective-permute-start(bf16[2,384,128]{2,1,0:T(8,128)(2,1)S(1)} %pad_maximum_fusion.1.refs_0_), channel_id=1, source_target_pairs={{112,0},{0,16},{16,32},{32,48},{48,64},{64,80},{80,96},{96,112},{2... | collective-permute-start | bytes 589832 | tf_op jit(solution)/shard_map/ppermute | solution.py:28
  247.9 7.5 %chain.1 = bf16[16,320,128]{2,1,0:T(8,128)(2,1)} custom-call(s32[1]{0:T(128)} %bitcast.2.section_ref, s32[1]{0:T(128)} %bitcast.3.core_ref, bf16[8,16,64,128]{3,2,1,0:T(8,128)(2,1)} %copy-done.1, bf16[8,16,64,128]{3,2,1,0:T(8,128)(2,1)} %collective-permute-done.10.other_ref, bf16[2,384,128]{2,1,0:T(8,128)(2,1)} %copy-done.6, bf16[2,384,128]{2,1,0:T(8,128)(2,1)} %copy-done.9, ...), custom_call_target="tpu_custom_call" | custom-call | tf_op jit(solution)/shard_map/chain/pallas_call | solution.py:388
  255.3 23.3 %all_to_all.31.shared_ref.parts_ref = bf16[16,320,128]{2,1,0:T(8,128)(2,1)} all-to-all(bf16[16,320,128]{2,1,0:T(8,128)(2,1)} %chain.1), channel_id=1, replica_groups=mesh['section'=16,'fsdp'=16] {'fsdp'}, dimensions={0} | all-to-all | bytes 2621440 | tf_op jit(solution)/shard_map/all_to_all | solution.py:46
  288.8 4.0 %shard_map.104 = f32[128,512]{1,0:T(8,128)} custom-call(bf16[16,192,512]{2,1,0:T(8,128)(2,1)} %copy-done, bf16[16,320,128]{2,1,0:T(8,128)(2,1)} %all_to_all.31.shared_ref.parts_ref), custom_call_target="tpu_custom_call" | custom-call | tf_op jit(solution)/shard_map/pallas_call | solution.py:424
  292.8 5.1 %collective-permute-done.19 = bf16[128,512]{1,0:T(8,128)(2,1)S(1)} collective-permute-done((bf16[128,512]{1,0:T(8,128)(2,1)}, bf16[128,512]{1,0:T(8,128)(2,1)S(1)}, u32[]{:S(2)}, u32[]{:S(2)}) %collective-permute-start.19) | collective-permute-done | bytes 131104 | tf_op jit(solution)/shard_map/ppermute | solution.py:42
  (116 shorter events, 78.1 us)
Async XLA Ops:
  7.2 120.7 %all-gather.4.cloned.1.call-start = ((), (), s32[]{:S(2)}) async-start(), calls=%async_computation.7 | async-start | bytes 2228224 | tf_op jit(solution)/shard_map/all_gather | solution.py:496
  12.1 87.2 %all-to-all-start = ((bf16[16,192,512]{2,1,0:T(8,128)(2,1)}), bf16[16,192,512]{2,1,0:T(8,128)(2,1)S(1)}, u32[]{:S(2)}, u32[]{:S(2)}) async-start(bf16[16,192,512]{2,1,0:T(8,128)(2,1)} %laid_out.1), calls=%async_computation | async-start | bytes 6291456 | tf_op jit(solution)/shard_map/all_to_all | solution.py:46
  17.4 282.3 %all-gather.6.cloned.1.call-start = ((), (), s32[]{:S(2)}) async-start(), calls=%async_computation.9 | async-start | bytes 2359296 | tf_op jit(solution)/shard_map/all_gather | solution.py:518
  18.4 31.1 %collective-permute-start = (bf16[128,512]{1,0:T(8,128)(2,1)S(1)}, bf16[128,512]{1,0:T(8,128)(2,1)S(1)}, u32[]{:S(2)}, u32[]{:S(2)}) collective-permute-start(bf16[128,512]{1,0:T(8,128)(2,1)S(1)} %get-tuple-element.17), channel_id=1, source_target_pairs={{0,128},{16,144},{32,160},{48,176},{64,192},{80,208},{96,224},{112... | collective-permute-start | bytes 393224 | tf_op jit(solution)/shard_map/ppermute | solution.py:500
  50.3 14.1 %collective-permute-start.1 = (bf16[128,512]{1,0:T(8,128)(2,1)}, bf16[128,512]{1,0:T(8,128)(2,1)S(1)}, u32[]{:S(2)}, u32[]{:S(2)}) collective-permute-start(bf16[128,512]{1,0:T(8,128)(2,1)} %get-tuple-element.18), channel_id=1, source_target_pairs={{16,0},{32,16},{48,32},{64,48},{80,64},{96,80},{112,96},{0,112},{1... | collective-permute-start | bytes 393224 | tf_op jit(solution)/shard_map/ppermute | solution.py:28
  59.3 11.4 %collective-permute-start.2 = (bf16[128,512]{1,0:T(8,128)(2,1)}, bf16[128,512]{1,0:T(8,128)(2,1)S(1)}, u32[]{:S(2)}, u32[]{:S(2)}) collective-permute-start(bf16[128,512]{1,0:T(8,128)(2,1)} %get-tuple-element.19), channel_id=1, source_target_pairs={{32,0},{48,16},{64,32},{80,48},{96,64},{112,80},{0,96},{16,112},{1... | collective-permute-start | bytes 393224 | tf_op jit(solution)/shard_map/ppermute | solution.py:28
  59.3 16.7 %collective-permute-start.3 = (bf16[128,512]{1,0:T(8,128)(2,1)}, bf16[128,512]{1,0:T(8,128)(2,1)S(1)}, u32[]{:S(2)}, u32[]{:S(2)}) collective-permute-start(bf16[128,512]{1,0:T(8,128)(2,1)} %get-tuple-element.20), channel_id=1, source_target_pairs={{48,0},{64,16},{80,32},{96,48},{112,64},{0,80},{16,96},{32,112},{1... | collective-permute-start | bytes 393224 | tf_op jit(solution)/shard_map/ppermute | solution.py:28
  59.3 19.7 %collective-permute-start.4 = (bf16[128,512]{1,0:T(8,128)(2,1)S(1)}, bf16[128,512]{1,0:T(8,128)(2,1)S(1)}, u32[]{:S(2)}, u32[]{:S(2)}) collective-permute-start(bf16[128,512]{1,0:T(8,128)(2,1)S(1)} %get-tuple-element.16), channel_id=1, source_target_pairs={{64,0},{80,16},{96,32},{112,48},{192,128},{208,144},{224,160},{240... | collective-permute-start | bytes 393224 | tf_op jit(solution)/shard_map/ppermute | solution.py:28
  60.6 23.8 %collective-permute-start.5 = (bf16[128,512]{1,0:T(8,128)(2,1)S(1)}, bf16[128,512]{1,0:T(8,128)(2,1)S(1)}, u32[]{:S(2)}, u32[]{:S(2)}) collective-permute-start(bf16[128,512]{1,0:T(8,128)(2,1)S(1)} %collective-permute-done.partner_ref), channel_id=1, source_target_pairs={{240,128},{128,144},{144,160},{160,176},{176,192},{192,208},{208,2... | collective-permute-start | bytes 393224 | tf_op jit(solution)/shard_map/ppermute | solution.py:37
  64.4 22.5 %collective-permute-start.6 = (bf16[128,512]{1,0:T(8,128)(2,1)S(1)}, bf16[128,512]{1,0:T(8,128)(2,1)S(1)}, u32[]{:S(2)}, u32[]{:S(2)}) collective-permute-start(bf16[128,512]{1,0:T(8,128)(2,1)S(1)} %collective-permute-done.partner_ref), channel_id=1, source_target_pairs={{224,128},{240,144},{128,160},{144,176},{160,192},{176,208},{192,2... | collective-permute-start | bytes 393224 | tf_op jit(solution)/shard_map/ppermute | solution.py:37
  70.7 16.2 %collective-permute-start.7 = (bf16[128,512]{1,0:T(8,128)(2,1)S(1)}, bf16[128,512]{1,0:T(8,128)(2,1)S(1)}, u32[]{:S(2)}, u32[]{:S(2)}) collective-permute-start(bf16[128,512]{1,0:T(8,128)(2,1)S(1)} %collective-permute-done.partner_ref), channel_id=1, source_target_pairs={{208,128},{224,144},{240,160},{128,176},{144,192},{160,208},{176,2... | collective-permute-start | bytes 393224 | tf_op jit(solution)/shard_map/ppermute | solution.py:37
  76.0 10.9 %collective-permute-start.8 = (bf16[128,512]{1,0:T(8,128)(2,1)S(1)}, bf16[128,512]{1,0:T(8,128)(2,1)S(1)}, u32[]{:S(2)}, u32[]{:S(2)}) collective-permute-start(bf16[128,512]{1,0:T(8,128)(2,1)S(1)} %collective-permute-done.partner_ref), channel_id=1, source_target_pairs={{160,128},{176,144},{192,160},{208,176},{224,192},{240,208},{128,2... | collective-permute-start | bytes 393224 | tf_op jit(solution)/shard_map/ppermute | solution.py:37
  79.0 20.4 %collective-permute-start.9 = (bf16[128,512]{1,0:T(8,128)(2,1)S(1)}, bf16[128,512]{1,0:T(8,128)(2,1)S(1)}, u32[]{:S(2)}, u32[]{:S(2)}) collective-permute-start(bf16[128,512]{1,0:T(8,128)(2,1)S(1)} %bitcast.38), channel_id=1, source_target_pairs={{0,240},{16,224},{32,208},{48,192},{64,176},{80,160},{96,144},{112... | collective-permute-start | bytes 393224 | tf_op jit(solution)/shard_map/ppermute | solution.py:42
  105.8 35.3 %all-to-all-start.1 = ((bf16[16,256,128]{2,1,0:T(8,128)(2,1)}), bf16[16,256,128]{2,1,0:T(8,128)(2,1)S(1)}, u32[]{:S(2)}, u32[]{:S(2)}) async-start(bf16[16,256,128]{2,1,0:T(8,128)(2,1)} %pre_parts.1), calls=%async_computation.1 | async-start | bytes 2097152 | tf_op jit(solution)/shard_map/all_to_all | solution.py:46
  160.7 32.9 %all-to-all-start.3 = ((bf16[8,16,64,128]{3,2,1,0:T(8,128)(2,1)}), bf16[8,16,64,128]{3,2,1,0:T(8,128)(2,1)S(1)}, u32[]{:S(2)}, u32[]{:S(2)}) async-start(bf16[8,16,64,128]{3,2,1,0:T(8,128)(2,1)} %broadcast_in_dim.12), calls=%async_computation.3 | async-start | bytes 4194304 | tf_op jit(solution)/shard_map/all_to_all | solution.py:46
  164.6 135.1 %reduce-scatter.2.cloned.1.call-start = ((), (), s32[]{:S(2)}) async-start(), calls=%async_computation.8 | async-start | bytes 2228224 | tf_op jit(solution)/shard_map/reduce_scatter | solution.py:544
  193.6 54.2 %collective-permute-start.10 = (bf16[8,16,64,128]{3,2,1,0:T(8,128)(2,1)S(1)}, bf16[8,16,64,128]{3,2,1,0:T(8,128)(2,1)}, u32[]{:S(2)}, u32[]{:S(2)}) collective-permute-start(bf16[8,16,64,128]{3,2,1,0:T(8,128)(2,1)S(1)} %all-to-all-done.3.same_ref), channel_id=1, source_target_pairs={{0,1},{1,0},{2,3},{3,2},{4,5},{5,4},{6,7},{7,6},{8,9},{9,8},{10,11... | collective-permute-start | bytes 6291464 | tf_op jit(solution)/shard_map/ppermute | solution.py:55
  205.2 21.3 %collective-permute-start.13 = (bf16[2,384,128]{2,1,0:T(8,128)(2,1)S(1)}, bf16[2,384,128]{2,1,0:T(8,128)(2,1)S(1)}, u32[]{:S(2)}, u32[]{:S(2)}) collective-permute-start(bf16[2,384,128]{2,1,0:T(8,128)(2,1)S(1)} %pad_maximum_fusion.1.refs_0_), channel_id=1, source_target_pairs={{32,0},{48,16},{64,32},{80,48},{96,64},{112,80},{0,96},{16,112},{1... | collective-permute-start | bytes 589832 | tf_op jit(solution)/shard_map/ppermute | solution.py:28
  207.1 25.4 %collective-permute-start.14 = (bf16[2,384,128]{2,1,0:T(8,128)(2,1)S(1)}, bf16[2,384,128]{2,1,0:T(8,128)(2,1)S(1)}, u32[]{:S(2)}, u32[]{:S(2)}) collective-permute-start(bf16[2,384,128]{2,1,0:T(8,128)(2,1)S(1)} %pad_maximum_fusion.1.refs_0_), channel_id=1, source_target_pairs={{48,0},{64,16},{80,32},{96,48},{112,64},{0,80},{16,96},{32,112},{1... | collective-permute-start | bytes 589832 | tf_op jit(solution)/shard_map/ppermute | solution.py:28
  210.5 34.1 %collective-permute-start.15 = (bf16[2,384,128]{2,1,0:T(8,128)(2,1)S(1)}, bf16[2,384,128]{2,1,0:T(8,128)(2,1)S(1)}, u32[]{:S(2)}, u32[]{:S(2)}) collective-permute-start(bf16[2,384,128]{2,1,0:T(8,128)(2,1)S(1)} %pad_maximum_fusion.1.refs_0_), channel_id=1, source_target_pairs={{64,0},{80,16},{96,32},{112,48},{0,64},{16,80},{32,96},{48,112},{1... | collective-permute-start | bytes 589832 | tf_op jit(solution)/shard_map/ppermute | solution.py:28
  213.1 31.4 %collective-permute-start.16 = (bf16[2,384,128]{2,1,0:T(8,128)(2,1)S(1)}, bf16[2,384,128]{2,1,0:T(8,128)(2,1)S(1)}, u32[]{:S(2)}, u32[]{:S(2)}) collective-permute-start(bf16[2,384,128]{2,1,0:T(8,128)(2,1)S(1)} %pad_maximum_fusion.1.refs_0_), channel_id=1, source_target_pairs={{80,0},{96,16},{112,32},{0,48},{16,64},{32,80},{48,96},{64,112},{2... | collective-permute-start | bytes 589832 | tf_op jit(solution)/shard_map/ppermute | solution.py:28
  226.5 18.9 %collective-permute-start.17 = (bf16[2,384,128]{2,1,0:T(8,128)(2,1)S(1)}, bf16[2,384,128]{2,1,0:T(8,128)(2,1)S(1)}, u32[]{:S(2)}, u32[]{:S(2)}) collective-permute-start(bf16[2,384,128]{2,1,0:T(8,128)(2,1)S(1)} %pad_maximum_fusion.1.refs_0_), channel_id=1, source_target_pairs={{96,0},{112,16},{0,32},{16,48},{32,64},{48,80},{64,96},{80,112},{2... | collective-permute-start | bytes 589832 | tf_op jit(solution)/shard_map/ppermute | solution.py:28
  232.5 15.3 %collective-permute-start.18 = (bf16[2,384,128]{2,1,0:T(8,128)(2,1)S(1)}, bf16[2,384,128]{2,1,0:T(8,128)(2,1)}, u32[]{:S(2)}, u32[]{:S(2)}) collective-permute-start(bf16[2,384,128]{2,1,0:T(8,128)(2,1)S(1)} %pad_maximum_fusion.1.refs_0_), channel_id=1, source_target_pairs={{112,0},{0,16},{16,32},{32,48},{48,64},{64,80},{80,96},{96,112},{2... | collective-permute-start | bytes 589832 | tf_op jit(solution)/shard_map/ppermute | solution.py:28
  280.9 18.9 %all-to-all-start.5 = ((bf16[16,128,128]{2,1,0:T(8,128)(2,1)}), bf16[16,128,128]{2,1,0:T(8,128)(2,1)S(1)}, u32[]{:S(2)}, u32[]{:S(2)}) async-start(bf16[16,128,128]{2,1,0:T(8,128)(2,1)} %folded.1), calls=%async_computation.5 | async-start | bytes 1048576 | tf_op jit(solution)/shard_map/all_to_all | solution.py:46
  (33 other events, 461.0 us)
Sparse Core Ops, SparseCore 0:
  9.8 69.6 all-gather.3
  81.3 39.7 all-gather.5
  179.9 67.7 reduce-scatter.1

commit v6 on v5

--- a/solution.py
+++ b/solution.py
@@ -42,6 +42,24 @@
     return lax.ppermute(value, "section", [(k, count - 1 - k) for k in range(count)])
 
 
+def upward(value, steps):
+    ring = lax.axis_size("section") // 2
+    pairs = []
+    for base in (0, ring):
+        pairs += [(base + z + steps, base + z) for z in range(ring - steps)]
+    return lax.ppermute(value, "section", pairs)
+
+
+def lower_only(value, steps):
+    ring = lax.axis_size("section") // 2
+    return lax.ppermute(value, "section", [((z + steps) % ring, z) for z in range(ring)])
+
+
+def between_chips(value, mask):
+    count = lax.axis_size("fsdp")
+    return lax.ppermute(value, "fsdp", [(f, f ^ (2 * mask)) for f in range(count)])
+
+
 def exchanged(parts, axis, groups=None):
     return lax.all_to_all(parts, axis, 0, 0, axis_index_groups=groups, tiled=True)
 
@@ -125,6 +143,39 @@
         out_specs=pl.BlockSpec((step, 2 * half, part), lambda b: (b, 0, 0)),
         name="laid_out",
     )(down, up)
+
+
+def stacked(pieces):
+    count = len(pieces)
+
+    def kernel(*refs):
+        for at in range(count):
+            refs[count][at] = refs[at][...]
+
+    return pl.pallas_call(
+        kernel,
+        out_shape=jax.ShapeDtypeStruct((count,) + pieces[0].shape, BF16),
+        in_specs=[vmem()] * count,
+        out_specs=vmem(),
+        name="stacked",
+    )(*pieces)
+
+
+def added(kept, received):
+    count = kept.shape[0]
+
+    def kernel(kept_ref, received_ref, *dests):
+        for at in range(count):
+            total = kept_ref[at].astype(F32) + received_ref[at].astype(F32)
+            dests[at][...] = total.astype(BF16)
+
+    return pl.pallas_call(
+        kernel,
+        out_shape=[jax.ShapeDtypeStruct(kept.shape[1:], BF16)] * count,
+        in_specs=[vmem(), vmem()],
+        out_specs=[vmem()] * count,
+        name="added",
+    )(kept, received)
 
 
 def folded(parts, copies, used):
@@ -239,22 +290,29 @@
     )(wide, coupled, in_t, far_in_t)
 
 
-def top_products(top, row_weight, head, out_full, place, step):
-    blocks, units, part = out_full.shape
+def chip_columns(rows, part, flip):
+    def index(m, spot):
+        core = 1 - spot[1] if flip else spot[1]
+        return (0, 2 * jnp.bitwise_xor(spot[0], m) + core)
+
+    return pl.BlockSpec((rows, part), index)
+
+
+def top_products(spot, top, row_weight, head, out_same, out_other, place):
+    chips, units, part = out_same.shape
     rows = top.shape[0]
 
-    def kernel(top_ref, weight_ref, head_ref, out_ref, place_ref, dest, acc):
+    def kernel(spot_ref, top0, top1, head0, head1, weight_ref, out0, out1, place_ref, dest, acc):
         at = pl.program_id(0)
 
         @pl.when(at == 0)
         def _():
             acc[...] = jnp.zeros_like(acc)
 
-        first = top_ref[...].astype(F32) + weight_ref[:, :1] * head_ref[...]
-        first = first.astype(BF16)
         total = acc[...]
-        for b in range(step):
-            total = total + dot(first[:, b * part : (b + 1) * part], out_ref[b], COLS_OF_BOTH)
+        for top_ref, head_ref, out_ref in ((top0, head0, out0), (top1, head1, out1)):
+            first = top_ref[...].astype(F32) + weight_ref[:, :1] * head_ref[...]
+            total = total + dot(first.astype(BF16), out_ref[0], COLS_OF_BOTH)
         acc[...] = total
 
         @pl.when(at == pl.num_programs(0) - 1)
@@ -265,51 +323,69 @@
 
     return pl.pallas_call(
         kernel,
-        grid=(blocks // step,),
+        grid_spec=pltpu.PrefetchScalarGridSpec(
+            num_scalar_prefetch=1,
+            grid=(chips,),
+            in_specs=[
+                chip_columns(rows, part, False),
+                chip_columns(rows, part, True),
+                chip_columns(1, part, False),
+                chip_columns(1, part, True),
+                pl.BlockSpec((rows, 128), lambda m, spot: (0, 0)),
+                pl.BlockSpec((1, units, part), lambda m, spot: (m, 0, 0)),
+                pl.BlockSpec((1, units, part), lambda m, spot: (m, 0, 0)),
+                pl.BlockSpec((rows, rows), lambda m, spot: (0, 0)),
+            ],
+            out_specs=pl.BlockSpec((rows, units), lambda m, spot: (0, 0)),
+            scratch_shapes=[pltpu.VMEM((rows, units), F32)],
+        ),
         out_shape=jax.ShapeDtypeStruct((rows, units), BF16),
-        in_specs=[
-            pl.BlockSpec((rows, step * part), lambda b: (0, b)),
-            pl.BlockSpec((rows, 128), lambda b: (0, 0)),
-            pl.BlockSpec((1, step * part), lambda b: (0, b)),
-            pl.BlockSpec((step, units, part), lambda b: (b, 0, 0)),
-            pl.BlockSpec((rows, rows), lambda b: (0, 0)),
-        ],
-        out_specs=pl.BlockSpec((rows, units), lambda b: (0, 0)),
-        scratch_shapes=[pltpu.VMEM((rows, units), F32)],
         name="top_products",
-    )(top, row_weight, head, out_full, place)
-
-
-def first_parts(top, row_weight, head, pre_down, pre_up, place, blocks, step):
+    )(spot, top, top, head, head, row_weight, out_same, out_other, place)
+
+
+def first_parts(spot, top, row_weight, head, pre_down, pre_up, place, chips):
     rows, width = top.shape
     half, units = pre_up.shape
-    part = width // blocks
-
-    def kernel(top_ref, weight_ref, head_ref, down_ref, up_ref, place_ref, dest):
-        value = jnp.concatenate([down_ref[:half], up_ref[...]], axis=0).astype(F32)
-        hidden = (value * jax.nn.sigmoid(value)).astype(BF16)
-        placed = dot(place_ref[...].astype(BF16), hidden).astype(BF16)
-        first = top_ref[...].astype(F32) + weight_ref[:, :1] * head_ref[...]
-        first = first.astype(BF16)
-        total = dot(placed, first, ROWS_OF_BOTH).astype(BF16)
-        for b in range(step):
-            dest[b] = total[:, b * part : (b + 1) * part]
-
-    return pl.pallas_call(
-        kernel,
-        grid=(blocks // step,),
-        out_shape=jax.ShapeDtypeStruct((blocks, units, part), BF16),
-        in_specs=[
-            pl.BlockSpec((rows, step * part), lambda b: (0, b)),
-            pl.BlockSpec((rows, 128), lambda b: (0, 0)),
-            pl.BlockSpec((1, step * part), lambda b: (0, b)),
-            pl.BlockSpec((2 * rows, units), lambda b: (0, 0)),
-            pl.BlockSpec((half, units), lambda b: (0, 0)),
-            pl.BlockSpec((rows, rows), lambda b: (0, 0)),
-        ],
-        out_specs=pl.BlockSpec((step, units, part), lambda b: (b, 0, 0)),
+    part = width // (2 * chips)
+
+    def kernel(
+        spot_ref, top0, top1, head0, head1, weight_ref, down_ref, up_ref, place_ref, kept, sent, at
+    ):
+        @pl.when(pl.program_id(0) == 0)
+        def _():
+            value = jnp.concatenate([down_ref[:half], up_ref[...]], axis=0).astype(F32)
+            hidden = (value * jax.nn.sigmoid(value)).astype(BF16)
+            at[...] = dot(place_ref[...].astype(BF16), hidden).astype(BF16)
+
+        for top_ref, head_ref, dest in ((top0, head0, kept), (top1, head1, sent)):
+            first = top_ref[...].astype(F32) + weight_ref[:, :1] * head_ref[...]
+            dest[0] = dot(at[...], first.astype(BF16), ROWS_OF_BOTH).astype(BF16)
+
+    return pl.pallas_call(
+        kernel,
+        grid_spec=pltpu.PrefetchScalarGridSpec(
+            num_scalar_prefetch=1,
+            grid=(chips,),
+            in_specs=[
+                chip_columns(rows, part, False),
+                chip_columns(rows, part, True),
+                chip_columns(1, part, False),
+                chip_columns(1, part, True),
+                pl.BlockSpec((rows, 128), lambda m, spot: (0, 0)),
+                pl.BlockSpec((2 * rows, units), lambda m, spot: (0, 0)),
+                pl.BlockSpec((half, units), lambda m, spot: (0, 0)),
+                pl.BlockSpec((rows, rows), lambda m, spot: (0, 0)),
+            ],
+            out_specs=[
+                pl.BlockSpec((1, units, part), lambda m, spot: (m, 0, 0)),
+                pl.BlockSpec((1, units, part), lambda m, spot: (m, 0, 0)),
+            ],
+            scratch_shapes=[pltpu.VMEM((rows, units), BF16)],
+        ),
+        out_shape=[jax.ShapeDtypeStruct((chips, units, part), BF16)] * 2,
         name="first_parts",
-    )(top, row_weight, head, pre_down, pre_up, place)
+    )(spot, top, top, head, head, row_weight, pre_down, pre_up, place)
 
 
 def held_at(upper, lower, count):
@@ -434,33 +510,41 @@
     )(wide, shared)
 
 
-def output_grads(section, cross, first, weights):
+def output_grads(section, cross, firsts, inner, outer):
     count, units, _ = cross.shape
-    part = first.shape[1]
+    part = firsts[0].shape[1]
     ring = count // 2
-
-    def kernel(section_ref, cross_ref, first_ref, weights_ref, dest):
+    terms = len(firsts)
+
+    def kernel(section_ref, cross_ref, *refs):
+        dest = refs[-1]
         own = section_ref[0]
         upper = own >= ring
         place = jnp.where(upper, own - ring, own)
-        dest[...] = first_ref[...].astype(F32)
-        for z in range(ring):
-
-            @pl.when(z > place)
+        total = refs[0][...].astype(F32)
+        for at in range(1, terms):
+            total = total + refs[at][...].astype(F32)
+        dest[...] = total
+        for steps in range(1, ring):
+
+            @pl.when(place + steps < ring)
             def _():
-                dest[...] += dot(cross_ref[z - place], weights_ref[z, 0])
+                dest[...] += dot(cross_ref[steps], refs[terms + steps - 1][...])
+
+        for steps in range(ring):
 
             @pl.when(jnp.logical_not(upper))
             def _():
-                dest[...] += dot(cross_ref[jnp.minimum(ring + z - place, count - 1)], weights_ref[z, 1])
+                at = ring + lax.rem(place + steps, ring) - place
+                dest[...] += dot(cross_ref[at], refs[terms + ring - 1 + steps][...])
 
     return pl.pallas_call(
         kernel,
         out_shape=jax.ShapeDtypeStruct((units, part), F32),
-        in_specs=[smem()] + [vmem()] * 3,
+        in_specs=[smem()] + [vmem()] * (1 + terms + len(inner) + len(outer)),
         out_specs=vmem(),
         name="output_grads",
-    )(section, cross, first, weights)
+    )(section, cross, *firsts, *inner, *outer)
 
 
 def on_device(
@@ -481,7 +565,6 @@
     section = section_idx.astype(jnp.int32).reshape(1)
     _, micro, row_count, width = down_inputs.shape
     units = branch_in.shape[2]
-    part = width // blocks
     half = micro * row_count
     rows = 2 * half
     step = 4
@@ -493,7 +576,6 @@
     out_t = branch_out[0]
     down = down_inputs[0].reshape(half, width)
     up = up_inputs[0].reshape(half, width)
-    out_full = lax.all_gather(out_t, "fsdp", axis=0)
     wide = exchanged(laid_out(down, up, blocks, step), "fsdp")
     ring = count // 2
     place_idx = section_idx % ring
@@ -515,12 +597,25 @@
     far_in_t = mirrored(in_t)
     for slot in range(ring // 2):
         outer.append(across(partner, slot))
-    weights = lax.all_gather(
-        jnp.stack([in_t, partner]),
-        "section",
-        axis=0,
-        axis_index_groups=[list(range(ring)), list(range(ring, count))],
-    )
+    chips = blocks // 2
+    spot = jnp.stack([fsdp_idx // 2, fsdp_idx % 2]).astype(jnp.int32)
+    pieces = [out_t]
+    for mask in range(1, chips):
+        pieces.append(between_chips(out_t, mask))
+    out_same = stacked(pieces)
+    out_other = from_other_core(out_same)
+    inner_all = list(inner)
+    for steps in range(ring // 2 + 1, ring):
+        inner_all.append(upward(in_t, steps))
+    outer_all = []
+    for steps in range(ring):
+        held = [slot for slot in range(ring // 2) if LOWER_OFFSETS[slot] % ring == steps]
+        if steps == 0:
+            outer_all.append(partner)
+        elif held:
+            outer_all.append(outer[held[0]])
+        else:
+            outer_all.append(lower_only(partner, steps))
 
     coupled = couplings(section, in_t, out_t, partner, inner, outer, count)
     coupled = coupled.reshape(blocks, -1, units)
@@ -532,7 +627,7 @@
     head = reward_head.reshape(1, width)
     parts = pre_parts(wide, coupled, in_t, far_in_t, step)
     parts = exchanged(parts, "fsdp")
-    reached = top_products(top, row_weight, head, out_full, place, step)
+    reached = top_products(spot, top, row_weight, head, out_same, out_other, place)
     coupled, known, far_pre = folded_with(parts, reached, count, lead)
     coupled = exchanged(coupled, "section")
     mirror_pre = mirrored(far_pre)
@@ -540,10 +635,12 @@
     held = [jnp.stack([known, known_partner])]
     for steps in range(1, ring):
         held.append(inside_half(held[0], steps, ring))
-    firsts = first_parts(top, row_weight, head, known, mirror_pre, place, blocks, step)
-    first = lax.psum_scatter(
-        firsts.reshape(blocks * units, part), "fsdp", scatter_dimension=0, tiled=True
-    )
+    kept, sent = first_parts(spot, top, row_weight, head, known, mirror_pre, place, chips)
+    received = from_other_core(sent)
+    merged = added(kept, received)
+    firsts = [merged[0]]
+    for mask in range(1, chips):
+        firsts.append(between_chips(merged[mask], mask))
     coupled_same = exchanged(
         jnp.broadcast_to(coupled[None], (blocks // 2,) + coupled.shape), "fsdp", groups
     )
@@ -551,11 +648,12 @@
 
     shared = chain(section, core, held, coupled_same, coupled_other, count)
     shared = exchanged(shared, "fsdp")
+    shared, *firsts[1:6] = lax.optimization_barrier((shared, *firsts[1:6]))
     far_in = input_grads(wide, shared, step, 1, BF16)
     back_in = mirrored(far_in)
     cross = exchanged(folded(shared, blocks, units), "fsdp")
     own_in = input_grads(wide, shared, step, 0, F32)
-    grad_out = output_grads(section, cross, first, weights)
+    grad_out = output_grads(section, cross, firsts, inner_all, outer_all)
     grad_in = (own_in + back_in.astype(F32)).T
     return (grad_in[None], grad_out[None])
 

time: 317 us -> 334 us (1.054)
  starting transfers between devices: 99.3 us -> 131 us
  waiting for transfers between devices: 99.9 us -> 75.7 us
  between operations: 14 us -> 1.3 us
  Pallas kernels: 48.1 us -> 59.6 us
  blocking collectives: 37.9 us -> 48.5 us
    ppermute x0 -> x21, starting transfers between devices: none -> 44.9 us  [the longest x14 38.4 us: between_chips(): lax.ppermute(value, 'fsdp', [(f, f ^ 2 * mask) for f in range(count)])]
    all_to_all x4, waiting for transfers between devices: 22.2 us -> 4.36 us  [exchanged(): lax.all_to_all(parts, axis, 0, 0, axis_index_groups=groups, tiled=True)]
    ppermute x0 -> x21, waiting for transfers between devices: none -> 16 us  [the longest x14 12.1 us: between_chips(): lax.ppermute(value, 'fsdp', [(f, f ^ 2 * mask) for f in range(count)])]
    all_to_all x4, starting transfers between devices: 31.6 us -> 16.6 us  [exchanged(): lax.all_to_all(parts, axis, 0, 0, axis_index_groups=groups, tiled=True)]
    pallas_call x2 -> x4, Pallas kernels: 10.1 us -> 21.4 us  [the longest x1 8.25 us: first_parts(): pl.pallas_call(kernel, grid_spec=pltpu.PrefetchScalarGridSpec(num_scalar_...]
    all_to_all x2, blocking collectives: 37.9 us -> 48.5 us  [exchanged(): lax.all_to_all(parts, axis, 0, 0, axis_index_groups=groups, tiled=True)]
    ppermute x3, waiting for transfers between devices: 18.1 us -> 7.72 us  [mirrored(): lax.ppermute(value, 'section', [(k, count - 1 - k) for k in range(count)])]
    ppermute x1, waiting for transfers between devices: 30.5 us -> 20.2 us  [on_device(): lax.ppermute(jnp.where(section_idx >= ring, in_t, out_t), 'section', [(k,...]
  transfers between devices with their start and end apart: 28 -> 48, of which waited for: 14 -> 19; matrix products, arithmetic and copies ran while one was open for 2% -> 1% of each run, Pallas kernels for 14% -> 12%
where the time goes in v6:
time: 334 us; the launch traced here: 328 us
  starting transfers between devices  131 us (39%)
  waiting for transfers between devices  75.7 us (23%)
  Pallas kernels  59.6 us (18%)
  blocking collectives  48.5 us (15%)
  local copies, waits for them, and re-layouts  10.2 us (3%)
    all_to_all x2, blocking collectives, exchanged(): lax.all_to_all(parts, axis, 0, 0, axis_index_groups=groups, tiled=True)  48.5 us
    ppermute x11, starting transfers between devices, inside_half(): return lax.ppermute(value, 'section', pairs)  39.5 us
    ppermute x14, starting transfers between devices, between_chips(): lax.ppermute(value, 'fsdp', [(f, f ^ 2 * mask) for f in range(count)])  38.4 us
    ppermute x1, waiting for transfers between devices, on_device(): lax.ppermute(jnp.where(section_idx >= ring, in_t, out_t), 'section', [(k,...  20.2 us
    all_to_all x4, starting transfers between devices, exchanged(): lax.all_to_all(parts, axis, 0, 0, axis_index_groups=groups, tiled=True)  16.6 us
    ppermute x11, waiting for transfers between devices, inside_half(): return lax.ppermute(value, 'section', pairs)  14 us
    ppermute x4, starting transfers between devices, across(): return lax.ppermute(value, 'section', pairs)  13.9 us
    ppermute x3, starting transfers between devices, mirrored(): lax.ppermute(value, 'section', [(k, count - 1 - k) for k in range(count)])  13.1 us
  transfers between devices with their start and end apart: 48, of which 19 were waited for; matrix products, arithmetic and copies ran while one was open for 1% of the time, Pallas kernels for 12%

profile of v6, /device:TPU:16, one launch (start us, length us, event | category | flops | bytes accessed | tf_op | source)
XLA Modules:
  0.0 328.2 jit_solution(3163337688219004238)
XLA Ops:
  0.6 4.2 %laid_out.1 = bf16[16,192,512]{2,1,0:T(8,128)(2,1)} custom-call(bf16[96,8192]{1,0:T(8,128)(2,1)} %bitcast.40, bf16[96,8192]{1,0:T(8,128)(2,1)} %bitcast.41), custom_call_target="tpu_custom_call" | custom-call | tf_op jit(solution)/shard_map/laid_out/pallas_call | solution.py:138
  4.8 5.3 %all-to-all-start = ((bf16[16,192,512]{2,1,0:T(8,128)(2,1)}), bf16[16,192,512]{2,1,0:T(8,128)(2,1)S(1)}, u32[]{:S(2)}, u32[]{:S(2)}) async-start(bf16[16,192,512]{2,1,0:T(8,128)(2,1)} %laid_out.1), calls=%async_computation | async-start | bytes 6291456 | tf_op jit(solution)/shard_map/all_to_all | solution.py:64
  11.0 5.8 %collective-permute-start.1 = (bf16[128,512]{1,0:T(8,128)(2,1)S(1)}, bf16[128,512]{1,0:T(8,128)(2,1)S(1)}, u32[]{:S(2)}, u32[]{:S(2)}) collective-permute-start(bf16[128,512]{1,0:T(8,128)(2,1)S(1)} %get-tuple-element.48), channel_id=1, source_target_pairs={{16,0},{32,16},{48,32},{64,48},{80,64},{96,80},{112,96},{0,112},{1... | collective-permute-start | bytes 393224 | tf_op jit(solution)/shard_map/ppermute | solution.py:28
  20.1 20.2 %collective-permute-done.partner_ref.refs_15_ = bf16[128,512]{1,0:T(8,128)(2,1)S(1)} collective-permute-done((bf16[128,512]{1,0:T(8,128)(2,1)S(1)}, bf16[128,512]{1,0:T(8,128)(2,1)S(1)}, u32[]{:S(2)}, u32[]{:S(2)}) %collective-permute-start) | collective-permute-done | bytes 131104 | tf_op jit(solution)/shard_map/ppermute | solution.py:582
  40.2 10.7 %collective-permute-start.10 = (bf16[128,512]{1,0:T(8,128)(2,1)S(1)}, bf16[128,512]{1,0:T(8,128)(2,1)S(1)}, u32[]{:S(2)}, u32[]{:S(2)}) collective-permute-start(bf16[128,512]{1,0:T(8,128)(2,1)S(1)} %bitcast.44), channel_id=1, source_target_pairs={{0,2},{1,3},{2,0},{3,1},{4,6},{5,7},{6,4},{7,5},{8,10},{9,11},{10,... | collective-permute-start | bytes 393224 | tf_op jit(solution)/shard_map/ppermute | solution.py:60
  70.0 4.0 %collective-permute-start.7 = (bf16[128,512]{1,0:T(8,128)(2,1)S(1)}, bf16[128,512]{1,0:T(8,128)(2,1)}, u32[]{:S(2)}, u32[]{:S(2)}) collective-permute-start(bf16[128,512]{1,0:T(8,128)(2,1)S(1)} %collective-permute-done.partner_ref.refs_15_), channel_id=1, source_target_pairs={{208,128},{224,144},{240,160},{128,176},{144,192},{160,208},{176,2... | collective-permute-start | bytes 393224 | tf_op jit(solution)/shard_map/ppermute | solution.py:37
  94.7 4.7 %pre_parts.1 = bf16[16,256,128]{2,1,0:T(8,128)(2,1)} custom-call(bf16[16,192,512]{2,1,0:T(8,128)(2,1)} %copy-done, bf16[16,64,128]{2,1,0:T(8,128)(2,1)} %bitcast.51, bf16[128,512]{1,0:T(8,128)(2,1)} %bitcast.36, bf16[128,512]{1,0:T(8,128)(2,1)} %copy-done.45), custom_call_target="tpu_custom_call" | custom-call | tf_op jit(solution)/shard_map/pre_parts/pallas_call | solution.py:278
  99.5 4.0 %all-to-all-start.1 = ((bf16[16,256,128]{2,1,0:T(8,128)(2,1)}), bf16[16,256,128]{2,1,0:T(8,128)(2,1)S(1)}, u32[]{:S(2)}, u32[]{:S(2)}) async-start(bf16[16,256,128]{2,1,0:T(8,128)(2,1)} %pre_parts.1), calls=%async_computation.1 | async-start | bytes 2097152 | tf_op jit(solution)/shard_map/all_to_all | solution.py:64
  107.3 8.2 %top_products.1.below_ref = bf16[192,128]{1,0:T(8,128)(2,1)} custom-call(s32[2]{0:T(128)} %pad_add_fusion.spot_ref, bf16[192,8192]{1,0:T(8,128)(2,1)} %bitcast.30, bf16[192,8192]{1,0:T(8,128)(2,1)} %bitcast.31, f32[1,8192]{1,0:T(1,128)} %bitcast.52, f32[1,8192]{1,0:T(1,128)} %bitcast.53, f32[192,128]{1,0:T(8,128)} %get-tuple-element.23.weight_ref, ...), custom_call_target="tpu_custom_call" | custom-call | tf_op jit(solution)/shard_map/top_products/pallas_call | solution.py:324
  115.5 4.4 %all-to-all-done.1.parts_ref = bf16[16,256,128]{2,1,0:T(8,128)(2,1)S(1)} async-done(((bf16[16,256,128]{2,1,0:T(8,128)(2,1)}), bf16[16,256,128]{2,1,0:T(8,128)(2,1)S(1)}, u32[]{:S(2)}, u32[]{:S(2)}) %all-to-all-start.1) | async-done | bytes 1048608 | tf_op jit(solution)/shard_map/all_to_all | solution.py:64
  123.0 20.2 %all_to_all.30 = bf16[16,64,128]{2,1,0:T(8,128)(2,1)S(1)} all-to-all(bf16[16,64,128]{2,1,0:T(8,128)(2,1)} %get-tuple-element.25), channel_id=1, replica_groups=mesh['section'=16,'fsdp'=16] {'section'}, dimensions={0} | all-to-all | bytes 524288 | tf_op jit(solution)/shard_map/all_to_all | solution.py:64
  143.7 28.3 %all_to_all.31.same_ref = bf16[8,16,64,128]{3,2,1,0:T(8,128)(2,1)S(1)} all-to-all(bf16[8,16,64,128]{3,2,1,0:T(8,128)(2,1)S(1)} %broadcast_in_dim.12), channel_id=1, replica_groups={{0,2,4,6,8,10,12,14},{1,3,5,7,9,11,13,15},{16,18,20,22,24,26,28,30},{17..., dimensions={0} | all-to-all | bytes 4194304 | tf_op jit(solution)/shard_map/all_to_all | solution.py:64
  174.4 4.2 %collective-permute-done.19 = bf16[384,128]{1,0:T(8,128)(2,1)S(1)} collective-permute-done((bf16[384,128]{1,0:T(8,128)(2,1)S(1)}, bf16[384,128]{1,0:T(8,128)(2,1)S(1)}, u32[]{:S(2)}, u32[]{:S(2)}) %collective-permute-start.19) | collective-permute-done | bytes 98336 | tf_op jit(solution)/shard_map/ppermute | solution.py:634
  188.9 6.0 %collective-permute-start.24 = (bf16[2,384,128]{2,1,0:T(8,128)(2,1)S(1)}, bf16[2,384,128]{2,1,0:T(8,128)(2,1)S(1)}, u32[]{:S(2)}, u32[]{:S(2)}) collective-permute-start(bf16[2,384,128]{2,1,0:T(8,128)(2,1)S(1)} %pad_maximum_fusion.refs_0_), channel_id=1, source_target_pairs={{80,0},{96,16},{112,32},{0,48},{16,64},{32,80},{48,96},{64,112},{2... | collective-permute-start | bytes 589832 | tf_op jit(solution)/shard_map/ppermute | solution.py:28
  195.0 8.3 %collective-permute-done.21.refs_2_ = bf16[2,384,128]{2,1,0:T(8,128)(2,1)S(1)} collective-permute-done((bf16[2,384,128]{2,1,0:T(8,128)(2,1)S(1)}, bf16[2,384,128]{2,1,0:T(8,128)(2,1)S(1)}, u32[]{:S(2)}, u32[]{:S(2)}) %collective-permute-start.21) | collective-permute-done | bytes 196640 | tf_op jit(solution)/shard_map/ppermute | solution.py:28
  208.5 11.4 %collective-permute-start.26 = (bf16[2,384,128]{2,1,0:T(8,128)(2,1)S(1)}, bf16[2,384,128]{2,1,0:T(8,128)(2,1)S(1)}, u32[]{:S(2)}, u32[]{:S(2)}) collective-permute-start(bf16[2,384,128]{2,1,0:T(8,128)(2,1)S(1)} %pad_maximum_fusion.refs_0_), channel_id=1, source_target_pairs={{112,0},{0,16},{16,32},{32,48},{48,64},{64,80},{80,96},{96,112},{2... | collective-permute-start | bytes 589832 | tf_op jit(solution)/shard_map/ppermute | solution.py:28
  223.9 7.4 %chain.1 = bf16[16,320,128]{2,1,0:T(8,128)(2,1)} custom-call(s32[1]{0:T(128)} %bitcast.2.section_ref, s32[1]{0:T(128)} %bitcast.3.core_ref, bf16[8,16,64,128]{3,2,1,0:T(8,128)(2,1)} %copy-done.2, bf16[8,16,64,128]{3,2,1,0:T(8,128)(2,1)} %collective-permute-done.18.other_ref, bf16[2,384,128]{2,1,0:T(8,128)(2,1)} %copy-done.9, ...), custom_call_target="tpu_custom_call" | custom-call | tf_op jit(solution)/shard_map/chain/pallas_call | solution.py:464
  236.6 6.3 %collective-permute-done.27.up_ref = bf16[96,128]{1,0:T(8,128)(2,1)S(1)} collective-permute-done((bf16[96,128]{1,0:T(8,128)(2,1)S(1)}, bf16[96,128]{1,0:T(8,128)(2,1)S(1)}, u32[]{:S(2)}, u32[]{:S(2)}) %collective-permute-start.27) | collective-permute-done | bytes 24608 | tf_op jit(solution)/shard_map/ppermute | solution.py:42
  243.5 8.3 %first_parts.1 = (bf16[8,128,512]{2,1,0:T(8,128)(2,1)}, bf16[8,128,512]{2,1,0:T(8,128)(2,1)}) custom-call(s32[2]{0:T(128)} %pad_add_fusion.spot_ref, bf16[192,8192]{1,0:T(8,128)(2,1)} %bitcast.32, bf16[192,8192]{1,0:T(8,128)(2,1)} %bitcast.33, f32[1,8192]{1,0:T(1,128)} %bitcast.54, f32[1,8192]{1,0:T(1,128)} %bitcast.55, ...), custom_call_target="tpu_custom_call" | custom-call | tf_op jit(solution)/shard_map/first_parts/pallas_call | solution.py:365
  269.2 5.2 %collective-permute-done.32.refs_4_ = bf16[128,512]{1,0:T(8,128)(2,1)S(1)} collective-permute-done((bf16[128,512]{1,0:T(8,128)(2,1)}, bf16[128,512]{1,0:T(8,128)(2,1)S(1)}, u32[]{:S(2)}, u32[]{:S(2)}) %collective-permute-start.32) | collective-permute-done | bytes 131104 | tf_op jit(solution)/shard_map/ppermute | solution.py:60
  292.5 9.7 %collective-permute-start.34 = (bf16[128,512]{1,0:T(8,128)(2,1)}, bf16[128,512]{1,0:T(8,128)(2,1)S(1)}, u32[]{:S(2)}, u32[]{:S(2)}) collective-permute-start(bf16[128,512]{1,0:T(8,128)(2,1)} %shard_map.105), channel_id=1, source_target_pairs={{0,240},{16,224},{32,208},{48,192},{64,176},{80,160},{96,144},{112... | collective-permute-start | bytes 393224 | tf_op jit(solution)/shard_map/ppermute | solution.py:42
  302.2 4.0 %shard_map.104 = f32[128,512]{1,0:T(8,128)} custom-call(bf16[16,192,512]{2,1,0:T(8,128)(2,1)} %copy-done, bf16[16,320,128]{2,1,0:T(8,128)(2,1)} %copy-done.1), custom_call_target="tpu_custom_call" | custom-call | tf_op jit(solution)/shard_map/pallas_call | solution.py:500
  315.2 4.4 %collective-permute-start.36 = (bf16[128,512]{1,0:T(8,128)(2,1)S(1)}, bf16[128,512]{1,0:T(8,128)(2,1)S(1)}, u32[]{:S(2)}, u32[]{:S(2)}) collective-permute-start(bf16[128,512]{1,0:T(8,128)(2,1)S(1)} %copy-done.50), channel_id=1, source_target_pairs={{0,14},{1,15},{2,12},{3,13},{4,10},{5,11},{6,8},{7,9},{8,6},{9,7},... | collective-permute-start | bytes 393224 | tf_op jit(solution)/shard_map/ppermute | solution.py:60
  324.2 4.1 %output_grads.1 = f32[128,512]{1,0:T(8,128)} custom-call(s32[1]{0:T(128)} %bitcast.2.section_ref, bf16[16,128,128]{2,1,0:T(8,128)(2,1)} %copy-done.6, bf16[128,512]{1,0:T(8,128)(2,1)} %get-tuple-element.36.refs_0_, bf16[128,512]{1,0:T(8,128)(2,1)} %copy-done.24, bf16[128,512]{1,0:T(8,128)(2,1)} %copy-done.25, bf16[128,512]{1,0:T(8,128)(2,1)} %copy-done.26, ...), custom_call_target="tpu_custom_call" | custom-call | tf_op jit(solution)/shard_map/output_grads/pallas_call | solution.py:541
  (203 shorter events, 127.8 us)
Async XLA Ops:
  4.8 88.3 %all-to-all-start = ((bf16[16,192,512]{2,1,0:T(8,128)(2,1)}), bf16[16,192,512]{2,1,0:T(8,128)(2,1)S(1)}, u32[]{:S(2)}, u32[]{:S(2)}) async-start(bf16[16,192,512]{2,1,0:T(8,128)(2,1)} %laid_out.1), calls=%async_computation | async-start | bytes 6291456 | tf_op jit(solution)/shard_map/all_to_all | solution.py:64
  10.3 29.9 %collective-permute-start = (bf16[128,512]{1,0:T(8,128)(2,1)S(1)}, bf16[128,512]{1,0:T(8,128)(2,1)S(1)}, u32[]{:S(2)}, u32[]{:S(2)}) collective-permute-start(bf16[128,512]{1,0:T(8,128)(2,1)S(1)} %get-tuple-element.47), channel_id=1, source_target_pairs={{0,128},{16,144},{32,160},{48,176},{64,192},{80,208},{96,224},{112... | collective-permute-start | bytes 393224 | tf_op jit(solution)/shard_map/ppermute | solution.py:582
  11.0 39.9 %collective-permute-start.1 = (bf16[128,512]{1,0:T(8,128)(2,1)S(1)}, bf16[128,512]{1,0:T(8,128)(2,1)S(1)}, u32[]{:S(2)}, u32[]{:S(2)}) collective-permute-start(bf16[128,512]{1,0:T(8,128)(2,1)S(1)} %get-tuple-element.48), channel_id=1, source_target_pairs={{16,0},{32,16},{48,32},{64,48},{80,64},{96,80},{112,96},{0,112},{1... | collective-permute-start | bytes 393224 | tf_op jit(solution)/shard_map/ppermute | solution.py:28
  16.9 35.5 %collective-permute-start.2 = (bf16[128,512]{1,0:T(8,128)(2,1)S(1)}, bf16[128,512]{1,0:T(8,128)(2,1)S(1)}, u32[]{:S(2)}, u32[]{:S(2)}) collective-permute-start(bf16[128,512]{1,0:T(8,128)(2,1)S(1)} %get-tuple-element.49), channel_id=1, source_target_pairs={{32,0},{48,16},{64,32},{80,48},{96,64},{112,80},{0,96},{16,112},{1... | collective-permute-start | bytes 393224 | tf_op jit(solution)/shard_map/ppermute | solution.py:28
  18.3 34.2 %collective-permute-start.3 = (bf16[128,512]{1,0:T(8,128)(2,1)S(1)}, bf16[128,512]{1,0:T(8,128)(2,1)S(1)}, u32[]{:S(2)}, u32[]{:S(2)}) collective-permute-start(bf16[128,512]{1,0:T(8,128)(2,1)S(1)} %get-tuple-element.50), channel_id=1, source_target_pairs={{48,0},{64,16},{80,32},{96,48},{112,64},{0,80},{16,96},{32,112},{1... | collective-permute-start | bytes 393224 | tf_op jit(solution)/shard_map/ppermute | solution.py:28
  18.8 36.7 %collective-permute-start.4 = (bf16[128,512]{1,0:T(8,128)(2,1)S(1)}, bf16[128,512]{1,0:T(8,128)(2,1)S(1)}, u32[]{:S(2)}, u32[]{:S(2)}) collective-permute-start(bf16[128,512]{1,0:T(8,128)(2,1)S(1)} %get-tuple-element.46), channel_id=1, source_target_pairs={{64,0},{80,16},{96,32},{112,48},{192,128},{208,144},{224,160},{240... | collective-permute-start | bytes 393224 | tf_op jit(solution)/shard_map/ppermute | solution.py:28
  62.8 18.8 %collective-permute-start.5 = (bf16[128,512]{1,0:T(8,128)(2,1)S(1)}, bf16[128,512]{1,0:T(8,128)(2,1)}, u32[]{:S(2)}, u32[]{:S(2)}) collective-permute-start(bf16[128,512]{1,0:T(8,128)(2,1)S(1)} %collective-permute-done.partner_ref.refs_15_), channel_id=1, source_target_pairs={{240,128},{128,144},{144,160},{160,176},{176,192},{192,208},{208,2... | collective-permute-start | bytes 393224 | tf_op jit(solution)/shard_map/ppermute | solution.py:37
  66.6 17.6 %collective-permute-start.6 = (bf16[128,512]{1,0:T(8,128)(2,1)S(1)}, bf16[128,512]{1,0:T(8,128)(2,1)}, u32[]{:S(2)}, u32[]{:S(2)}) collective-permute-start(bf16[128,512]{1,0:T(8,128)(2,1)S(1)} %collective-permute-done.partner_ref.refs_15_), channel_id=1, source_target_pairs={{224,128},{240,144},{128,160},{144,176},{160,192},{176,208},{192,2... | collective-permute-start | bytes 393224 | tf_op jit(solution)/shard_map/ppermute | solution.py:37
  70.0 18.0 %collective-permute-start.7 = (bf16[128,512]{1,0:T(8,128)(2,1)S(1)}, bf16[128,512]{1,0:T(8,128)(2,1)}, u32[]{:S(2)}, u32[]{:S(2)}) collective-permute-start(bf16[128,512]{1,0:T(8,128)(2,1)S(1)} %collective-permute-done.partner_ref.refs_15_), channel_id=1, source_target_pairs={{208,128},{224,144},{240,160},{128,176},{144,192},{160,208},{176,2... | collective-permute-start | bytes 393224 | tf_op jit(solution)/shard_map/ppermute | solution.py:37
  81.6 25.7 %collective-permute-start.17 = (bf16[8,128,512]{2,1,0:T(8,128)(2,1)}, bf16[8,128,512]{2,1,0:T(8,128)(2,1)}, u32[]{:S(2)}, u32[]{:S(2)}) collective-permute-start(bf16[8,128,512]{2,1,0:T(8,128)(2,1)} %stacked.1.out0), channel_id=1, source_target_pairs={{0,1},{1,0},{2,3},{3,2},{4,5},{5,4},{6,7},{7,6},{8,9},{9,8},{10,11... | collective-permute-start | bytes 3145736 | tf_op jit(solution)/shard_map/ppermute | solution.py:73
  99.5 20.4 %all-to-all-start.1 = ((bf16[16,256,128]{2,1,0:T(8,128)(2,1)}), bf16[16,256,128]{2,1,0:T(8,128)(2,1)S(1)}, u32[]{:S(2)}, u32[]{:S(2)}) async-start(bf16[16,256,128]{2,1,0:T(8,128)(2,1)} %pre_parts.1), calls=%async_computation.1 | async-start | bytes 2097152 | tf_op jit(solution)/shard_map/all_to_all | solution.py:64
  171.9 51.9 %collective-permute-start.18 = (bf16[8,16,64,128]{3,2,1,0:T(8,128)(2,1)S(1)}, bf16[8,16,64,128]{3,2,1,0:T(8,128)(2,1)}, u32[]{:S(2)}, u32[]{:S(2)}) collective-permute-start(bf16[8,16,64,128]{3,2,1,0:T(8,128)(2,1)S(1)} %all_to_all.31.same_ref), channel_id=1, source_target_pairs={{0,1},{1,0},{2,3},{3,2},{4,5},{5,4},{6,7},{7,6},{8,9},{9,8},{10,11... | collective-permute-start | bytes 6291464 | tf_op jit(solution)/shard_map/ppermute | solution.py:73
  181.5 21.7 %collective-permute-start.21 = (bf16[2,384,128]{2,1,0:T(8,128)(2,1)S(1)}, bf16[2,384,128]{2,1,0:T(8,128)(2,1)S(1)}, u32[]{:S(2)}, u32[]{:S(2)}) collective-permute-start(bf16[2,384,128]{2,1,0:T(8,128)(2,1)S(1)} %pad_maximum_fusion.refs_0_), channel_id=1, source_target_pairs={{32,0},{48,16},{64,32},{80,48},{96,64},{112,80},{0,96},{16,112},{1... | collective-permute-start | bytes 589832 | tf_op jit(solution)/shard_map/ppermute | solution.py:28
  183.0 25.5 %collective-permute-start.22 = (bf16[2,384,128]{2,1,0:T(8,128)(2,1)S(1)}, bf16[2,384,128]{2,1,0:T(8,128)(2,1)S(1)}, u32[]{:S(2)}, u32[]{:S(2)}) collective-permute-start(bf16[2,384,128]{2,1,0:T(8,128)(2,1)S(1)} %pad_maximum_fusion.refs_0_), channel_id=1, source_target_pairs={{48,0},{64,16},{80,32},{96,48},{112,64},{0,80},{16,96},{32,112},{1... | collective-permute-start | bytes 589832 | tf_op jit(solution)/shard_map/ppermute | solution.py:28
  186.2 33.6 %collective-permute-start.23 = (bf16[2,384,128]{2,1,0:T(8,128)(2,1)S(1)}, bf16[2,384,128]{2,1,0:T(8,128)(2,1)S(1)}, u32[]{:S(2)}, u32[]{:S(2)}) collective-permute-start(bf16[2,384,128]{2,1,0:T(8,128)(2,1)S(1)} %pad_maximum_fusion.refs_0_), channel_id=1, source_target_pairs={{64,0},{80,16},{96,32},{112,48},{0,64},{16,80},{32,96},{48,112},{1... | collective-permute-start | bytes 589832 | tf_op jit(solution)/shard_map/ppermute | solution.py:28
  188.9 30.9 %collective-permute-start.24 = (bf16[2,384,128]{2,1,0:T(8,128)(2,1)S(1)}, bf16[2,384,128]{2,1,0:T(8,128)(2,1)S(1)}, u32[]{:S(2)}, u32[]{:S(2)}) collective-permute-start(bf16[2,384,128]{2,1,0:T(8,128)(2,1)S(1)} %pad_maximum_fusion.refs_0_), channel_id=1, source_target_pairs={{80,0},{96,16},{112,32},{0,48},{16,64},{32,80},{48,96},{64,112},{2... | collective-permute-start | bytes 589832 | tf_op jit(solution)/shard_map/ppermute | solution.py:28
  203.2 17.8 %collective-permute-start.25 = (bf16[2,384,128]{2,1,0:T(8,128)(2,1)S(1)}, bf16[2,384,128]{2,1,0:T(8,128)(2,1)S(1)}, u32[]{:S(2)}, u32[]{:S(2)}) collective-permute-start(bf16[2,384,128]{2,1,0:T(8,128)(2,1)S(1)} %pad_maximum_fusion.refs_0_), channel_id=1, source_target_pairs={{96,0},{112,16},{0,32},{16,48},{32,64},{48,80},{64,96},{80,112},{2... | collective-permute-start | bytes 589832 | tf_op jit(solution)/shard_map/ppermute | solution.py:28
  231.3 45.7 %all-to-all-start.4 = ((bf16[16,320,128]{2,1,0:T(8,128)(2,1)}), bf16[16,320,128]{2,1,0:T(8,128)(2,1)S(1)}, u32[]{:S(2)}, u32[]{:S(2)}) async-start(bf16[16,320,128]{2,1,0:T(8,128)(2,1)} %chain.1), calls=%async_computation.4 | async-start | bytes 2621440 | tf_op jit(solution)/shard_map/all_to_all | solution.py:64
  280.4 43.0 %all-to-all-start.5 = ((bf16[16,128,128]{2,1,0:T(8,128)(2,1)}), bf16[16,128,128]{2,1,0:T(8,128)(2,1)S(1)}, u32[]{:S(2)}, u32[]{:S(2)}) async-start(bf16[16,128,128]{2,1,0:T(8,128)(2,1)} %folded.1), calls=%async_computation.5 | async-start | bytes 1048576 | tf_op jit(solution)/shard_map/all_to_all | solution.py:64
  283.9 22.2 %collective-permute-start.37 = (bf16[128,512]{1,0:T(8,128)(2,1)S(1)}, bf16[128,512]{1,0:T(8,128)(2,1)S(1)}, u32[]{:S(2)}, u32[]{:S(2)}) collective-permute-start(bf16[128,512]{1,0:T(8,128)(2,1)S(1)} %bitcast.37), channel_id=1, source_target_pairs={{80,0},{96,16},{112,32},{208,128},{224,144},{240,160},{81,1},{97,1... | collective-permute-start | bytes 393224 | tf_op jit(solution)/shard_map/ppermute | solution.py:50
  285.2 21.6 %collective-permute-start.38 = (bf16[128,512]{1,0:T(8,128)(2,1)S(1)}, bf16[128,512]{1,0:T(8,128)(2,1)S(1)}, u32[]{:S(2)}, u32[]{:S(2)}) collective-permute-start(bf16[128,512]{1,0:T(8,128)(2,1)S(1)} %bitcast.38), channel_id=1, source_target_pairs={{96,0},{112,16},{224,128},{240,144},{97,1},{113,17},{225,129},{241... | collective-permute-start | bytes 393224 | tf_op jit(solution)/shard_map/ppermute | solution.py:50
  286.5 24.9 %collective-permute-start.39 = (bf16[128,512]{1,0:T(8,128)(2,1)S(1)}, bf16[128,512]{1,0:T(8,128)(2,1)S(1)}, u32[]{:S(2)}, u32[]{:S(2)}) collective-permute-start(bf16[128,512]{1,0:T(8,128)(2,1)S(1)} %bitcast.39), channel_id=1, source_target_pairs={{112,0},{240,128},{113,1},{241,129},{114,2},{242,130},{115,3},{243... | collective-permute-start | bytes 393224 | tf_op jit(solution)/shard_map/ppermute | solution.py:50
  287.9 24.3 %collective-permute-start.40 = (bf16[128,512]{1,0:T(8,128)(2,1)S(1)}, bf16[128,512]{1,0:T(8,128)(2,1)S(1)}, u32[]{:S(2)}, u32[]{:S(2)}) collective-permute-start(bf16[128,512]{1,0:T(8,128)(2,1)S(1)} %copy-done.11), channel_id=1, source_target_pairs={{16,0},{32,16},{48,32},{64,48},{80,64},{96,80},{112,96},{0,112},{1... | collective-permute-start | bytes 393224 | tf_op jit(solution)/shard_map/ppermute | solution.py:55
  292.5 22.7 %collective-permute-start.34 = (bf16[128,512]{1,0:T(8,128)(2,1)}, bf16[128,512]{1,0:T(8,128)(2,1)S(1)}, u32[]{:S(2)}, u32[]{:S(2)}) collective-permute-start(bf16[128,512]{1,0:T(8,128)(2,1)} %shard_map.105), channel_id=1, source_target_pairs={{0,240},{16,224},{32,208},{48,192},{64,176},{80,160},{96,144},{112... | collective-permute-start | bytes 393224 | tf_op jit(solution)/shard_map/ppermute | solution.py:42
  (77 other events, 1220.9 us)

commit v7 on v5

--- a/solution.py
+++ b/solution.py
@@ -131,18 +131,19 @@
     blocks, _, units = parts.shape
 
     def kernel(parts_ref, dest):
-        total = parts_ref[0, :used].astype(F32)
+        total = parts_ref[0].astype(F32)
         for b in range(1, blocks):
-            total = total + parts_ref[b, :used].astype(F32)
+            total = total + parts_ref[b].astype(F32)
         total = total.astype(BF16)
         for c in range(copies):
             dest[c] = total
 
     return pl.pallas_call(
         kernel,
+        grid=(1,),
         out_shape=jax.ShapeDtypeStruct((copies, used, units), BF16),
-        in_specs=[vmem()],
-        out_specs=vmem(),
+        in_specs=[pl.BlockSpec((blocks, used, units), lambda b: (0, 0, 0))],
+        out_specs=pl.BlockSpec((copies, used, units), lambda b: (0, 0, 0)),
         name="folded",
     )(parts)
 

time: 317 us -> 317 us (level)
  no operation moved by 1% of the time
where the time goes in v7:
time: 317 us; the launch traced here: 311 us
  waiting for transfers between devices  100 us (32%)
  starting transfers between devices  99.3 us (31%)
  Pallas kernels  47.9 us (15%)
  blocking collectives  37.9 us (12%)
  between operations  14 us (4%)
  local copies, waits for them, and re-layouts  8.91 us (3%)
    ppermute x11, starting transfers between devices, inside_half(): return lax.ppermute(value, 'section', pairs)  42.9 us
    all_to_all x2, blocking collectives, exchanged(): lax.all_to_all(parts, axis, 0, 0, axis_index_groups=groups, tiled=True)  37.9 us
    all_to_all x4, starting transfers between devices, exchanged(): lax.all_to_all(parts, axis, 0, 0, axis_index_groups=groups, tiled=True)  31.6 us
    ppermute x1, waiting for transfers between devices, on_device(): lax.ppermute(jnp.where(section_idx >= ring, in_t, out_t), 'section', [(k,...  30.5 us
    all_to_all x4, waiting for transfers between devices, exchanged(): lax.all_to_all(parts, axis, 0, 0, axis_index_groups=groups, tiled=True)  22.2 us
    ppermute x11, waiting for transfers between devices, inside_half(): return lax.ppermute(value, 'section', pairs)  19.8 us
    ppermute x3, waiting for transfers between devices, mirrored(): lax.ppermute(value, 'section', [(k, count - 1 - k) for k in range(count)])  18.1 us
    ppermute x4, starting transfers between devices, across(): return lax.ppermute(value, 'section', pairs)  11.3 us
  transfers between devices with their start and end apart: 28, of which 14 were waited for; matrix products, arithmetic and copies ran while one was open for 2% of the time, Pallas kernels for 14%

profile of v7, /device:TPU:16, one launch (start us, length us, event | category | flops | bytes accessed | tf_op | source)
XLA Modules:
  0.0 310.6 jit_solution(8767392758090070105)
XLA Ops:
  7.9 4.2 %laid_out.1 = bf16[16,192,512]{2,1,0:T(8,128)(2,1)} custom-call(bf16[96,8192]{1,0:T(8,128)(2,1)} %bitcast.42, bf16[96,8192]{1,0:T(8,128)(2,1)} %bitcast.43), custom_call_target="tpu_custom_call" | custom-call | tf_op jit(solution)/shard_map/laid_out/pallas_call | solution.py:120
  12.1 5.3 %all-to-all-start = ((bf16[16,192,512]{2,1,0:T(8,128)(2,1)}), bf16[16,192,512]{2,1,0:T(8,128)(2,1)S(1)}, u32[]{:S(2)}, u32[]{:S(2)}) async-start(bf16[16,192,512]{2,1,0:T(8,128)(2,1)} %laid_out.1), calls=%async_computation | async-start | bytes 6291456 | tf_op jit(solution)/shard_map/all_to_all | solution.py:46
  19.1 30.5 %collective-permute-done.partner_ref = bf16[128,512]{1,0:T(8,128)(2,1)S(1)} collective-permute-done((bf16[128,512]{1,0:T(8,128)(2,1)S(1)}, bf16[128,512]{1,0:T(8,128)(2,1)S(1)}, u32[]{:S(2)}, u32[]{:S(2)}) %collective-permute-start) | collective-permute-done | bytes 131104 | tf_op jit(solution)/shard_map/ppermute | solution.py:501
  50.3 9.0 %collective-permute-start.1 = (bf16[128,512]{1,0:T(8,128)(2,1)}, bf16[128,512]{1,0:T(8,128)(2,1)S(1)}, u32[]{:S(2)}, u32[]{:S(2)}) collective-permute-start(bf16[128,512]{1,0:T(8,128)(2,1)} %get-tuple-element.18), channel_id=1, source_target_pairs={{16,0},{32,16},{48,32},{64,48},{80,64},{96,80},{112,96},{0,112},{1... | collective-permute-start | bytes 393224 | tf_op jit(solution)/shard_map/ppermute | solution.py:28
  79.0 5.4 %collective-permute-start.9 = (bf16[128,512]{1,0:T(8,128)(2,1)S(1)}, bf16[128,512]{1,0:T(8,128)(2,1)S(1)}, u32[]{:S(2)}, u32[]{:S(2)}) collective-permute-start(bf16[128,512]{1,0:T(8,128)(2,1)S(1)} %bitcast.38), channel_id=1, source_target_pairs={{0,240},{16,224},{32,208},{48,192},{64,176},{80,160},{96,144},{112... | collective-permute-start | bytes 393224 | tf_op jit(solution)/shard_map/ppermute | solution.py:42
  91.3 8.0 %collective-permute-done.9.far_ref = bf16[128,512]{1,0:T(8,128)(2,1)S(1)} collective-permute-done((bf16[128,512]{1,0:T(8,128)(2,1)S(1)}, bf16[128,512]{1,0:T(8,128)(2,1)S(1)}, u32[]{:S(2)}, u32[]{:S(2)}) %collective-permute-start.9) | collective-permute-done | bytes 131104 | tf_op jit(solution)/shard_map/ppermute | solution.py:42
  101.0 4.8 %pre_parts.1 = bf16[16,256,128]{2,1,0:T(8,128)(2,1)} custom-call(bf16[16,192,512]{2,1,0:T(8,128)(2,1)} %copy-done, bf16[16,64,128]{2,1,0:T(8,128)(2,1)} %bitcast.45, bf16[128,512]{1,0:T(8,128)(2,1)} %bitcast.40, bf16[128,512]{1,0:T(8,128)(2,1)} %copy-done.22), custom_call_target="tpu_custom_call" | custom-call | tf_op jit(solution)/shard_map/pre_parts/pallas_call | solution.py:228
  105.8 18.9 %all-to-all-start.1 = ((bf16[16,256,128]{2,1,0:T(8,128)(2,1)}), bf16[16,256,128]{2,1,0:T(8,128)(2,1)S(1)}, u32[]{:S(2)}, u32[]{:S(2)}) async-start(bf16[16,256,128]{2,1,0:T(8,128)(2,1)} %pre_parts.1), calls=%async_computation.1 | async-start | bytes 2097152 | tf_op jit(solution)/shard_map/all_to_all | solution.py:46
  127.9 4.9 %top_products.1.below_ref = bf16[192,128]{1,0:T(8,128)(2,1)} custom-call(bf16[192,8192]{1,0:T(8,128)(2,1)} %bitcast.34, f32[192,128]{1,0:T(8,128)} %get-tuple-element.7.weight_ref, f32[1,8192]{1,0:T(1,128)} %bitcast.49, bf16[16,128,512]{2,1,0:T(8,128)(2,1)} %all-gather.4.cloned.1.call-done.out_ref, f32[192,192]{1,0:T(8,128)} %get-tuple-element.8.place_ref), custom_call_target="tpu_custom_call" | custom-call | tf_op jit(solution)/shard_map/top_products/pallas_call | solution.py:267
  132.8 8.3 %all-to-all-done.1.parts_ref = bf16[16,256,128]{2,1,0:T(8,128)(2,1)S(1)} async-done(((bf16[16,256,128]{2,1,0:T(8,128)(2,1)}), bf16[16,256,128]{2,1,0:T(8,128)(2,1)S(1)}, u32[]{:S(2)}, u32[]{:S(2)}) %all-to-all-start.1) | async-done | bytes 1048608 | tf_op jit(solution)/shard_map/all_to_all | solution.py:46
  144.2 14.6 %all_to_all.30 = bf16[16,64,128]{2,1,0:T(8,128)(2,1)S(1)} all-to-all(bf16[16,64,128]{2,1,0:T(8,128)(2,1)} %get-tuple-element.9), channel_id=1, replica_groups=mesh['section'=16,'fsdp'=16] {'section'}, dimensions={0} | all-to-all | bytes 524288 | tf_op jit(solution)/shard_map/all_to_all | solution.py:46
  164.7 4.3 %collective-permute-start.20 = (bf16[96,128]{1,0:T(8,128)(2,1)S(1)}, bf16[96,128]{1,0:T(8,128)(2,1)S(1)}, u32[]{:S(2)}, u32[]{:S(2)}) collective-permute-start(bf16[96,128]{1,0:T(8,128)(2,1)S(1)} %copy-done.28), channel_id=1, source_target_pairs={{0,240},{16,224},{32,208},{48,192},{64,176},{80,160},{96,144},{112... | collective-permute-start | bytes 73736 | tf_op jit(solution)/shard_map/ppermute | solution.py:42
  168.9 5.0 %collective-permute-done.20.up_ref = bf16[96,128]{1,0:T(8,128)(2,1)S(1)} collective-permute-done((bf16[96,128]{1,0:T(8,128)(2,1)S(1)}, bf16[96,128]{1,0:T(8,128)(2,1)S(1)}, u32[]{:S(2)}, u32[]{:S(2)}) %collective-permute-start.20) | collective-permute-done | bytes 24608 | tf_op jit(solution)/shard_map/ppermute | solution.py:42
  174.5 5.2 %first_parts.1 = bf16[16,128,512]{2,1,0:T(8,128)(2,1)} custom-call(bf16[192,8192]{1,0:T(8,128)(2,1)} %bitcast.35, f32[192,128]{1,0:T(8,128)} %get-tuple-element.7.weight_ref, f32[1,8192]{1,0:T(1,128)} %bitcast.50, bf16[384,128]{1,0:T(8,128)(2,1)} %get-tuple-element.10.down_ref, bf16[96,128]{1,0:T(8,128)(2,1)} %copy-done.25, ...), custom_call_target="tpu_custom_call" | custom-call | tf_op jit(solution)/shard_map/first_parts/pallas_call | solution.py:299
  179.7 13.9 %all-to-all-done.3.same_ref = bf16[8,16,64,128]{3,2,1,0:T(8,128)(2,1)S(1)} async-done(((bf16[8,16,64,128]{3,2,1,0:T(8,128)(2,1)}), bf16[8,16,64,128]{3,2,1,0:T(8,128)(2,1)S(1)}, u32[]{:S(2)}, u32[]{:S(2)}) %all-to-all-start.3) | async-done | bytes 2097184 | tf_op jit(solution)/shard_map/all_to_all | solution.py:46
  196.3 6.1 %collective-permute-done.11 = bf16[384,128]{1,0:T(8,128)(2,1)S(1)} collective-permute-done((bf16[384,128]{1,0:T(8,128)(2,1)S(1)}, bf16[384,128]{1,0:T(8,128)(2,1)S(1)}, u32[]{:S(2)}, u32[]{:S(2)}) %collective-permute-start.11) | collective-permute-done | bytes 98336 | tf_op jit(solution)/shard_map/ppermute | solution.py:540
  213.1 4.6 %collective-permute-start.16 = (bf16[2,384,128]{2,1,0:T(8,128)(2,1)S(1)}, bf16[2,384,128]{2,1,0:T(8,128)(2,1)S(1)}, u32[]{:S(2)}, u32[]{:S(2)}) collective-permute-start(bf16[2,384,128]{2,1,0:T(8,128)(2,1)S(1)} %pad_maximum_fusion.1.refs_0_), channel_id=1, source_target_pairs={{80,0},{96,16},{112,32},{0,48},{16,64},{32,80},{48,96},{64,112},{2... | collective-permute-start | bytes 589832 | tf_op jit(solution)/shard_map/ppermute | solution.py:28
  217.7 8.7 %collective-permute-done.13.refs_2_ = bf16[2,384,128]{2,1,0:T(8,128)(2,1)S(1)} collective-permute-done((bf16[2,384,128]{2,1,0:T(8,128)(2,1)S(1)}, bf16[2,384,128]{2,1,0:T(8,128)(2,1)S(1)}, u32[]{:S(2)}, u32[]{:S(2)}) %collective-permute-start.13) | collective-permute-done | bytes 196640 | tf_op jit(solution)/shard_map/ppermute | solution.py:28
  226.5 5.2 %collective-permute-start.17 = (bf16[2,384,128]{2,1,0:T(8,128)(2,1)S(1)}, bf16[2,384,128]{2,1,0:T(8,128)(2,1)S(1)}, u32[]{:S(2)}, u32[]{:S(2)}) collective-permute-start(bf16[2,384,128]{2,1,0:T(8,128)(2,1)S(1)} %pad_maximum_fusion.1.refs_0_), channel_id=1, source_target_pairs={{96,0},{112,16},{0,32},{16,48},{32,64},{48,80},{64,96},{80,112},{2... | collective-permute-start | bytes 589832 | tf_op jit(solution)/shard_map/ppermute | solution.py:28
  232.5 12.1 %collective-permute-start.18 = (bf16[2,384,128]{2,1,0:T(8,128)(2,1)S(1)}, bf16[2,384,128]{2,1,0:T(8,128)(2,1)}, u32[]{:S(2)}, u32[]{:S(2)}) collective-permute-start(bf16[2,384,128]{2,1,0:T(8,128)(2,1)S(1)} %pad_maximum_fusion.1.refs_0_), channel_id=1, source_target_pairs={{112,0},{0,16},{16,32},{32,48},{48,64},{64,80},{80,96},{96,112},{2... | collective-permute-start | bytes 589832 | tf_op jit(solution)/shard_map/ppermute | solution.py:28
  247.9 7.5 %chain.1 = bf16[16,320,128]{2,1,0:T(8,128)(2,1)} custom-call(s32[1]{0:T(128)} %bitcast.2.section_ref, s32[1]{0:T(128)} %bitcast.3.core_ref, bf16[8,16,64,128]{3,2,1,0:T(8,128)(2,1)} %copy-done.1, bf16[8,16,64,128]{3,2,1,0:T(8,128)(2,1)} %collective-permute-done.10.other_ref, bf16[2,384,128]{2,1,0:T(8,128)(2,1)} %copy-done.6, bf16[2,384,128]{2,1,0:T(8,128)(2,1)} %copy-done.9, ...), custom_call_target="tpu_custom_call" | custom-call | tf_op jit(solution)/shard_map/chain/pallas_call | solution.py:389
  255.3 23.3 %all_to_all.31.shared_ref.parts_ref = bf16[16,320,128]{2,1,0:T(8,128)(2,1)} all-to-all(bf16[16,320,128]{2,1,0:T(8,128)(2,1)} %chain.1), channel_id=1, replica_groups=mesh['section'=16,'fsdp'=16] {'fsdp'}, dimensions={0} | all-to-all | bytes 2621440 | tf_op jit(solution)/shard_map/all_to_all | solution.py:46
  288.5 4.0 %shard_map.104 = f32[128,512]{1,0:T(8,128)} custom-call(bf16[16,192,512]{2,1,0:T(8,128)(2,1)} %copy-done, bf16[16,320,128]{2,1,0:T(8,128)(2,1)} %all_to_all.31.shared_ref.parts_ref), custom_call_target="tpu_custom_call" | custom-call | tf_op jit(solution)/shard_map/pallas_call | solution.py:425
  292.5 5.1 %collective-permute-done.19 = bf16[128,512]{1,0:T(8,128)(2,1)S(1)} collective-permute-done((bf16[128,512]{1,0:T(8,128)(2,1)}, bf16[128,512]{1,0:T(8,128)(2,1)S(1)}, u32[]{:S(2)}, u32[]{:S(2)}) %collective-permute-start.19) | collective-permute-done | bytes 131104 | tf_op jit(solution)/shard_map/ppermute | solution.py:42
  (116 shorter events, 77.9 us)
Async XLA Ops:
  7.2 120.7 %all-gather.4.cloned.1.call-start = ((), (), s32[]{:S(2)}) async-start(), calls=%async_computation.7 | async-start | bytes 2228224 | tf_op jit(solution)/shard_map/all_gather | solution.py:497
  12.1 87.2 %all-to-all-start = ((bf16[16,192,512]{2,1,0:T(8,128)(2,1)}), bf16[16,192,512]{2,1,0:T(8,128)(2,1)S(1)}, u32[]{:S(2)}, u32[]{:S(2)}) async-start(bf16[16,192,512]{2,1,0:T(8,128)(2,1)} %laid_out.1), calls=%async_computation | async-start | bytes 6291456 | tf_op jit(solution)/shard_map/all_to_all | solution.py:46
  17.4 282.1 %all-gather.6.cloned.1.call-start = ((), (), s32[]{:S(2)}) async-start(), calls=%async_computation.9 | async-start | bytes 2359296 | tf_op jit(solution)/shard_map/all_gather | solution.py:519
  18.4 31.1 %collective-permute-start = (bf16[128,512]{1,0:T(8,128)(2,1)S(1)}, bf16[128,512]{1,0:T(8,128)(2,1)S(1)}, u32[]{:S(2)}, u32[]{:S(2)}) collective-permute-start(bf16[128,512]{1,0:T(8,128)(2,1)S(1)} %get-tuple-element.17), channel_id=1, source_target_pairs={{0,128},{16,144},{32,160},{48,176},{64,192},{80,208},{96,224},{112... | collective-permute-start | bytes 393224 | tf_op jit(solution)/shard_map/ppermute | solution.py:501
  50.3 14.1 %collective-permute-start.1 = (bf16[128,512]{1,0:T(8,128)(2,1)}, bf16[128,512]{1,0:T(8,128)(2,1)S(1)}, u32[]{:S(2)}, u32[]{:S(2)}) collective-permute-start(bf16[128,512]{1,0:T(8,128)(2,1)} %get-tuple-element.18), channel_id=1, source_target_pairs={{16,0},{32,16},{48,32},{64,48},{80,64},{96,80},{112,96},{0,112},{1... | collective-permute-start | bytes 393224 | tf_op jit(solution)/shard_map/ppermute | solution.py:28
  59.3 11.4 %collective-permute-start.2 = (bf16[128,512]{1,0:T(8,128)(2,1)}, bf16[128,512]{1,0:T(8,128)(2,1)S(1)}, u32[]{:S(2)}, u32[]{:S(2)}) collective-permute-start(bf16[128,512]{1,0:T(8,128)(2,1)} %get-tuple-element.19), channel_id=1, source_target_pairs={{32,0},{48,16},{64,32},{80,48},{96,64},{112,80},{0,96},{16,112},{1... | collective-permute-start | bytes 393224 | tf_op jit(solution)/shard_map/ppermute | solution.py:28
  59.3 16.7 %collective-permute-start.3 = (bf16[128,512]{1,0:T(8,128)(2,1)}, bf16[128,512]{1,0:T(8,128)(2,1)S(1)}, u32[]{:S(2)}, u32[]{:S(2)}) collective-permute-start(bf16[128,512]{1,0:T(8,128)(2,1)} %get-tuple-element.20), channel_id=1, source_target_pairs={{48,0},{64,16},{80,32},{96,48},{112,64},{0,80},{16,96},{32,112},{1... | collective-permute-start | bytes 393224 | tf_op jit(solution)/shard_map/ppermute | solution.py:28
  59.3 19.7 %collective-permute-start.4 = (bf16[128,512]{1,0:T(8,128)(2,1)S(1)}, bf16[128,512]{1,0:T(8,128)(2,1)S(1)}, u32[]{:S(2)}, u32[]{:S(2)}) collective-permute-start(bf16[128,512]{1,0:T(8,128)(2,1)S(1)} %get-tuple-element.16), channel_id=1, source_target_pairs={{64,0},{80,16},{96,32},{112,48},{192,128},{208,144},{224,160},{240... | collective-permute-start | bytes 393224 | tf_op jit(solution)/shard_map/ppermute | solution.py:28
  60.6 23.8 %collective-permute-start.5 = (bf16[128,512]{1,0:T(8,128)(2,1)S(1)}, bf16[128,512]{1,0:T(8,128)(2,1)S(1)}, u32[]{:S(2)}, u32[]{:S(2)}) collective-permute-start(bf16[128,512]{1,0:T(8,128)(2,1)S(1)} %collective-permute-done.partner_ref), channel_id=1, source_target_pairs={{240,128},{128,144},{144,160},{160,176},{176,192},{192,208},{208,2... | collective-permute-start | bytes 393224 | tf_op jit(solution)/shard_map/ppermute | solution.py:37
  64.4 22.5 %collective-permute-start.6 = (bf16[128,512]{1,0:T(8,128)(2,1)S(1)}, bf16[128,512]{1,0:T(8,128)(2,1)S(1)}, u32[]{:S(2)}, u32[]{:S(2)}) collective-permute-start(bf16[128,512]{1,0:T(8,128)(2,1)S(1)} %collective-permute-done.partner_ref), channel_id=1, source_target_pairs={{224,128},{240,144},{128,160},{144,176},{160,192},{176,208},{192,2... | collective-permute-start | bytes 393224 | tf_op jit(solution)/shard_map/ppermute | solution.py:37
  70.7 16.2 %collective-permute-start.7 = (bf16[128,512]{1,0:T(8,128)(2,1)S(1)}, bf16[128,512]{1,0:T(8,128)(2,1)S(1)}, u32[]{:S(2)}, u32[]{:S(2)}) collective-permute-start(bf16[128,512]{1,0:T(8,128)(2,1)S(1)} %collective-permute-done.partner_ref), channel_id=1, source_target_pairs={{208,128},{224,144},{240,160},{128,176},{144,192},{160,208},{176,2... | collective-permute-start | bytes 393224 | tf_op jit(solution)/shard_map/ppermute | solution.py:37
  76.0 10.9 %collective-permute-start.8 = (bf16[128,512]{1,0:T(8,128)(2,1)S(1)}, bf16[128,512]{1,0:T(8,128)(2,1)S(1)}, u32[]{:S(2)}, u32[]{:S(2)}) collective-permute-start(bf16[128,512]{1,0:T(8,128)(2,1)S(1)} %collective-permute-done.partner_ref), channel_id=1, source_target_pairs={{160,128},{176,144},{192,160},{208,176},{224,192},{240,208},{128,2... | collective-permute-start | bytes 393224 | tf_op jit(solution)/shard_map/ppermute | solution.py:37
  79.0 20.4 %collective-permute-start.9 = (bf16[128,512]{1,0:T(8,128)(2,1)S(1)}, bf16[128,512]{1,0:T(8,128)(2,1)S(1)}, u32[]{:S(2)}, u32[]{:S(2)}) collective-permute-start(bf16[128,512]{1,0:T(8,128)(2,1)S(1)} %bitcast.38), channel_id=1, source_target_pairs={{0,240},{16,224},{32,208},{48,192},{64,176},{80,160},{96,144},{112... | collective-permute-start | bytes 393224 | tf_op jit(solution)/shard_map/ppermute | solution.py:42
  105.8 35.3 %all-to-all-start.1 = ((bf16[16,256,128]{2,1,0:T(8,128)(2,1)}), bf16[16,256,128]{2,1,0:T(8,128)(2,1)S(1)}, u32[]{:S(2)}, u32[]{:S(2)}) async-start(bf16[16,256,128]{2,1,0:T(8,128)(2,1)} %pre_parts.1), calls=%async_computation.1 | async-start | bytes 2097152 | tf_op jit(solution)/shard_map/all_to_all | solution.py:46
  160.7 32.9 %all-to-all-start.3 = ((bf16[8,16,64,128]{3,2,1,0:T(8,128)(2,1)}), bf16[8,16,64,128]{3,2,1,0:T(8,128)(2,1)S(1)}, u32[]{:S(2)}, u32[]{:S(2)}) async-start(bf16[8,16,64,128]{3,2,1,0:T(8,128)(2,1)} %broadcast_in_dim.12), calls=%async_computation.3 | async-start | bytes 4194304 | tf_op jit(solution)/shard_map/all_to_all | solution.py:46
  164.6 134.8 %reduce-scatter.2.cloned.1.call-start = ((), (), s32[]{:S(2)}) async-start(), calls=%async_computation.8 | async-start | bytes 2228224 | tf_op jit(solution)/shard_map/reduce_scatter | solution.py:545
  193.6 54.2 %collective-permute-start.10 = (bf16[8,16,64,128]{3,2,1,0:T(8,128)(2,1)S(1)}, bf16[8,16,64,128]{3,2,1,0:T(8,128)(2,1)}, u32[]{:S(2)}, u32[]{:S(2)}) collective-permute-start(bf16[8,16,64,128]{3,2,1,0:T(8,128)(2,1)S(1)} %all-to-all-done.3.same_ref), channel_id=1, source_target_pairs={{0,1},{1,0},{2,3},{3,2},{4,5},{5,4},{6,7},{7,6},{8,9},{9,8},{10,11... | collective-permute-start | bytes 6291464 | tf_op jit(solution)/shard_map/ppermute | solution.py:55
  205.2 21.3 %collective-permute-start.13 = (bf16[2,384,128]{2,1,0:T(8,128)(2,1)S(1)}, bf16[2,384,128]{2,1,0:T(8,128)(2,1)S(1)}, u32[]{:S(2)}, u32[]{:S(2)}) collective-permute-start(bf16[2,384,128]{2,1,0:T(8,128)(2,1)S(1)} %pad_maximum_fusion.1.refs_0_), channel_id=1, source_target_pairs={{32,0},{48,16},{64,32},{80,48},{96,64},{112,80},{0,96},{16,112},{1... | collective-permute-start | bytes 589832 | tf_op jit(solution)/shard_map/ppermute | solution.py:28
  207.1 25.4 %collective-permute-start.14 = (bf16[2,384,128]{2,1,0:T(8,128)(2,1)S(1)}, bf16[2,384,128]{2,1,0:T(8,128)(2,1)S(1)}, u32[]{:S(2)}, u32[]{:S(2)}) collective-permute-start(bf16[2,384,128]{2,1,0:T(8,128)(2,1)S(1)} %pad_maximum_fusion.1.refs_0_), channel_id=1, source_target_pairs={{48,0},{64,16},{80,32},{96,48},{112,64},{0,80},{16,96},{32,112},{1... | collective-permute-start | bytes 589832 | tf_op jit(solution)/shard_map/ppermute | solution.py:28
  210.5 34.1 %collective-permute-start.15 = (bf16[2,384,128]{2,1,0:T(8,128)(2,1)S(1)}, bf16[2,384,128]{2,1,0:T(8,128)(2,1)S(1)}, u32[]{:S(2)}, u32[]{:S(2)}) collective-permute-start(bf16[2,384,128]{2,1,0:T(8,128)(2,1)S(1)} %pad_maximum_fusion.1.refs_0_), channel_id=1, source_target_pairs={{64,0},{80,16},{96,32},{112,48},{0,64},{16,80},{32,96},{48,112},{1... | collective-permute-start | bytes 589832 | tf_op jit(solution)/shard_map/ppermute | solution.py:28
  213.1 31.4 %collective-permute-start.16 = (bf16[2,384,128]{2,1,0:T(8,128)(2,1)S(1)}, bf16[2,384,128]{2,1,0:T(8,128)(2,1)S(1)}, u32[]{:S(2)}, u32[]{:S(2)}) collective-permute-start(bf16[2,384,128]{2,1,0:T(8,128)(2,1)S(1)} %pad_maximum_fusion.1.refs_0_), channel_id=1, source_target_pairs={{80,0},{96,16},{112,32},{0,48},{16,64},{32,80},{48,96},{64,112},{2... | collective-permute-start | bytes 589832 | tf_op jit(solution)/shard_map/ppermute | solution.py:28
  226.5 18.9 %collective-permute-start.17 = (bf16[2,384,128]{2,1,0:T(8,128)(2,1)S(1)}, bf16[2,384,128]{2,1,0:T(8,128)(2,1)S(1)}, u32[]{:S(2)}, u32[]{:S(2)}) collective-permute-start(bf16[2,384,128]{2,1,0:T(8,128)(2,1)S(1)} %pad_maximum_fusion.1.refs_0_), channel_id=1, source_target_pairs={{96,0},{112,16},{0,32},{16,48},{32,64},{48,80},{64,96},{80,112},{2... | collective-permute-start | bytes 589832 | tf_op jit(solution)/shard_map/ppermute | solution.py:28
  232.5 15.3 %collective-permute-start.18 = (bf16[2,384,128]{2,1,0:T(8,128)(2,1)S(1)}, bf16[2,384,128]{2,1,0:T(8,128)(2,1)}, u32[]{:S(2)}, u32[]{:S(2)}) collective-permute-start(bf16[2,384,128]{2,1,0:T(8,128)(2,1)S(1)} %pad_maximum_fusion.1.refs_0_), channel_id=1, source_target_pairs={{112,0},{0,16},{16,32},{32,48},{48,64},{64,80},{80,96},{96,112},{2... | collective-permute-start | bytes 589832 | tf_op jit(solution)/shard_map/ppermute | solution.py:28
  280.6 18.9 %all-to-all-start.5 = ((bf16[16,128,128]{2,1,0:T(8,128)(2,1)}), bf16[16,128,128]{2,1,0:T(8,128)(2,1)S(1)}, u32[]{:S(2)}, u32[]{:S(2)}) async-start(bf16[16,128,128]{2,1,0:T(8,128)(2,1)} %folded.1), calls=%async_computation.5 | async-start | bytes 1048576 | tf_op jit(solution)/shard_map/all_to_all | solution.py:46
  (33 other events, 461.1 us)
Sparse Core Ops, SparseCore 0:
  9.8 69.6 all-gather.3
  81.3 39.7 all-gather.5
  179.9 67.7 reduce-scatter.1
